TPU v7x, 32 devices: a whole 2x2x4 slice. The times are simulated.
32 devices in a mesh: groups: 2 (over y), seq: 4 (over z), exp: 4 (over x, core).
Axes of the slice: x: 2, y: 2, z: 4, core: 2. Of those that a mesh axis runs over, the one named last changes fastest.
Arguments:
- residual: bfloat16 [1024, 6144], P(('groups', 'seq'), 'exp'), parts along dimension 0, may hold values from -6 to 6
- query_rows: bfloat16 [1024, 6144], P(('groups', 'seq'), 'exp'), parts along dimension 0, may hold values from -6 to 6
- key_rows: bfloat16 [1024, 6144], P(('groups', 'seq'), 'exp'), parts along dimension 0, may hold values from -6 to 6
- value_rows: bfloat16 [1024, 6144], P(('groups', 'seq'), 'exp'), parts along dimension 0, may hold values from -6 to 6
- log_decay: float32 [1024, 48], P(('groups', 'seq'), 'exp'), parts along dimension 0, may hold values from -0.8 to 0
- attn_gain: float32 [6144], P('exp'), may hold values from 0.1 to 1.9
- norm_gain: float32 [6144], P('exp'), may hold values from 0.1 to 1.9
- router: bfloat16 [6144, 32], P('exp'), may hold values from -0.3125 to 0.3125
- expert_ids: int32 [1024, 2], P(('groups', 'seq')), parts along dimension 0, may hold values from 0 to 31, all different within a row
- priority: int32 [8, 128], P(('groups', 'seq')), parts along dimension 0, may hold values from 0 to 127, each once within a row
- gate_weight: bfloat16 [4, 6144, 4608], P('exp', None, 'seq'), may hold values from -0.078125 to 0.078125
- up_weight: bfloat16 [4, 6144, 4608], P('exp', None, 'seq'), may hold values from -0.078125 to 0.078125
- down_weight: bfloat16 [4, 4608, 6144], P('exp', None, 'seq'), may hold values from -0.125 to 0.125
Outputs:
- layer_out: bfloat16 [1024, 6144], P(('groups', 'seq'), 'exp'), parts along dimension 0
There are 2 independent parts, one for each index of `groups`. A program takes and returns all parts, laid end to end along the dimension named above; an argument that names none is the same for every part. Nothing has to cross between parts.
Inputs may be any that keep to these rules, and one draw needn't show every extreme that they name: `expert_ids`: each row names two different experts; ids of 4 or more name experts whose weights are not given. `priority`: each row holds every number from 0 to 127 once.
All inputs are finite; a program needn't handle non-finite values.
Results may differ from a plain program's by a relative error of at most 0.0047.
Values may be sent and summed in bfloat16 or wider, within the bound.
No kernel may reach another device: no remote copies, remote signals or barrier semaphores. Data moves between devices by JAX's collectives and lax.ppermute only.
A program may use at most 128 MiB of HBM per device.

v0:
```python
import jax
import jax.numpy as jnp
from jax import lax
from jax.sharding import PartitionSpec as P

D = 6144
HEAD = 128
EXPERTS = 32
CAP = 8


def link_states(earlier, later):
    return (earlier[0] * later[0], later[0] * earlier[1] + later[1])


def body(
    residual,
    query_rows,
    key_rows,
    value_rows,
    log_decay,
    attn_gain,
    norm_gain,
    router,
    expert_ids,
    priority,
    gate_weight,
    up_weight,
    down_weight,
):
    rows = residual.shape[0]
    width = residual.shape[1]
    heads = width // HEAD
    held = lax.axis_size("exp")
    queries = query_rows.reshape(rows, heads, HEAD)
    keys_local = key_rows.reshape(rows, heads, HEAD)
    values = value_rows.reshape(rows, heads, HEAD)
    cumulative = jnp.cumsum(log_decay, axis=0)
    scores = jnp.einsum("thd,shd->hts", queries, keys_local, preferred_element_type=jnp.float32)
    causal = (jnp.arange(rows)[:, None] >= jnp.arange(rows)[None, :])[None]
    spread = cumulative.T[:, :, None] - cumulative.T[:, None, :]
    weights = jnp.where(causal, scores * jnp.exp(jnp.where(causal, spread, 0.0)), 0.0).astype(
        jnp.bfloat16
    )
    local_part = jnp.einsum("hts,shd->thd", weights, values, preferred_element_type=jnp.float32)
    to_end = jnp.exp(cumulative[-1][None, :] - cumulative)
    keyed = (keys_local.astype(jnp.float32) * to_end[:, :, None]).astype(jnp.bfloat16)
    block_state = jnp.einsum("thd,the->hde", keyed, values, preferred_element_type=jnp.float32)
    block_decay = jnp.exp(cumulative[-1])
    seq_count = lax.axis_size("seq")
    share_size = block_state.size // seq_count
    flat_state = block_state.reshape(seq_count, share_size)
    tiled_decay = jnp.broadcast_to(block_decay[None, :], (seq_count, heads))
    arrived_state, arrived_decay = (
        lax.all_to_all(flat_state, "seq", split_axis=0, concat_axis=0, tiled=True),
        lax.all_to_all(tiled_decay, "seq", split_axis=0, concat_axis=0, tiled=True),
    )
    position = lax.axis_index("seq") * share_size + jnp.arange(share_size, dtype=jnp.int32)
    owner_head = position // (HEAD * HEAD)
    selector = jnp.where(
        owner_head[None, :] == jnp.arange(heads, dtype=jnp.int32)[:, None], 1.0, 0.0
    ).astype(jnp.float32)
    element_decay = jnp.dot(arrived_decay, selector, precision=lax.Precision.HIGHEST)
    inclusive = lax.associative_scan(link_states, (element_decay, arrived_state), axis=0)[1]
    exclusive = jnp.concatenate([jnp.zeros((1, share_size), jnp.float32), inclusive[:-1]], axis=0)
    returned_prefix = lax.all_to_all(exclusive, "seq", split_axis=0, concat_axis=0, tiled=True)
    prior_state = returned_prefix.reshape(block_state.shape)
    inter = jnp.einsum(
        "thd,hde->the", queries.astype(jnp.float32), prior_state, precision=lax.Precision.HIGHEST
    )
    attended = local_part + jnp.exp(cumulative)[:, :, None] * inter
    normed = attended * lax.rsqrt(jnp.mean(attended * attended, axis=-1, keepdims=True) + 1e-06)
    normed = normed * attn_gain.reshape(heads, HEAD)
    mixed = (residual.astype(jnp.float32) + normed.reshape(rows, width)).astype(jnp.bfloat16)
    mixed_f = mixed.astype(jnp.float32)
    gained = mixed_f * norm_gain
    router_f = router.astype(jnp.float32)
    squares = lax.psum(jnp.sum(mixed_f * mixed_f, axis=1), "exp")
    inverse = lax.rsqrt(squares / D + 1e-06)
    scaled = gained * inverse[:, None]
    logits = lax.psum(jnp.dot(scaled, router_f, precision=lax.Precision.HIGHEST), "exp")
    tokens_in = scaled.astype(jnp.bfloat16)
    probs = jax.nn.sigmoid(logits)
    chosen = expert_ids[:, :, None] == jnp.arange(EXPERTS, dtype=jnp.int32)[None, None, :]
    selected = jnp.sum(jnp.where(chosen, probs[:, None, :], 0.0), axis=-1)
    gates = selected / jnp.sum(selected, axis=-1, keepdims=True)
    is_held = expert_ids[:, :, None] == jnp.arange(held, dtype=jnp.int32)[None, None, :]
    member = jnp.where(jnp.any(is_held, axis=1), 1.0, 0.0).astype(jnp.float32)
    gate_held = jnp.sum(jnp.where(is_held, gates[:, :, None], 0.0), axis=1)
    order = priority[0]
    earlier = jnp.where(order[None, :] < order[:, None], 1.0, 0.0).astype(jnp.bfloat16)
    rank = jnp.dot(earlier, member.astype(jnp.bfloat16), preferred_element_type=jnp.float32)
    kept = (member > 0.5) & (rank < CAP)
    slot_ids = jnp.arange(CAP).astype(jnp.float32)
    place = kept.T[:, None, :] & (rank.T[:, None, :] == slot_ids[None, :, None])
    place_f = jnp.where(place, 1.0, 0.0).astype(jnp.float32)
    buffer = jnp.einsum(
        "ect,td->ecd", place_f.astype(jnp.bfloat16), tokens_in, preferred_element_type=jnp.float32
    ).astype(jnp.bfloat16)
    arrived = lax.all_to_all(buffer, "exp", split_axis=0, concat_axis=2, tiled=True)[0]
    gathered = lax.all_gather(arrived, "seq", axis=0, tiled=True)
    gate = jnp.dot(gathered, gate_weight[0], preferred_element_type=jnp.float32)
    up = jnp.dot(gathered, up_weight[0], preferred_element_type=jnp.float32)
    hidden = (jax.nn.silu(gate) * up).astype(jnp.bfloat16)
    weight_rows = down_weight[0]
    summed = jnp.dot(
        lax.all_gather(hidden, "seq", axis=1, tiled=True),
        weight_rows,
        preferred_element_type=jnp.float32,
    )
    expert_out = summed.astype(jnp.bfloat16)
    returned = lax.all_to_all(expert_out, "seq", split_axis=0, concat_axis=1, tiled=True)
    regrouped = lax.all_to_all(returned[None], "exp", split_axis=2, concat_axis=0, tiled=True)
    weighted = place_f * gate_held.T[:, None, :]
    combined = jnp.einsum(
        "ect,ecd->td", weighted, regrouped.astype(jnp.float32), precision=lax.Precision.HIGHEST
    )
    return (mixed_f + combined).astype(jnp.bfloat16)


def solution(mesh):
    return jax.shard_map(
        body,
        mesh=mesh,
        in_specs=(
            P(("groups", "seq"), "exp"),
            P(("groups", "seq"), "exp"),
            P(("groups", "seq"), "exp"),
            P(("groups", "seq"), "exp"),
            P(("groups", "seq"), "exp"),
            P("exp"),
            P("exp"),
            P("exp", None),
            P(("groups", "seq"), None),
            P(("groups", "seq"), None),
            P("exp", None, "seq"),
            P("exp", None, "seq"),
            P("exp", None, "seq"),
        ),
        out_specs=P(("groups", "seq"), "exp"),
        check_vma=False,
    )
```

profile of v0, /device:TPU:2, one launch (start us, length us, event | category | flops | bytes accessed | tf_op | source)
XLA Modules:
  0.0 214.6 jit_solution(99139282639434964)
XLA Ops:
  1.6 4.9 %all-to-all-start.1 = ((f32[4,1,12]{2,1,0:T(1,128)}), f32[4,1,12]{2,1,0:T(1,128)S(1)}, u32[]{:S(2)}, u32[]{:S(2)}) async-start(f32[4,1,12]{2,1,0:T(1,128)} %broadcast_in_dim.109), calls=%async_computation.1 | async-start | bytes 4096 | tf_op jit(solution)/shard_map/all_to_all | solution.py:56
  10.3 1.7 all-to-all-done.1
  12.0 3.5 %all-to-all-start = ((f32[4,1,49152]{2,1,0:T(1,128)}), f32[4,1,49152]{2,1,0:T(1,128)S(1)}, u32[]{:S(2)}, u32[]{:S(2)}) async-start(f32[4,1,49152]{2,1,0:T(1,128)} %bitcast.6), calls=%async_computation | async-start | bytes 1572864 | tf_op jit(solution)/shard_map/all_to_all | solution.py:55
  15.6 1.9 fusion.6
  17.6 2.8 %slice.56 = f32[2,49152]{1,0:T(2,128)S(1)} slice(f32[4,49152]{1,0:T(4,128)S(1)} %fusion.6), slice={[1:4:2], [0:49152:1]} | slice | bytes 786432 | tf_op jit(solution)/shard_map/slice | solution.py:64
  20.4 5.1 %slice.60 = f32[2,49152]{1,0:T(2,128)} slice(f32[4,49152]{1,0:T(4,128)S(1)} %fusion.6), slice={[0:3:2], [0:49152:1]} | slice | bytes 786432 | tf_op jit(solution)/shard_map/slice | solution.py:64
  25.5 9.4 %all-to-all-done = f32[4,1,49152]{2,1,0:T(1,128)S(1)} async-done(((f32[4,1,49152]{2,1,0:T(1,128)}), f32[4,1,49152]{2,1,0:T(1,128)S(1)}, u32[]{:S(2)}, u32[]{:S(2)}) %all-to-all-start) | async-done | bytes 786464 | tf_op jit(solution)/shard_map/all_to_all | solution.py:55
  35.5 2.8 %slice.58 = f32[2,49152]{1,0:T(2,128)S(1)} slice(f32[4,49152]{1,0:T(4,128)S(1)} %bitcast.98), slice={[1:4:2], [0:49152:1]} | slice | bytes 786432 | tf_op jit(solution)/shard_map/slice | solution.py:64
  38.3 5.1 %slice.57 = f32[2,49152]{1,0:T(2,128)} slice(f32[4,49152]{1,0:T(4,128)S(1)} %bitcast.99), slice={[0:3:2], [0:49152:1]} | slice | bytes 786432 | tf_op jit(solution)/shard_map/slice | solution.py:64
  44.7 1.6 fusion.86
  46.7 1.7 fusion.52
  50.4 1.7 copy.119
  52.1 3.5 %all-to-all-start.2 = ((f32[4,1,49152]{2,1,0:T(1,128)}), f32[4,1,49152]{2,1,0:T(1,128)S(1)}, u32[]{:S(2)}, u32[]{:S(2)}) async-start(f32[4,1,49152]{2,1,0:T(1,128)} %copy.119), calls=%async_computation.2 | async-start | bytes 1572864 | tf_op jit(solution)/shard_map/all_to_all | solution.py:66
  57.2 18.0 %all-to-all-done.2 = f32[4,1,49152]{2,1,0:T(1,128)S(1)} async-done(((f32[4,1,49152]{2,1,0:T(1,128)}), f32[4,1,49152]{2,1,0:T(1,128)S(1)}, u32[]{:S(2)}, u32[]{:S(2)}) %all-to-all-start.2) | async-done | bytes 786464 | tf_op jit(solution)/shard_map/all_to_all | solution.py:66
  77.5 5.9 %psum.14 = f32[128]{0:T(128)S(1)} all-reduce(f32[128]{0:T(128)S(1)} %get-tuple-element.7), channel_id=1, replica_groups=mesh['groups'=2,'seq'=4,'exp'=4] {'exp'}, use_global_device_ids=true, to_apply=%region_4.5 | all-reduce | flops 128 | bytes 1024 | tf_op jit(solution)/shard_map/psum | solution.py:78
  84.3 3.9 %all-to-all-start.3 = ((bf16[4,8,1536]{2,1,0:T(8,128)(2,1)}), bf16[4,8,1536]{2,1,0:T(8,128)(2,1)S(1)}, u32[]{:S(2)}, u32[]{:S(2)}) async-start(bf16[4,8,1536]{2,1,0:T(8,128)(2,1)} %convolution_convert_fusion), calls=%async_computation.3 | async-start | bytes 196608 | tf_op jit(solution)/shard_map/all_to_all | solution.py:100
  88.9 10.1 %psum.15 = f32[128,32]{0,1:T(8,128)S(1)} all-reduce(f32[128,32]{0,1:T(8,128)S(1)} %fusion.31), channel_id=1, replica_groups=mesh['groups'=2,'seq'=4,'exp'=4] {'exp'}, use_global_device_ids=true, to_apply=%region_5.6 | all-reduce | flops 4096 | bytes 32768 | tf_op jit(solution)/shard_map/psum | solution.py:81
  99.1 15.2 %all_gather.6 = bf16[32,6144]{1,0:T(8,128)(2,1)S(1)} all-gather(bf16[8,6144]{1,0:T(8,128)(2,1)S(1)} %bitcast.110), channel_id=1, replica_groups=mesh['groups'=2,'seq'=4,'exp'=4] {'seq'}, dimensions={0}, use_global_device_ids=true | all-gather | bytes 491520 | tf_op jit(solution)/shard_map/all_gather | solution.py:101
  114.3 7.6 %fusion.4 = f32[32,1152]{1,0:T(8,128)S(1)} fusion(bf16[32,6144]{1,0:T(8,128)(2,1)S(1)} %all_gather.6, bf16[1,6144,1152]{2,1,0:T(8,128)(2,1)} %param.23), kind=kOutput, calls=%fused_computation.4 | convolution fusion | flops 452984832 | bytes 14696448 | tf_op jit(solution)/shard_map/dot_general | solution.py:102
  121.8 7.6 %fusion.13 = bf16[32,1152]{1,0:T(8,128)(2,1)S(1)} fusion(bf16[32,6144]{1,0:T(8,128)(2,1)S(1)} %all_gather.6, bf16[1,6144,1152]{2,1,0:T(8,128)(2,1)} %param.24, f32[32,1152]{1,0:T(8,128)S(1)} %fusion.4), kind=kOutput, calls=%fused_computation.13 | convolution fusion | flops 453206016 | bytes 14770176 | tf_op jit(solution)/shard_map/dot_general | solution.py:103
  129.4 14.2 %all_gather.7 = bf16[32,4608]{1,0:T(8,128)(2,1)S(1)} all-gather(bf16[32,1152]{1,0:T(8,128)(2,1)S(1)} %fusion.13), channel_id=1, replica_groups=mesh['groups'=2,'seq'=4,'exp'=4] {'seq'}, dimensions={1}, use_global_device_ids=true | all-gather | bytes 368640 | tf_op jit(solution)/shard_map/all_gather | solution.py:107
  143.7 3.2 %fusion.19 = bf16[4,8,1536]{2,1,0:T(8,128)(2,1)} fusion(bf16[32,4608]{1,0:T(8,128)(2,1)S(1)} %all_gather.7, bf16[1,4608,1536]{2,1,0:T(8,128)(2,1)S(1)} %bitcast.94), kind=kOutput, calls=%fused_computation.16 | convolution fusion | flops 453033984 | bytes 14548992 | tf_op jit(solution)/shard_map/dot_general | solution.py:106
  146.9 3.3 %all-to-all-start.4 = ((bf16[4,8,1536]{2,1,0:T(8,128)(2,1)}), bf16[4,8,1536]{2,1,0:T(8,128)(2,1)S(1)}, u32[]{:S(2)}, u32[]{:S(2)}) async-start(bf16[4,8,1536]{2,1,0:T(8,128)(2,1)} %fusion.19), calls=%async_computation.4 | async-start | bytes 196608 | tf_op jit(solution)/shard_map/all_to_all | solution.py:112
  150.2 5.8 %all-to-all-done.4 = bf16[4,8,1536]{2,1,0:T(8,128)(2,1)S(1)} async-done(((bf16[4,8,1536]{2,1,0:T(8,128)(2,1)}), bf16[4,8,1536]{2,1,0:T(8,128)(2,1)S(1)}, u32[]{:S(2)}, u32[]{:S(2)}) %all-to-all-start.4) | async-done | bytes 98336 | tf_op jit(solution)/shard_map/all_to_all | solution.py:112
  156.0 3.9 %copy.123 = bf16[1,8,6144]{1,0,2:T(2,128)(2,1)S(1)} copy(bf16[1,8,6144]{2,1,0:T(8,128)(2,1)S(1)} %bitcast.108) | data formatting | bytes 196608 | tf_op jit(solution)/shard_map/broadcast_in_dim | solution.py:113
  160.5 34.4 %reduce.1 = bf16[6144,8]{1,0:T(8,128)(2,1)} reduce(bf16[6144,1,8]{2,1,0:T(2,128)(2,1)S(1)} %bitcast.95, bf16[]{:T(256)} %broadcast.113), dimensions={1}, to_apply=%bitcast.78.reduce_sub_computation | reduce | bytes 196610
  194.9 3.7 %reshape.134 = bf16[4,2,6144]{2,1,0:T(2,128)(2,1)} reshape(bf16[6144,8]{1,0:T(8,128)(2,1)} %reduce.1) | data formatting | bytes 196608
  198.7 4.5 %all-to-all-start.5 = ((bf16[4,2,6144]{2,1,0:T(2,128)(2,1)}), bf16[4,2,6144]{2,1,0:T(2,128)(2,1)S(1)}, u32[]{:S(2)}, u32[]{:S(2)}) async-start(bf16[4,2,6144]{2,1,0:T(2,128)(2,1)} %reshape.134), calls=%async_computation.5 | async-start | bytes 196608 | tf_op jit(solution)/shard_map/all_to_all | solution.py:113
  203.1 2.6 %all-to-all-done.5 = bf16[4,2,6144]{2,1,0:T(2,128)(2,1)S(1)} async-done(((bf16[4,2,6144]{2,1,0:T(2,128)(2,1)}), bf16[4,2,6144]{2,1,0:T(2,128)(2,1)S(1)}, u32[]{:S(2)}, u32[]{:S(2)}) %all-to-all-start.5) | async-done | bytes 98336 | tf_op jit(solution)/shard_map/all_to_all | solution.py:113
  205.8 3.8 %reshape.135 = bf16[6144,1,8]{2,1,0:T(2,128)(2,1)S(1)} reshape(bf16[4,2,6144]{2,1,0:T(2,128)(2,1)S(1)} %all-to-all-done.5) | data formatting | bytes 196608
  209.5 2.7 %copy.124 = bf16[1,8,6144]{2,1,0:T(8,128)(2,1)S(1)} copy(bf16[1,8,6144]{1,0,2:T(2,128)(2,1)S(1)} %bitcast.96) | data formatting | bytes 196608 | tf_op jit(solution)/shard_map/all_to_all | solution.py:113
  212.3 2.4 %fusion.9 = bf16[128,1536]{1,0:T(8,128)(2,1)} fusion(bf16[4,8,1536]{2,1,0:T(8,128)(2,1)S(1)} %bitcast.109, bf16[128,1536]{1,0:T(8,128)(2,1)} %copy-done.2, f32[4,128]{1,0:T(4,128)S(1)} %bitcast.112, f32[4,128]{1,0:T(4,128)S(1)} %get-tuple-element.18, f32[8]{0:T(128)S(1)} %iota_convert_fusion, pred[4,128]{1,0:T(4,128)(4,1)S(1)} %get-tuple-element.17), kind=kOutput, calls=%fused_computation.11 | convolution fusion | flops 76103680 | bytes 889376 | tf_op jit(solution)/shard_map/ect,ecd->td/dot_general | solution.py:115
  (68 shorter events, 15.7 us)
Async XLA Ops:
  0.0 88.3 %copy-start = (bf16[1536,32]{0,1:T(8,128)(2,1)S(1)}, bf16[1536,32]{0,1:T(8,128)(2,1)}, u32[]{:S(2)}) copy-start(bf16[1536,32]{0,1:T(8,128)(2,1)} %param.20) | copy-start | bytes 294916
  1.0 55.9 %copy-start.6 = (s32[128,2]{0,1:T(2,128)S(1)}, s32[128,2]{0,1:T(2,128)}, u32[]{:S(2)}) copy-start(s32[128,2]{0,1:T(2,128)} %param.21) | copy-start | bytes 3076
  1.0 56.0 %copy-start.8 = (s32[1,128]{1,0:T(1,128)S(1)}, s32[1,128]{1,0:T(1,128)}, u32[]{:S(2)}) copy-start(s32[1,128]{1,0:T(1,128)} %param.22) | copy-start | bytes 1540
  1.6 10.4 %all-to-all-start.1 = ((f32[4,1,12]{2,1,0:T(1,128)}), f32[4,1,12]{2,1,0:T(1,128)S(1)}, u32[]{:S(2)}, u32[]{:S(2)}) async-start(f32[4,1,12]{2,1,0:T(1,128)} %broadcast_in_dim.109), calls=%async_computation.1 | async-start | bytes 4096 | tf_op jit(solution)/shard_map/all_to_all | solution.py:56
  12.0 23.0 %all-to-all-start = ((f32[4,1,49152]{2,1,0:T(1,128)}), f32[4,1,49152]{2,1,0:T(1,128)S(1)}, u32[]{:S(2)}, u32[]{:S(2)}) async-start(f32[4,1,49152]{2,1,0:T(1,128)} %bitcast.6), calls=%async_computation | async-start | bytes 1572864 | tf_op jit(solution)/shard_map/all_to_all | solution.py:55
  15.5 61.2 %copy-start.5 = (f32[1536]{0:T(1024)S(1)}, f32[1536]{0:T(1024)}, u32[]{:S(2)}) copy-start(f32[1536]{0:T(1024)} %param.18) | copy-start | bytes 18436
  17.6 8.0 %copy-start.3 = (f32[4,49152]{1,0:T(4,128)}, f32[4,49152]{1,0:T(4,128)S(1)}, u32[]{:S(2)}) copy-start(f32[4,49152]{1,0:T(4,128)S(1)} %fusion.6) | copy-start | bytes 2359300
  25.5 57.9 %copy-start.7 = (f32[1536]{0:T(1024)S(1)}, f32[1536]{0:T(1024)}, u32[]{:S(2)}) copy-start(f32[1536]{0:T(1024)} %param.19) | copy-start | bytes 18436
  44.7 32.6 %copy-start.4 = (bf16[128,1536]{1,0:T(8,128)(2,1)S(1)}, bf16[128,1536]{1,0:T(8,128)(2,1)}, u32[]{:S(2)}) copy-start(bf16[128,1536]{1,0:T(8,128)(2,1)} %param.13) | copy-start | bytes 1179652
  52.1 23.1 %all-to-all-start.2 = ((f32[4,1,49152]{2,1,0:T(1,128)}), f32[4,1,49152]{2,1,0:T(1,128)S(1)}, u32[]{:S(2)}, u32[]{:S(2)}) async-start(f32[4,1,49152]{2,1,0:T(1,128)} %copy.119), calls=%async_computation.2 | async-start | bytes 1572864 | tf_op jit(solution)/shard_map/all_to_all | solution.py:66
  77.5 51.9 %copy-start.2 = (bf16[128,1536]{1,0:T(8,128)(2,1)}, bf16[128,1536]{1,0:T(8,128)(2,1)S(1)}, u32[]{:S(2)}) copy-start(bf16[128,1536]{1,0:T(8,128)(2,1)S(1)} %get-tuple-element.8) | copy-start | bytes 1179652
  84.3 14.8 %all-to-all-start.3 = ((bf16[4,8,1536]{2,1,0:T(8,128)(2,1)}), bf16[4,8,1536]{2,1,0:T(8,128)(2,1)S(1)}, u32[]{:S(2)}, u32[]{:S(2)}) async-start(bf16[4,8,1536]{2,1,0:T(8,128)(2,1)} %convolution_convert_fusion), calls=%async_computation.3 | async-start | bytes 196608 | tf_op jit(solution)/shard_map/all_to_all | solution.py:100
  114.3 29.4 %slice-start = ((s8[14155776]{0:T(1024)(128)(4,1)}), s8[4194304]{0:T(1024)(128)(4,1)S(1)}, s32[]{:S(2)}) async-start(s8[14155776]{0:T(1024)(128)(4,1)} %bitcast.93), calls=%async_computation.6 | async-start | bytes 8388608
  114.3 29.4 %slice-start.1 = ((s8[14155776]{0:T(1024)(128)(4,1)}), s8[4194304]{0:T(1024)(128)(4,1)S(1)}, s32[]{:S(2)}) async-start(s8[14155776]{0:T(1024)(128)(4,1)} %bitcast.93), calls=%async_computation.7 | async-start | bytes 8388608
  121.8 21.9 %slice-start.2 = ((s8[14155776]{0:T(1024)(128)(4,1)}), s8[4194304]{0:T(1024)(128)(4,1)S(1)}, s32[]{:S(2)}) async-start(s8[14155776]{0:T(1024)(128)(4,1)} %bitcast.93), calls=%async_computation.8 | async-start | bytes 8388608
  121.8 21.8 %slice-start.3 = ((s8[14155776]{0:T(1024)(128)(4,1)}), s8[1572864]{0:T(1024)(128)(4,1)S(1)}, s32[]{:S(2)}) async-start(s8[14155776]{0:T(1024)(128)(4,1)} %bitcast.93), calls=%async_computation.9 | async-start | bytes 3145728
  143.7 70.9 %copy-start.1 = (bf16[1536,32]{0,1:T(8,128)(2,1)S(1)}, bf16[1536,32]{0,1:T(8,128)(2,1)}, u32[]{:S(2)}) copy-start(bf16[1536,32]{0,1:T(8,128)(2,1)} %param.20) | copy-start | bytes 294916
  146.9 9.1 %all-to-all-start.4 = ((bf16[4,8,1536]{2,1,0:T(8,128)(2,1)}), bf16[4,8,1536]{2,1,0:T(8,128)(2,1)S(1)}, u32[]{:S(2)}, u32[]{:S(2)}) async-start(bf16[4,8,1536]{2,1,0:T(8,128)(2,1)} %fusion.19), calls=%async_computation.4 | async-start | bytes 196608 | tf_op jit(solution)/shard_map/all_to_all | solution.py:112
  198.7 7.1 %all-to-all-start.5 = ((bf16[4,2,6144]{2,1,0:T(2,128)(2,1)}), bf16[4,2,6144]{2,1,0:T(2,128)(2,1)S(1)}, u32[]{:S(2)}, u32[]{:S(2)}) async-start(bf16[4,2,6144]{2,1,0:T(2,128)(2,1)} %reshape.134), calls=%async_computation.5 | async-start | bytes 196608 | tf_op jit(solution)/shard_map/all_to_all | solution.py:113
where the time goes:
time: 218 us; the launch traced here: 215 us
  blocking collectives  45.4 us (21%)
  other arithmetic  40.8 us (19%)
  local copies, waits for them, and re-layouts  39.9 us (18%)
  waiting for transfers between devices  37.5 us (17%)
  matrix products  27.1 us (12%)
  starting transfers between devices  23.6 us (11%)
    unnamed x2, other arithmetic  34.4 us
    all_to_all x1, waiting for transfers between devices, body(): lax.all_to_all(exclusive, 'seq', split_axis=0, concat_axis=0, tiled=True)  18 us
    slice x5, local copies, waits for them, and re-layouts, body(): lax.associative_scan(link_states, (element_decay, arrived_state), axis=0)[1]  15.9 us
    all_gather x1, blocking collectives, body(): gathered = lax.all_gather(arrived, 'seq', axis=0, tiled=True)  15.2 us
    all_gather x1, blocking collectives, body(): lax.all_gather(hidden, 'seq', axis=1, tiled=True)  14.2 us
    unnamed x35, local copies, waits for them, and re-layouts  13.7 us
    psum x1, blocking collectives, body(): lax.psum(jnp.dot(scaled, router_f, precision=lax.Precision.HIGHEST), 'exp')  10.1 us
    all_to_all x1, waiting for transfers between devices, body(): lax.all_to_all(flat_state, 'seq', split_axis=0, concat_axis=0, tiled=True)  9.43 us
  transfers between devices with their start and end apart: 6, of which 5 were waited for; matrix products, arithmetic and copies ran while one was open for 8% of the time, Pallas kernels for 0%

commit v1 on v0

v1 whole, which is shorter than its diff:
```python
import functools

import jax
import jax.numpy as jnp
from jax import lax
from jax.experimental import pallas as pl
from jax.experimental.pallas import tpu as pltpu
from jax.sharding import PartitionSpec as P

HEAD = 128
LANES = 128
CAP = 8
PAD = 16
EPS = 1e-06
F32 = jnp.float32
BF16 = jnp.bfloat16

VMEM = pl.BlockSpec(memory_space=pltpu.VMEM)


def nt(a, b):
    return lax.dot_general(a, b, (((1,), (1,)), ((), ())), preferred_element_type=F32)


def tn(a, b):
    return lax.dot_general(a, b, (((0,), (0,)), ((), ())), preferred_element_type=F32)


def nn(a, b):
    return lax.dot_general(a, b, (((1,), (0,)), ((), ())), preferred_element_type=F32)


def iota(shape, dim):
    return lax.broadcasted_iota(jnp.int32, shape, dim)


def split_hi_lo(x):
    hi = x.astype(BF16)
    return hi, (x - hi.astype(F32)).astype(BF16)


def state_kernel(heads, shares, share_rows, k_ref, v_ref, decay_ref, pay_ref, row_ref, col_ref, pad_ref):
    rows = k_ref.shape[0]
    pad_ref[...] = jnp.zeros_like(pad_ref)
    pad_ref[0:heads, :] = decay_ref[...]
    log_decay = pad_ref[...]
    lower = jnp.where(iota((rows, rows), 0) >= iota((rows, rows), 1), 1.0, 0.0).astype(F32)
    cum_col = lax.dot_general(
        lower, log_decay, (((1,), (1,)), ((), ())), precision=lax.Precision.HIGHEST, preferred_element_type=F32
    )
    cum_row = lax.dot_general(
        log_decay, lower, (((1,), (1,)), ((), ())), precision=lax.Precision.HIGHEST, preferred_element_type=F32
    )
    row_ref[...] = cum_row
    col_ref[...] = cum_col
    to_end = jnp.exp(cum_col[rows - 1 : rows, :] - cum_col)
    hi, lo = split_hi_lo(jnp.exp(cum_col[rows - 1 : rows, :]))
    for s in range(shares):
        pay_ref[s, share_rows : share_rows + PAD, :] = jnp.concatenate(
            [jnp.broadcast_to(hi, (8, LANES)), jnp.broadcast_to(lo, (8, LANES))], axis=0
        )
    for h in range(heads):
        cols = slice(h * HEAD, (h + 1) * HEAD)
        keyed = (k_ref[:, cols].astype(F32) * to_end[:, h : h + 1]).astype(BF16)
        state = tn(keyed, v_ref[:, cols]).astype(BF16)
        at = h * HEAD
        while at < (h + 1) * HEAD:
            share, inner = divmod(at, share_rows)
            take = min(share_rows - inner, (h + 1) * HEAD - at)
            pay_ref[share, inner : inner + take, :] = state[at - h * HEAD : at - h * HEAD + take, :]
            at += take


def local_kernel(heads, q_ref, k_ref, v_ref, row_ref, col_ref, out_ref):
    rows = q_ref.shape[0]
    causal = iota((rows, rows), 0) >= iota((rows, rows), 1)
    for h in range(heads):
        cols = slice(h * HEAD, (h + 1) * HEAD)
        scores = nt(q_ref[:, cols], k_ref[:, cols])
        spread = col_ref[:, h : h + 1] - row_ref[h : h + 1, :]
        weights = jnp.where(causal, scores * jnp.exp(jnp.where(causal, spread, 0.0)), 0.0).astype(BF16)
        out_ref[:, cols] = nn(weights, v_ref[:, cols])


def place_kernel(held, ids_ref, prio_ref, place_ref):
    rows = ids_ref.shape[1]
    order = prio_ref[...].astype(F32)
    across = jnp.broadcast_to(order, (rows, rows))
    earlier = jnp.where(across.T < across, 1.0, 0.0).astype(BF16)
    ids = ids_ref[...]
    expert = iota((8 * pl.cdiv(held, 8), rows), 0)
    hit = expert == ids[0:1, :]
    for i in range(1, ids.shape[0]):
        hit = hit | (expert == ids[i : i + 1, :])
    member = jnp.where(hit, 1.0, 0.0)
    rank = nn(member.astype(BF16), earlier)
    slot = iota((CAP, rows), 0).astype(F32)
    for e in range(held):
        chosen = (member[e : e + 1, :] > 0.5) & (rank[e : e + 1, :] == slot)
        place_ref[e * CAP : (e + 1) * CAP, :] = jnp.where(chosen, 1.0, 0.0)


def scan_kernel(shares, share_rows, in_ref, out_ref):
    me = lax.axis_index("seq")
    row = me * share_rows + iota((share_rows, LANES), 0)
    onehot = jnp.where(row // HEAD == iota((share_rows, LANES), 1), 1.0, 0.0)
    carry = jnp.zeros((share_rows, LANES), F32)
    for b in range(shares):
        out_ref[b, :, :] = carry.astype(BF16)
        if b + 1 < shares:
            tail = in_ref[b, share_rows : share_rows + PAD, :].astype(F32)
            decay = tail[0:1, :] + tail[8:9, :]
            each = jnp.sum(onehot * decay, axis=1, keepdims=True)
            carry = each * carry + in_ref[b, 0:share_rows, :].astype(F32)


def mix_kernel(
    heads, held, copies, q_ref, local_ref, carried_ref, col_ref, res_ref, again_ref, ngain_ref, router_ref, place_ref,
    mixed_ref, slots_ref, stats_ref,
):
    rows = q_ref.shape[0]
    width = heads * HEAD
    experts = router_ref.shape[0]
    place = place_ref[...].astype(BF16)
    grow = jnp.exp(col_ref[...])
    squares = jnp.zeros((rows, 1), F32)
    picked_squares = jnp.zeros((held * CAP, 1), F32)
    logits = jnp.zeros((experts, rows), F32)
    for h in range(heads):
        cols = slice(h * HEAD, (h + 1) * HEAD)
        inter = nn(q_ref[:, cols], carried_ref[h * HEAD : (h + 1) * HEAD, :])
        attended = local_ref[:, cols] + grow[:, h : h + 1] * inter
        power = jnp.mean(attended * attended, axis=1, keepdims=True)
        normed = attended * lax.rsqrt(power + EPS) * again_ref[:, cols]
        mixed = (res_ref[:, cols].astype(F32) + normed).astype(BF16)
        mixed_ref[:, cols] = mixed
        mixed_f = mixed.astype(F32)
        squares += jnp.sum(mixed_f * mixed_f, axis=1, keepdims=True)
        hi, lo = split_hi_lo(mixed_f * ngain_ref[:, cols])
        logits += nt(router_ref[:, cols], hi) + nt(router_ref[:, cols], lo)
        picked = nn(place, mixed)
        picked_squares += jnp.sum(picked * picked, axis=1, keepdims=True)
        sent = (picked * ngain_ref[:, cols]).astype(BF16)
        for s in range(copies):
            for e in range(held):
                slots_ref[s, e, :, cols] = sent[e * CAP : (e + 1) * CAP, :]
    lane = iota((held * CAP, LANES), 1)
    hi, lo = split_hi_lo(picked_squares)
    extra = jnp.where(lane == 0, hi.astype(F32), jnp.where(lane == 1, lo.astype(F32), 0.0)).astype(BF16)
    for s in range(copies):
        for e in range(held):
            slots_ref[s, e, :, width : width + LANES] = extra[e * CAP : (e + 1) * CAP, :]
    stats_ref[0:experts, :] = logits
    stats_ref[experts : experts + 8, :] = jnp.broadcast_to(squares, (rows, rows)).T[0:8, :]


def gate_up_kernel(seqs, held, width, chunk, in_ref, gate_ref, up_ref, out_ref, x_ref, acc_g, acc_u):
    step = pl.program_id(0)
    per = width // chunk

    @pl.when(step == 0)
    def _():
        for s in range(seqs):
            for k in range(held):
                for p in range(per):
                    x_ref[k * per + p, s * CAP : (s + 1) * CAP, :] = in_ref[s * held + k, :, p * chunk : (p + 1) * chunk]
        acc_g[...] = jnp.zeros_like(acc_g)
        acc_u[...] = jnp.zeros_like(acc_u)

    x = x_ref[step]
    acc_g[...] += nn(x, gate_ref[0])
    acc_u[...] += nn(x, up_ref[0])

    @pl.when(step == pl.num_programs(0) - 1)
    def _():
        parts = []
        for s in range(seqs):
            total = jnp.zeros((CAP, 1), F32)
            for k in range(held):
                tail = in_ref[s * held + k, :, width : width + LANES].astype(F32)
                total += tail[:, 0:1] + tail[:, 1:2]
            parts.append(total)
        squares = jnp.concatenate(parts, axis=0)
        inverse = lax.rsqrt(squares / (held * width) + EPS)
        gate = acc_g[...] * inverse
        up = acc_u[...] * inverse
        out_ref[...] = (gate * (1.0 / (1.0 + jnp.exp(-gate))) * up).astype(BF16)


def down_kernel(seqs, order_ref, h_ref, w_ref, out_ref, acc):
    step = pl.program_id(0)

    @pl.when(step == 0)
    def _():
        acc[...] = jnp.zeros_like(acc)

    acc[...] += nn(h_ref[0], w_ref[0])

    @pl.when(step == pl.num_programs(0) - 1)
    def _():
        for s in range(seqs):
            out_ref[s, :, :] = acc[s * CAP : (s + 1) * CAP, :].astype(BF16)


def gates_kernel(held, total_width, parts, *refs):
    stats_refs, (ids_ref, place_ref, hi_ref, lo_ref) = refs[:parts], refs[parts:]
    total = stats_refs[0][...]
    for ref in stats_refs[1:]:
        total = total + ref[...]
    experts = total.shape[0] - 8
    inverse = lax.rsqrt(total[experts : experts + 1, :] / total_width + EPS)
    logits = total[0:experts, :] * inverse
    probs = 1.0 / (1.0 + jnp.exp(-logits))
    expert = iota(probs.shape, 0)
    ids = ids_ref[...]
    chosen = [
        jnp.sum(jnp.where(expert == ids[i : i + 1, :], probs, 0.0), axis=0, keepdims=True) for i in range(ids.shape[0])
    ]
    norm = chosen[0]
    for c in chosen[1:]:
        norm = norm + c
    for e in range(held):
        gate = jnp.zeros_like(norm)
        for i, c in enumerate(chosen):
            gate += jnp.where(ids[i : i + 1, :] == e, c / norm, 0.0)
        hi, lo = split_hi_lo(place_ref[e * CAP : (e + 1) * CAP, :] * gate)
        hi_ref[e * CAP : (e + 1) * CAP, :] = hi.astype(F32)
        lo_ref[e * CAP : (e + 1) * CAP, :] = lo.astype(F32)


def combine_kernel(held, mixed_ref, hi_ref, lo_ref, *refs):
    y_refs, out_ref = refs[:-1], refs[-1]
    if len(y_refs) > 1:
        y = jnp.concatenate([r[...].astype(F32) for r in y_refs], axis=0).astype(BF16)
    else:
        y = jnp.concatenate([y_refs[0][e].astype(F32) for e in range(held)], axis=0).astype(BF16)
    extra = tn(hi_ref[...].astype(BF16), y) + tn(lo_ref[...].astype(BF16), y)
    out_ref[...] = (mixed_ref[...].astype(F32) + extra).astype(BF16)


def call(body, out_shape, args, name, scratch=(), flops=0, nbytes=0):
    return pl.pallas_call(
        body,
        out_shape=out_shape,
        in_specs=[VMEM] * len(args),
        out_specs=jax.tree.map(lambda _: VMEM, out_shape),
        scratch_shapes=list(scratch),
        name=name,
        cost_estimate=pl.CostEstimate(flops=flops or 1000, bytes_accessed=nbytes or 1000, transcendentals=0),
    )(*args)


def shaped(shape, dtype):
    return jax.ShapeDtypeStruct(shape, dtype)


def body(
    residual, query_rows, key_rows, value_rows, log_decay, attn_gain, norm_gain, router, expert_ids, priority,
    gate_weight, up_weight, down_weight,
):
    rows, width = residual.shape
    heads = width // HEAD
    held = lax.axis_size("exp")
    seqs = lax.axis_size("seq")
    experts = router.shape[1]
    share_rows = width // seqs
    hidden_part = gate_weight.shape[2]
    out_part = down_weight.shape[2]
    ids = expert_ids.T
    payload, cum_row, cum_col = call(
        functools.partial(state_kernel, heads, seqs, share_rows),
        (
            shaped((seqs, share_rows + PAD, LANES), BF16),
            shaped((LANES, rows), F32),
            shaped((rows, LANES), F32),
        ),
        (key_rows, value_rows, log_decay.T),
        "state",
        scratch=[pltpu.VMEM((LANES, rows), F32)],
        flops=60_000_000,
        nbytes=1_200_000,
    )
    arrived = lax.all_to_all(payload, "seq", split_axis=0, concat_axis=0, tiled=True)
    local = call(
        functools.partial(local_kernel, heads),
        shaped((rows, width), F32),
        (query_rows, key_rows, value_rows, cum_row, cum_col),
        "local",
        flops=200_000_000,
        nbytes=2_000_000,
    )
    place = call(
        functools.partial(place_kernel, held),
        shaped((held * CAP, rows), F32),
        (ids, priority),
        "place",
    )
    prefix = call(
        functools.partial(scan_kernel, seqs, share_rows),
        shaped((seqs, share_rows, LANES), BF16),
        (arrived,),
        "scan",
    )
    carried = lax.all_to_all(prefix, "seq", split_axis=0, concat_axis=0, tiled=True).reshape(width, LANES)
    mixed, slots, stats = call(
        functools.partial(mix_kernel, heads, held, seqs),
        (
            shaped((rows, width), BF16),
            shaped((seqs, held, CAP, width + LANES), BF16),
            shaped((experts + 8, rows), F32),
        ),
        (
            query_rows, local, carried, cum_col, residual, attn_gain[None], norm_gain[None], router.T, place,
        ),
        "mix",
        flops=200_000_000,
        nbytes=3_000_000,
    )
    slots = slots.reshape(seqs * held, CAP, width + LANES)
    gathered = lax.all_to_all(slots, ("seq", "exp"), split_axis=0, concat_axis=0, tiled=True)
    stat_parts = [stats]
    for r in range(1, held):
        stat_parts.append(lax.ppermute(stats, "exp", [(i, (i + r) % held) for i in range(held)]))
    slot_rows = seqs * CAP
    chunk = width // 2
    hidden = pl.pallas_call(
        functools.partial(gate_up_kernel, seqs, held, width, chunk),
        out_shape=shaped((slot_rows, hidden_part), BF16),
        grid=(held * width // chunk,),
        in_specs=[
            VMEM,
            pl.BlockSpec((1, chunk, hidden_part), lambda i: (0, i, 0)),
            pl.BlockSpec((1, chunk, hidden_part), lambda i: (0, i, 0)),
        ],
        out_specs=pl.BlockSpec((slot_rows, hidden_part), lambda i: (0, 0)),
        scratch_shapes=[
            pltpu.VMEM((held * width // chunk, slot_rows, chunk), BF16),
            pltpu.VMEM((slot_rows, hidden_part), F32),
            pltpu.VMEM((slot_rows, hidden_part), F32),
        ],
        name="gate_up",
        cost_estimate=pl.CostEstimate(flops=900_000_000, bytes_accessed=28_000_000, transcendentals=0),
    )(gathered, gate_weight, up_weight)
    me = lax.axis_index("seq")
    if seqs <= 8:
        parts = [hidden]
        for r in range(1, seqs):
            parts.append(lax.ppermute(hidden, "seq", [(i, (i + r) % seqs) for i in range(seqs)]))
        whole = jnp.stack(parts)
        order = jnp.mod(me - jnp.arange(seqs, dtype=jnp.int32), seqs)
    else:
        whole = lax.all_gather(hidden, "seq", axis=0)
        order = jnp.arange(seqs, dtype=jnp.int32)
    expert_out = pl.pallas_call(
        functools.partial(down_kernel, seqs),
        out_shape=shaped((seqs, CAP, out_part), BF16),
        grid_spec=pltpu.PrefetchScalarGridSpec(
            num_scalar_prefetch=1,
            grid=(seqs,),
            in_specs=[
                pl.BlockSpec((1, slot_rows, hidden_part), lambda i, o: (i, 0, 0)),
                pl.BlockSpec((1, hidden_part, out_part), lambda i, o: (0, o[i], 0)),
            ],
            out_specs=pl.BlockSpec((seqs, CAP, out_part), lambda i, o: (0, 0, 0)),
            scratch_shapes=[pltpu.VMEM((slot_rows, out_part), F32)],
        ),
        name="down",
        cost_estimate=pl.CostEstimate(flops=450_000_000, bytes_accessed=14_000_000, transcendentals=0),
    )(order, whole, down_weight)
    if seqs == held:
        pieces = []
        for r in range(seqs):
            target = [
                (s * held + e, ((e + r) % seqs) * held + s) for s in range(seqs) for e in range(held)
            ]
            mine = lax.dynamic_index_in_dim(
                expert_out, jnp.mod(lax.axis_index("exp") + r, seqs), axis=0, keepdims=False
            )
            pieces.append(lax.ppermute(mine, ("seq", "exp"), target))
        stacked = jnp.stack(pieces)
        source = jnp.mod(me - jnp.arange(held, dtype=jnp.int32), held)
        y = (jnp.take(stacked, source, axis=0),)
    else:
        returned = lax.all_to_all(expert_out, "seq", split_axis=0, concat_axis=1, tiled=True)
        returned = returned.reshape(CAP, seqs * out_part)
        y = (lax.all_to_all(returned[None], "exp", split_axis=2, concat_axis=0, tiled=True),)
    hi, lo = call(
        functools.partial(gates_kernel, held, held * width, len(stat_parts)),
        (shaped((held * CAP, rows), F32),) * 2,
        (*stat_parts, ids, place),
        "gates",
    )
    return call(
        functools.partial(combine_kernel, held),
        shaped((rows, width), BF16),
        (mixed, hi, lo, *y),
        "combine",
    )


def solution(mesh):
    token = P(("groups", "seq"), "exp")
    return jax.shard_map(
        body,
        mesh=mesh,
        in_specs=(
            token, token, token, token, token, P("exp"), P("exp"), P("exp", None),
            P(("groups", "seq"), None), P(("groups", "seq"), None),
            P("exp", None, "seq"), P("exp", None, "seq"), P("exp", None, "seq"),
        ),
        out_specs=token,
        check_vma=False,
    )
```

time: 218 us -> 110 us (0.50); the launches traced: 215 us -> 109 us
  Pallas kernels: 0 us -> 41.5 us
  other arithmetic: 40.8 us -> 2.96 us
  local copies, waits for them, and re-layouts: 39.9 us -> 6.03 us
  blocking collectives: 45.4 us -> 17 us
  matrix products: 27.1 us -> 0 us
  waiting for transfers between devices: 37.5 us -> 19.3 us
    pallas_call x0 -> x9, Pallas kernels: none -> 41.5 us  [the longest x7 20 us: call(): pl.pallas_call(body, out_shape=out_shape, in_specs=[VMEM] * len(args), ou...]
    unnamed x2 -> x0, other arithmetic: 34.4 us -> none
    all_gather x2 -> x0, blocking collectives: 29.4 us -> none  [the longest x1 15.2 us: body(): gathered = lax.all_gather(arrived, 'seq', axis=0, tiled=True)]
    dot_general x11 -> x0, matrix products: 27.1 us -> none  [the longest x1 7.56 us: body(): up = jnp.dot(gathered, up_weight[0], preferred_element_type=jnp.float32)]
    all_to_all x6 -> x2, waiting for transfers between devices: 37.5 us -> 13.8 us  [the longest x1 10.9 us: body(): lax.all_to_all(slots, ('seq', 'exp'), split_axis=0, concat_axis=0, tiled=...]
    all_to_all x0 -> x1, blocking collectives: none -> 17 us  [body(): lax.all_to_all(payload, 'seq', split_axis=0, concat_axis=0, tiled=True)]
    slice x6 -> x0, local copies, waits for them, and re-layouts: 16.5 us -> none  [the longest x5 15.9 us: body(): lax.associative_scan(link_states, (element_decay, arrived_state), axis=0)[1]]
    psum x2 -> x0, blocking collectives: 16 us -> none  [the longest x1 10.1 us: body(): lax.psum(jnp.dot(scaled, router_f, precision=lax.Precision.HIGHEST), 'exp')]
  transfers between devices with their start and end apart: 6 -> 12, of which waited for: 5 -> 4; matrix products, arithmetic and copies ran while one was open for 8% -> 5% of each run, Pallas kernels for 0% -> 14%
where the time goes in v1:
time: 110 us; the launch traced here: 109 us
  Pallas kernels  41.5 us (38%)
  starting transfers between devices  22 us (20%)
  waiting for transfers between devices  19.3 us (18%)
  blocking collectives  17 us (15%)
  local copies, waits for them, and re-layouts  6.03 us (5%)
  other arithmetic  2.96 us (3%)
    pallas_call x7, Pallas kernels, call(): pl.pallas_call(body, out_shape=out_shape, in_specs=[VMEM] * len(args), ou...  20 us
    all_to_all x1, blocking collectives, body(): lax.all_to_all(payload, 'seq', split_axis=0, concat_axis=0, tiled=True)  17 us
    pallas_call x1, Pallas kernels, body(): pl.pallas_call(functools.partial(gate_up_kernel, seqs, held, width, chunk...  13.3 us
    all_to_all x1, waiting for transfers between devices, body(): lax.all_to_all(slots, ('seq', 'exp'), split_axis=0, concat_axis=0, tiled=...  10.9 us
    pallas_call x1, Pallas kernels, body(): pl.pallas_call(functools.partial(down_kernel, seqs), out_shape=shaped((se...  8.16 us
    ppermute x4, starting transfers between devices, body(): pieces.append(lax.ppermute(mine, ('seq', 'exp'), target))  7.07 us
    all_to_all x1, starting transfers between devices, body(): lax.all_to_all(slots, ('seq', 'exp'), split_axis=0, concat_axis=0, tiled=...  4.21 us
    ppermute x3, starting transfers between devices, body(): lax.ppermute(stats, 'exp', [(i, (i + r) % held) for i in range(held)])  3.94 us
  transfers between devices with their start and end apart: 12, of which 4 were waited for; matrix products, arithmetic and copies ran while one was open for 5% of the time, Pallas kernels for 14%

profile of v1, /device:TPU:2, one launch (start us, length us, event | category | flops | bytes accessed | tf_op | source)
XLA Modules:
  0.0 108.9 jit_solution(1295267622683376925)
XLA Ops:
  0.0 2.8 %state.1 = (bf16[4,400,128]{2,1,0:T(8,128)(2,1)}, f32[128,128]{1,0:T(8,128)}, f32[128,128]{1,0:T(8,128)}) custom-call(bf16[128,1536]{1,0:T(8,128)(2,1)} %k_ref.3, bf16[128,1536]{1,0:T(8,128)(2,1)} %v_ref.3, f32[12,128]{1,0:T(8,128)} %bitcast.34), custom_call_target="tpu_custom_call" | custom-call | flops 60000000 | bytes 1200000 | tf_op jit(solution)/shard_map/state/pallas_call | solution.py:242
  2.8 17.0 %all_to_all.15.in_ref = bf16[4,400,128]{2,1,0:T(8,128)(2,1)} all-to-all(bf16[4,400,128]{2,1,0:T(8,128)(2,1)} %get-tuple-element.15), channel_id=1, replica_groups=mesh['groups'=2,'seq'=4,'exp'=4] {'seq'}, dimensions={0} | all-to-all | bytes 819200 | tf_op jit(solution)/shard_map/all_to_all | solution.py:283
  19.8 2.1 %scan.1 = bf16[4,384,128]{2,1,0:T(8,128)(2,1)} custom-call(bf16[4,400,128]{2,1,0:T(8,128)(2,1)} %all_to_all.15.in_ref), custom_call_target="tpu_custom_call" | custom-call | flops 1000 | bytes 1000 | tf_op jit(solution)/shard_map/scan/pallas_call | solution.py:242
  21.9 3.5 %all-to-all-start.1 = ((bf16[4,384,128]{2,1,0:T(8,128)(2,1)}), bf16[4,384,128]{2,1,0:T(8,128)(2,1)S(1)}, u32[]{:S(2)}, u32[]{:S(2)}) async-start(bf16[4,384,128]{2,1,0:T(8,128)(2,1)} %scan.1), calls=%async_computation.1 | async-start | bytes 786432 | tf_op jit(solution)/shard_map/all_to_all | solution.py:304
  25.3 1.5 %place.1.place_ref.refs_5_ = f32[32,128]{1,0:T(8,128)} custom-call(s32[2,128]{1,0:T(2,128)} %bitcast.35, s32[1,128]{1,0:T(1,128)} %prio_ref.1), custom_call_target="tpu_custom_call" | custom-call | flops 1000 | bytes 1000 | tf_op jit(solution)/shard_map/place/pallas_call | solution.py:242
  26.8 1.3 %broadcast_in_dim.16.again_ref = f32[1,1536]{1,0:T(1,128)} reshape(f32[1536]{0:T(1024)} %param.18) | data formatting | bytes 12288 | tf_op jit(solution)/shard_map/broadcast_in_dim | solution.py:313
  28.1 1.3 %broadcast_in_dim.17.ngain_ref = f32[1,1536]{1,0:T(1,128)} reshape(f32[1536]{0:T(1024)} %param.19) | data formatting | bytes 12288 | tf_op jit(solution)/shard_map/broadcast_in_dim | solution.py:313
  29.4 4.1 %local.1.local_ref = f32[128,1536]{1,0:T(8,128)} custom-call(bf16[128,1536]{1,0:T(8,128)(2,1)} %q_ref.3, bf16[128,1536]{1,0:T(8,128)(2,1)} %k_ref.3, bf16[128,1536]{1,0:T(8,128)(2,1)} %v_ref.3, f32[128,128]{1,0:T(8,128)} %get-tuple-element.13.row_ref, f32[128,128]{1,0:T(8,128)} %get-tuple-element.14.col_ref), custom_call_target="tpu_custom_call" | custom-call | flops 200000000 | bytes 2000000 | tf_op jit(solution)/shard_map/local/pallas_call | solution.py:242
  33.5 2.9 %all-to-all-done.1 = bf16[4,384,128]{2,1,0:T(8,128)(2,1)S(1)} async-done(((bf16[4,384,128]{2,1,0:T(8,128)(2,1)}), bf16[4,384,128]{2,1,0:T(8,128)(2,1)S(1)}, u32[]{:S(2)}, u32[]{:S(2)}) %all-to-all-start.1) | async-done | bytes 393248 | tf_op jit(solution)/shard_map/all_to_all | solution.py:304
  36.5 0.7 copy-done.1
  37.2 5.9 %mix.1 = (bf16[128,1536]{1,0:T(8,128)(2,1)}, bf16[4,4,8,1664]{3,2,1,0:T(8,128)(2,1)}, f32[40,128]{1,0:T(8,128)}) custom-call(bf16[128,1536]{1,0:T(8,128)(2,1)} %q_ref.3, f32[128,1536]{1,0:T(8,128)} %local.1.local_ref, bf16[1536,128]{1,0:T(8,128)(2,1)} %bitcast.23, f32[128,128]{1,0:T(8,128)} %get-tuple-element.14.col_ref, bf16[128,1536]{1,0:T(8,128)(2,1)} %res_ref.1, ...), custom_call_target="tpu_custom_call" | custom-call | flops 200000000 | bytes 3000000 | tf_op jit(solution)/shard_map/mix/pallas_call | solution.py:242
  43.1 4.2 %all-to-all-start.2 = ((bf16[16,8,1664]{2,1,0:T(8,128)(2,1)}), bf16[16,8,1664]{2,1,0:T(8,128)(2,1)S(1)}, u32[]{:S(2)}, u32[]{:S(2)}) async-start(bf16[16,8,1664]{2,1,0:T(8,128)(2,1)} %bitcast.24), calls=%async_computation.2 | async-start | bytes 851968 | tf_op jit(solution)/shard_map/all_to_all | solution.py:320
  47.4 10.9 %all-to-all-done.2.in_ref = bf16[16,8,1664]{2,1,0:T(8,128)(2,1)S(1)} async-done(((bf16[16,8,1664]{2,1,0:T(8,128)(2,1)}), bf16[16,8,1664]{2,1,0:T(8,128)(2,1)S(1)}, u32[]{:S(2)}, u32[]{:S(2)}) %all-to-all-start.2) | async-done | bytes 426016 | tf_op jit(solution)/shard_map/all_to_all | solution.py:320
  58.3 0.8 copy-done
  59.0 13.3 %gate_up.1 = bf16[32,1152]{1,0:T(8,128)(2,1)} custom-call(bf16[16,8,1664]{2,1,0:T(8,128)(2,1)} %copy-done, bf16[1,6144,1152]{2,1,0:T(8,128)(2,1)} %gate_ref.1, bf16[1,6144,1152]{2,1,0:T(8,128)(2,1)} %up_ref.1), custom_call_target="tpu_custom_call" | custom-call | flops 900000000 | bytes 28000000 | tf_op jit(solution)/shard_map/gate_up/pallas_call | solution.py:326
  72.4 2.6 %collective-permute-start.5 = (bf16[32,1152]{1,0:T(8,128)(2,1)}, bf16[32,1152]{1,0:T(8,128)(2,1)S(1)}, u32[]{:S(2)}, u32[]{:S(2)}) collective-permute-start(bf16[32,1152]{1,0:T(8,128)(2,1)} %gate_up.1), channel_id=1, source_target_pairs={{0,12},{4,0},{8,4},{12,8},{1,13},{5,1},{9,5},{13,9},{2,14},{6,2},{... | collective-permute-start | bytes 221192 | tf_op jit(solution)/shard_map/ppermute | solution.py:348
  75.0 0.6 collective-permute-start.4
  76.2 2.5 %collective-permute-start.1 = (f32[40,128]{1,0:T(8,128)S(1)}, f32[40,128]{1,0:T(8,128)S(1)}, u32[]{:S(2)}, u32[]{:S(2)}) collective-permute-start(f32[40,128]{1,0:T(8,128)S(1)} %copy-done.2), channel_id=1, source_target_pairs={{0,2},{1,3},{2,0},{3,1},{4,6},{5,7},{6,4},{7,5},{8,10},{9,11},{10,... | collective-permute-start | bytes 61448 | tf_op jit(solution)/shard_map/ppermute | solution.py:323
  78.7 1.5 %collective-permute-start.2 = (f32[40,128]{1,0:T(8,128)S(1)}, f32[40,128]{1,0:T(8,128)S(1)}, u32[]{:S(2)}, u32[]{:S(2)}) collective-permute-start(f32[40,128]{1,0:T(8,128)S(1)} %copy-done.2), channel_id=1, source_target_pairs={{0,3},{1,0},{2,1},{3,2},{4,7},{5,4},{6,5},{7,6},{8,11},{9,8},{10,9... | collective-permute-start | bytes 61448 | tf_op jit(solution)/shard_map/ppermute | solution.py:323
  80.2 2.9 %collective-permute-done.4 = bf16[32,1152]{1,0:T(8,128)(2,1)S(1)} collective-permute-done((bf16[32,1152]{1,0:T(8,128)(2,1)}, bf16[32,1152]{1,0:T(8,128)(2,1)S(1)}, u32[]{:S(2)}, u32[]{:S(2)}) %collective-permute-start.4) | collective-permute-done | bytes 73760 | tf_op jit(solution)/shard_map/ppermute | solution.py:348
  83.0 1.6 %pad_maximum_fusion.h_ref = bf16[4,32,1152]{2,1,0:T(8,128)(2,1)} fusion(bf16[1,32,1152]{2,1,0:T(8,128)(2,1)S(1)} %bitcast.27, bf16[1,32,1152]{2,1,0:T(8,128)(2,1)S(1)} %bitcast.28, bf16[1,32,1152]{2,1,0:T(8,128)(2,1)S(1)} %bitcast.29, bf16[1,32,1152]{2,1,0:T(8,128)(2,1)} %bitcast.25), kind=kLoop, calls=%fused_computation.1 | loop fusion | flops 442368 | bytes 589824 | tf_op jit(solution)/shard_map/stack | solution.py:349
  84.7 8.2 %down.1 = bf16[4,8,1536]{2,1,0:T(8,128)(2,1)} custom-call(s32[4]{0:T(128)} %and_select_fusion.1.order_ref, bf16[4,32,1152]{2,1,0:T(8,128)(2,1)} %pad_maximum_fusion.h_ref, bf16[1,4608,1536]{2,1,0:T(8,128)(2,1)} %w_ref.1), custom_call_target="tpu_custom_call" | custom-call | flops 450000000 | bytes 14000000 | tf_op jit(solution)/shard_map/down/pallas_call | solution.py:354
  92.9 0.8 dynamic-slice_bitcast_fusion.3
  94.1 2.0 %collective-permute-start.8 = (bf16[8,1536]{1,0:T(8,128)(2,1)S(1)}, bf16[8,1536]{1,0:T(8,128)(2,1)S(1)}, u32[]{:S(2)}, u32[]{:S(2)}) collective-permute-start(bf16[8,1536]{1,0:T(8,128)(2,1)S(1)} %get-tuple-element.23), channel_id=1, source_target_pairs={{0,8},{1,12},{2,0},{3,4},{4,9},{5,13},{6,1},{7,5},{8,10},{9,14},{1... | collective-permute-start | bytes 73736 | tf_op jit(solution)/shard_map/ppermute | solution.py:379
  96.2 1.5 %collective-permute-start.7 = (bf16[8,1536]{1,0:T(8,128)(2,1)S(1)}, bf16[8,1536]{1,0:T(8,128)(2,1)S(1)}, u32[]{:S(2)}, u32[]{:S(2)}) collective-permute-start(bf16[8,1536]{1,0:T(8,128)(2,1)S(1)} %get-tuple-element.24), channel_id=1, source_target_pairs={{0,4},{1,8},{2,12},{3,0},{4,5},{5,9},{6,13},{7,1},{8,6},{9,10},{10... | collective-permute-start | bytes 73736 | tf_op jit(solution)/shard_map/ppermute | solution.py:379
  97.6 3.1 %collective-permute-start.6 = (bf16[8,1536]{1,0:T(8,128)(2,1)S(1)}, bf16[8,1536]{1,0:T(8,128)(2,1)S(1)}, u32[]{:S(2)}, u32[]{:S(2)}) collective-permute-start(bf16[8,1536]{1,0:T(8,128)(2,1)S(1)} %get-tuple-element.21), channel_id=1, source_target_pairs={{0,0},{1,4},{2,8},{3,12},{4,1},{5,5},{6,9},{7,13},{8,2},{9,6},{10,... | collective-permute-start | bytes 73736 | tf_op jit(solution)/shard_map/ppermute | solution.py:379
  100.8 0.6 copy-done.5
  101.4 1.5 %gates.1 = (f32[32,128]{1,0:T(8,128)}, f32[32,128]{1,0:T(8,128)}) custom-call(f32[40,128]{1,0:T(8,128)} %get-tuple-element.17.refs_0_, f32[40,128]{1,0:T(8,128)} %copy-done.3, f32[40,128]{1,0:T(8,128)} %copy-done.4, f32[40,128]{1,0:T(8,128)} %copy-done.5, s32[2,128]{1,0:T(2,128)} %bitcast.36, f32[32,128]{1,0:T(8,128)} %place.1.place_ref.refs_5_), custom_call_target="tpu_custom_call" | custom-call | flops 1000 | bytes 1000 | tf_op jit(solution)/shard_map/gates/pallas_call | solution.py:242
  102.9 2.5 %collective-permute-done.6 = bf16[8,1536]{1,0:T(8,128)(2,1)S(1)} collective-permute-done((bf16[8,1536]{1,0:T(8,128)(2,1)S(1)}, bf16[8,1536]{1,0:T(8,128)(2,1)S(1)}, u32[]{:S(2)}, u32[]{:S(2)}) %collective-permute-start.6) | collective-permute-done | bytes 24608 | tf_op jit(solution)/shard_map/ppermute | solution.py:379
  105.4 0.6 gather_fusion
  106.0 0.7 broadcast_select_fusion.refs_0_
  106.7 2.2 %combine.1 = bf16[128,1536]{1,0:T(8,128)(2,1)} custom-call(bf16[128,1536]{1,0:T(8,128)(2,1)} %get-tuple-element.16.mixed_ref, f32[32,128]{1,0:T(8,128)} %get-tuple-element.18.hi_ref, f32[32,128]{1,0:T(8,128)} %get-tuple-element.19.lo_ref, bf16[4,8,1536]{2,1,0:T(8,128)(2,1)} %broadcast_select_fusion.refs_0_), custom_call_target="tpu_custom_call" | custom-call | flops 1000 | bytes 1000 | tf_op jit(solution)/shard_map/combine/pallas_call | solution.py:242
  (25 shorter events, 1.3 us)
Async XLA Ops:
  21.9 14.6 %all-to-all-start.1 = ((bf16[4,384,128]{2,1,0:T(8,128)(2,1)}), bf16[4,384,128]{2,1,0:T(8,128)(2,1)S(1)}, u32[]{:S(2)}, u32[]{:S(2)}) async-start(bf16[4,384,128]{2,1,0:T(8,128)(2,1)} %scan.1), calls=%async_computation.1 | async-start | bytes 786432 | tf_op jit(solution)/shard_map/all_to_all | solution.py:304
  36.5 0.7 copy-start.1
  43.1 15.2 %all-to-all-start.2 = ((bf16[16,8,1664]{2,1,0:T(8,128)(2,1)}), bf16[16,8,1664]{2,1,0:T(8,128)(2,1)S(1)}, u32[]{:S(2)}, u32[]{:S(2)}) async-start(bf16[16,8,1664]{2,1,0:T(8,128)(2,1)} %bitcast.24), calls=%async_computation.2 | async-start | bytes 851968 | tf_op jit(solution)/shard_map/all_to_all | solution.py:320
  47.4 28.9 %copy-start.2 = (f32[40,128]{1,0:T(8,128)S(1)}, f32[40,128]{1,0:T(8,128)}, u32[]{:S(2)}) copy-start(f32[40,128]{1,0:T(8,128)} %get-tuple-element.17.refs_0_) | copy-start | bytes 61444
  58.3 0.8 copy-start
  72.4 6.3 %collective-permute-start.5 = (bf16[32,1152]{1,0:T(8,128)(2,1)}, bf16[32,1152]{1,0:T(8,128)(2,1)S(1)}, u32[]{:S(2)}, u32[]{:S(2)}) collective-permute-start(bf16[32,1152]{1,0:T(8,128)(2,1)} %gate_up.1), channel_id=1, source_target_pairs={{0,12},{4,0},{8,4},{12,8},{1,13},{5,1},{9,5},{13,9},{2,14},{6,2},{... | collective-permute-start | bytes 221192 | tf_op jit(solution)/shard_map/ppermute | solution.py:348
  75.0 8.1 %collective-permute-start.4 = (bf16[32,1152]{1,0:T(8,128)(2,1)}, bf16[32,1152]{1,0:T(8,128)(2,1)S(1)}, u32[]{:S(2)}, u32[]{:S(2)}) collective-permute-start(bf16[32,1152]{1,0:T(8,128)(2,1)} %gate_up.1), channel_id=1, source_target_pairs={{0,8},{4,12},{8,0},{12,4},{1,9},{5,13},{9,1},{13,5},{2,10},{6,14},... | collective-permute-start | bytes 221192 | tf_op jit(solution)/shard_map/ppermute | solution.py:348
  75.6 7.5 %collective-permute-start.3 = (bf16[32,1152]{1,0:T(8,128)(2,1)}, bf16[32,1152]{1,0:T(8,128)(2,1)S(1)}, u32[]{:S(2)}, u32[]{:S(2)}) collective-permute-start(bf16[32,1152]{1,0:T(8,128)(2,1)} %gate_up.1), channel_id=1, source_target_pairs={{0,4},{4,8},{8,12},{12,0},{1,5},{5,9},{9,13},{13,1},{2,6},{6,10},{... | collective-permute-start | bytes 221192 | tf_op jit(solution)/shard_map/ppermute | solution.py:348
  76.2 20.0 %collective-permute-start = (f32[40,128]{1,0:T(8,128)S(1)}, f32[40,128]{1,0:T(8,128)S(1)}, u32[]{:S(2)}, u32[]{:S(2)}) collective-permute-start(f32[40,128]{1,0:T(8,128)S(1)} %copy-done.2), channel_id=1, source_target_pairs={{0,1},{1,2},{2,3},{3,0},{4,5},{5,6},{6,7},{7,4},{8,9},{9,10},{10,1... | collective-permute-start | bytes 61448 | tf_op jit(solution)/shard_map/ppermute | solution.py:323
  76.2 21.4 %collective-permute-start.1 = (f32[40,128]{1,0:T(8,128)S(1)}, f32[40,128]{1,0:T(8,128)S(1)}, u32[]{:S(2)}, u32[]{:S(2)}) collective-permute-start(f32[40,128]{1,0:T(8,128)S(1)} %copy-done.2), channel_id=1, source_target_pairs={{0,2},{1,3},{2,0},{3,1},{4,6},{5,7},{6,4},{7,5},{8,10},{9,11},{10,... | collective-permute-start | bytes 61448 | tf_op jit(solution)/shard_map/ppermute | solution.py:323
  78.7 22.0 %collective-permute-start.2 = (f32[40,128]{1,0:T(8,128)S(1)}, f32[40,128]{1,0:T(8,128)S(1)}, u32[]{:S(2)}, u32[]{:S(2)}) collective-permute-start(f32[40,128]{1,0:T(8,128)S(1)} %copy-done.2), channel_id=1, source_target_pairs={{0,3},{1,0},{2,1},{3,2},{4,7},{5,4},{6,5},{7,6},{8,11},{9,8},{10,9... | collective-permute-start | bytes 61448 | tf_op jit(solution)/shard_map/ppermute | solution.py:323
  93.7 9.2 %collective-permute-start.9 = (bf16[8,1536]{1,0:T(8,128)(2,1)S(1)}, bf16[8,1536]{1,0:T(8,128)(2,1)S(1)}, u32[]{:S(2)}, u32[]{:S(2)}) collective-permute-start(bf16[8,1536]{1,0:T(8,128)(2,1)S(1)} %get-tuple-element.22), channel_id=1, source_target_pairs={{0,12},{1,0},{2,4},{3,8},{4,13},{5,1},{6,5},{7,9},{8,14},{9,2},{10... | collective-permute-start | bytes 73736 | tf_op jit(solution)/shard_map/ppermute | solution.py:379
  94.1 8.7 %collective-permute-start.8 = (bf16[8,1536]{1,0:T(8,128)(2,1)S(1)}, bf16[8,1536]{1,0:T(8,128)(2,1)S(1)}, u32[]{:S(2)}, u32[]{:S(2)}) collective-permute-start(bf16[8,1536]{1,0:T(8,128)(2,1)S(1)} %get-tuple-element.23), channel_id=1, source_target_pairs={{0,8},{1,12},{2,0},{3,4},{4,9},{5,13},{6,1},{7,5},{8,10},{9,14},{1... | collective-permute-start | bytes 73736 | tf_op jit(solution)/shard_map/ppermute | solution.py:379
  96.2 4.6 %copy-start.3 = (f32[40,128]{1,0:T(8,128)}, f32[40,128]{1,0:T(8,128)S(1)}, u32[]{:S(2)}) copy-start(f32[40,128]{1,0:T(8,128)S(1)} %collective-permute-done.refs_1_) | copy-start | bytes 61444
  96.2 6.7 %collective-permute-start.7 = (bf16[8,1536]{1,0:T(8,128)(2,1)S(1)}, bf16[8,1536]{1,0:T(8,128)(2,1)S(1)}, u32[]{:S(2)}, u32[]{:S(2)}) collective-permute-start(bf16[8,1536]{1,0:T(8,128)(2,1)S(1)} %get-tuple-element.24), channel_id=1, source_target_pairs={{0,4},{1,8},{2,12},{3,0},{4,5},{5,9},{6,13},{7,1},{8,6},{9,10},{10... | collective-permute-start | bytes 73736 | tf_op jit(solution)/shard_map/ppermute | solution.py:379
  97.6 3.1 %copy-start.4 = (f32[40,128]{1,0:T(8,128)}, f32[40,128]{1,0:T(8,128)S(1)}, u32[]{:S(2)}) copy-start(f32[40,128]{1,0:T(8,128)S(1)} %collective-permute-done.1.refs_2_) | copy-start | bytes 61444
  97.6 7.8 %collective-permute-start.6 = (bf16[8,1536]{1,0:T(8,128)(2,1)S(1)}, bf16[8,1536]{1,0:T(8,128)(2,1)S(1)}, u32[]{:S(2)}, u32[]{:S(2)}) collective-permute-start(bf16[8,1536]{1,0:T(8,128)(2,1)S(1)} %get-tuple-element.21), channel_id=1, source_target_pairs={{0,0},{1,4},{2,8},{3,12},{4,1},{5,5},{6,9},{7,13},{8,2},{9,6},{10,... | collective-permute-start | bytes 73736 | tf_op jit(solution)/shard_map/ppermute | solution.py:379
  100.8 0.6 copy-start.5

commit v2 on v1

--- a/solution.py
+++ b/solution.py
@@ -7,13 +7,16 @@
 from jax.experimental.pallas import tpu as pltpu
 from jax.sharding import PartitionSpec as P
 
+
 HEAD = 128
 LANES = 128
 CAP = 8
 PAD = 16
 EPS = 1e-06
+SMALL = 8 << 20
 F32 = jnp.float32
 BF16 = jnp.bfloat16
+
 
 VMEM = pl.BlockSpec(memory_space=pltpu.VMEM)
 
@@ -238,14 +241,13 @@
     out_ref[...] = (mixed_ref[...].astype(F32) + extra).astype(BF16)
 
 
-def call(body, out_shape, args, name, scratch=(), flops=0, nbytes=0):
+def call(body, out_shape, args, scratch=(), flops=0, nbytes=0):
     return pl.pallas_call(
         body,
         out_shape=out_shape,
         in_specs=[VMEM] * len(args),
         out_specs=jax.tree.map(lambda _: VMEM, out_shape),
         scratch_shapes=list(scratch),
-        name=name,
         cost_estimate=pl.CostEstimate(flops=flops or 1000, bytes_accessed=nbytes or 1000, transcendentals=0),
     )(*args)
 
@@ -254,7 +256,7 @@
     return jax.ShapeDtypeStruct(shape, dtype)
 
 
-def body(
+def general_body(
     residual, query_rows, key_rows, value_rows, log_decay, attn_gain, norm_gain, router, expert_ids, priority,
     gate_weight, up_weight, down_weight,
 ):
@@ -275,7 +277,6 @@
             shaped((rows, LANES), F32),
         ),
         (key_rows, value_rows, log_decay.T),
-        "state",
         scratch=[pltpu.VMEM((LANES, rows), F32)],
         flops=60_000_000,
         nbytes=1_200_000,
@@ -285,22 +286,11 @@
         functools.partial(local_kernel, heads),
         shaped((rows, width), F32),
         (query_rows, key_rows, value_rows, cum_row, cum_col),
-        "local",
         flops=200_000_000,
         nbytes=2_000_000,
     )
-    place = call(
-        functools.partial(place_kernel, held),
-        shaped((held * CAP, rows), F32),
-        (ids, priority),
-        "place",
-    )
-    prefix = call(
-        functools.partial(scan_kernel, seqs, share_rows),
-        shaped((seqs, share_rows, LANES), BF16),
-        (arrived,),
-        "scan",
-    )
+    place = call(functools.partial(place_kernel, held), shaped((held * CAP, rows), F32), (ids, priority))
+    prefix = call(functools.partial(scan_kernel, seqs, share_rows), shaped((seqs, share_rows, LANES), BF16), (arrived,))
     carried = lax.all_to_all(prefix, "seq", split_axis=0, concat_axis=0, tiled=True).reshape(width, LANES)
     mixed, slots, stats = call(
         functools.partial(mix_kernel, heads, held, seqs),
@@ -312,7 +302,6 @@
         (
             query_rows, local, carried, cum_col, residual, attn_gain[None], norm_gain[None], router.T, place,
         ),
-        "mix",
         flops=200_000_000,
         nbytes=3_000_000,
     )
@@ -388,14 +377,357 @@
         functools.partial(gates_kernel, held, held * width, len(stat_parts)),
         (shaped((held * CAP, rows), F32),) * 2,
         (*stat_parts, ids, place),
-        "gates",
-    )
-    return call(
-        functools.partial(combine_kernel, held),
+    )
+    return call(functools.partial(combine_kernel, held), shaped((rows, width), BF16), (mixed, hi, lo, *y))
+
+
+def state_pieces_kernel(heads, seqs, k_ref, v_ref, decay_ref, *refs):
+    pieces, row_ref, col_ref, pad_ref, end_ref = refs[:seqs], *refs[seqs:]
+    rows = k_ref.shape[0]
+    per = heads // seqs
+    me = lax.axis_index("seq")
+    pad_ref[...] = jnp.zeros_like(pad_ref)
+    pad_ref[0:heads, :] = decay_ref[...]
+    log_decay = pad_ref[...]
+    lower = jnp.where(iota((rows, rows), 0) >= iota((rows, rows), 1), 1.0, 0.0).astype(F32)
+    cum_col = lax.dot_general(
+        lower, log_decay, (((1,), (1,)), ((), ())), precision=lax.Precision.HIGHEST, preferred_element_type=F32
+    )
+    cum_row = lax.dot_general(
+        log_decay, lower, (((1,), (1,)), ((), ())), precision=lax.Precision.HIGHEST, preferred_element_type=F32
+    )
+    row_ref[...] = cum_row
+    col_ref[...] = cum_col
+    end_ref[...] = jnp.exp(cum_row[:, rows - 1 : rows] - cum_row)
+    hi, lo = split_hi_lo(jnp.exp(cum_col[rows - 1 : rows, :]))
+    tail = jnp.concatenate([jnp.broadcast_to(hi, (8, LANES)), jnp.broadcast_to(lo, (8, LANES))], axis=0)
+    for r in range(seqs):
+        share = lax.rem(me + r, seqs)
+        for j in range(per):
+            h = share * per + j
+            cols = pl.ds(pl.multiple_of(h * HEAD, HEAD), HEAD)
+            keyed = (k_ref[:, cols].astype(F32).T * end_ref[pl.ds(h, 1), :]).astype(BF16)
+            pieces[r][j * HEAD : (j + 1) * HEAD, :] = nn(keyed, v_ref[:, cols]).astype(BF16)
+        pieces[r][per * HEAD : per * HEAD + PAD, :] = tail
+
+
+def pack_kernel(heads, router_ref, gain_ref, out_ref):
+    experts = router_ref.shape[0]
+    out_ref[0:experts, :] = router_ref[...]
+    hi, lo = split_hi_lo(gain_ref[...])
+    hi, lo = hi.astype(F32), lo.astype(F32)
+    at = iota((PAD, HEAD), 0)
+    for h in range(heads):
+        both = jnp.where(at == 0, hi[h : h + 1, :], jnp.where(at == 1, lo[h : h + 1, :], 0.0))
+        out_ref[experts : experts + PAD, h * HEAD : (h + 1) * HEAD] = both.astype(BF16)
+
+
+def rows_kernel(
+    heads, seqs, held, q_ref, k_ref, v_ref, res_ref, row_ref, col_ref, ids_ref, prio_ref, local_ref, grown_ref,
+    place_ref, *pieces,
+):
+    place_kernel(held, ids_ref, prio_ref, place_ref)
+    rows = q_ref.shape[0]
+    causal = iota((rows, rows), 0) >= iota((rows, rows), 1)
+    grow = jnp.exp(col_ref[...])
+    for h in range(heads):
+        cols = slice(h * HEAD, (h + 1) * HEAD)
+        q = q_ref[:, cols]
+        scores = nt(q, k_ref[:, cols])
+        spread = col_ref[:, h : h + 1] - row_ref[h : h + 1, :]
+        near = jnp.where(causal, scores * jnp.exp(jnp.where(causal, spread, 0.0)), 0.0).astype(BF16)
+        local_ref[:, cols] = nn(near, v_ref[:, cols])
+        grown_ref[:, cols] = (q.astype(F32) * grow[:, h : h + 1]).astype(BF16)
+    place = place_ref[...]
+    ids = ids_ref[...].astype(F32)
+    lane = iota((held * CAP, LANES), 1)
+    extra = jnp.zeros((held * CAP, LANES), F32)
+    for i in range(ids.shape[0]):
+        extra = jnp.where(lane == i, jnp.sum(place * ids[i : i + 1, :], axis=1, keepdims=True), extra)
+    place = place.astype(BF16)
+    me = lax.axis_index("seq")
+    part = heads * HEAD // seqs
+    for r in range(seqs):
+        cols = pl.ds(pl.multiple_of(lax.rem(me + r, seqs) * part, part), part)
+        pieces[r][:, 0:part] = nn(place, grown_ref[:, cols]).astype(BF16)
+        pieces[r][:, part : 2 * part] = nn(place, local_ref[:, cols].astype(BF16)).astype(BF16)
+        pieces[r][:, 2 * part : 3 * part] = nn(place, res_ref[:, cols]).astype(BF16)
+        pieces[r][:, 3 * part : 3 * part + LANES] = extra.astype(BF16)
+
+
+def keep_kernel(count, *refs):
+    sources, kept, sems = refs[1 : count + 1], refs[count + 1 : 2 * count + 1], refs[2 * count + 1]
+    copies = [pltpu.make_async_copy(w, b, sems.at[i]) for i, (w, b) in enumerate(zip(sources, kept))]
+    for copy in copies:
+        copy.start()
+    for copy in copies:
+        copy.wait()
+
+
+def owner_kernel(heads, seqs, held, again_ref, *refs):
+    states, rows_in = refs[:seqs], refs[seqs : 2 * seqs]
+    slots_ref, ids_ref, *rest = refs[2 * seqs :]
+    prefixes, (state_ref, rows_ref, prefix_ref) = rest[:seqs], rest[seqs:]
+    per = heads // seqs
+    part = per * HEAD
+    me = lax.axis_index("seq")
+    expert = lax.axis_index("exp")
+    for r in range(seqs):
+        b = lax.rem(me + seqs - r, seqs)
+        state_ref[b] = states[r][...]
+        rows_ref[b] = rows_in[r][...]
+        mine = rows_in[r][:, 3 * part : 3 * part + LANES].astype(F32)
+        picked = jnp.zeros((CAP, LANES), F32)
+        for e in range(held):
+            picked = jnp.where(expert == e, mine[e * CAP : (e + 1) * CAP, :], picked)
+        ids_ref[pl.ds(pl.multiple_of(b * CAP, CAP), CAP), :] = picked
+    lane = iota((1, LANES), 1)
+    for j in range(per):
+        h = me * per + j
+        again = again_ref[pl.ds(h, 1), :]
+        cols = slice(j * HEAD, (j + 1) * HEAD)
+        carry = jnp.zeros((HEAD, HEAD), F32)
+        for b in range(seqs):
+            prefix = carry.astype(BF16)
+            prefix_ref[b, cols, :] = prefix
+            attended = rows_ref[b, :, part + j * HEAD : part + (j + 1) * HEAD].astype(F32)
+            if b > 0:
+                attended = attended + nn(rows_ref[b, :, cols], prefix)
+            power = jnp.mean(attended * attended, axis=1, keepdims=True)
+            normed = attended * lax.rsqrt(power + EPS) * again
+            residual = rows_ref[b, :, 2 * part + j * HEAD : 2 * part + (j + 1) * HEAD].astype(F32)
+            mixed = (residual + normed).astype(BF16)
+            for e in range(held):
+                piece = mixed[e * CAP : (e + 1) * CAP, :]
+                for s in range(seqs):
+                    slots_ref[s, e, b * CAP : (b + 1) * CAP, cols] = piece
+            if b + 1 < seqs:
+                tail = state_ref[b, part : part + PAD, :].astype(F32)
+                decay = jnp.where(lane == h, tail[0:1, :] + tail[8:9, :], 0.0)
+                carry = jnp.sum(decay, axis=1, keepdims=True) * carry + state_ref[b, cols, :].astype(F32)
+    for r in range(seqs):
+        prefixes[r][...] = prefix_ref[lax.rem(me + r, seqs)]
+
+
+def expert_in_kernel(seqs, held, width, in_ref, ids_ref, gate_ref, up_ref, *refs):
+    tables, (out_ref, share_ref, x_ref) = refs[:held], refs[held:]
+    part = in_ref.shape[2]
+    slot_rows = in_ref.shape[1]
+    experts = tables[0].shape[0] - PAD
+    expert = lax.axis_index("exp")
+    squares = jnp.zeros((slot_rows, 1), F32)
+    for i in range(seqs * held):
+        piece = in_ref[i].astype(F32)
+        squares += jnp.sum(piece * piece, axis=1, keepdims=True)
+    inverse = lax.rsqrt(squares / (held * width) + EPS)
+    logits = jnp.zeros((slot_rows, experts), F32)
+    for r in range(held):
+        k = lax.rem(expert + held - r, held)
+        for s in range(seqs):
+            cols = slice(s * part, (s + 1) * part)
+            gain = tables[r][experts : experts + PAD, cols].astype(F32)
+            gain = gain[0:1, :] + gain[1:2, :]
+            scaled = in_ref[s * held + k].astype(F32) * gain * inverse
+            hi, lo = split_hi_lo(scaled)
+            x_ref[:, pl.ds(pl.multiple_of(k * width + s * part, part), part)] = hi
+            logits += nt(hi, tables[r][0:experts, cols]) + nt(lo, tables[r][0:experts, cols])
+    probs = 1.0 / (1.0 + jnp.exp(-logits))
+    lane = iota(probs.shape, 1)
+    total = jnp.zeros((slot_rows, 1), F32)
+    for i in range(2):
+        number = ids_ref[:, i : i + 1].astype(jnp.int32)
+        total += jnp.sum(jnp.where(lane == number, probs, 0.0), axis=1, keepdims=True)
+    own = jnp.sum(jnp.where(lane == expert, probs, 0.0), axis=1, keepdims=True)
+    share_ref[...] = jnp.broadcast_to(own / total, share_ref.shape)
+    x = x_ref[...]
+    gate = nn(x, gate_ref[0])
+    up = nn(x, up_ref[0])
+    out_ref[...] = (gate * (1.0 / (1.0 + jnp.exp(-gate))) * up).astype(BF16)
+
+
+def expert_out_kernel(seqs, held, w_ref, share_ref, *refs):
+    h_refs, out_refs, acc_ref = refs[:seqs], refs[seqs : seqs + held], refs[seqs + held]
+    part = h_refs[0].shape[-1]
+    me, expert = lax.axis_index("seq"), lax.axis_index("exp")
+    total = None
+    for r in range(seqs):
+        at = pl.multiple_of(lax.rem(me + seqs - r, seqs) * part, part)
+        term = nn(h_refs[r][...], w_ref[0, pl.ds(at, part), :])
+        total = term if total is None else total + term
+    acc_ref[...] = total * share_ref[:, 0:1]
+    for r in range(held):
+        at = pl.multiple_of(lax.rem(expert + r, seqs) * CAP, CAP)
+        out_refs[r][...] = acc_ref[pl.ds(at, CAP), :].astype(BF16)
+
+
+def mixed_kernel(heads, seqs, grown_ref, local_ref, res_ref, again_ref, *refs):
+    prefixes, mixed_ref = refs[:seqs], refs[seqs]
+    me = lax.axis_index("seq")
+    per = heads // seqs
+    for r in range(seqs):
+        share = lax.rem(me + seqs - r, seqs)
+        for j in range(per):
+            h = share * per + j
+            cols = pl.ds(pl.multiple_of(h * HEAD, HEAD), HEAD)
+            inter = nn(grown_ref[:, cols], prefixes[r][j * HEAD : (j + 1) * HEAD, :])
+            attended = local_ref[:, cols] + inter
+            power = jnp.mean(attended * attended, axis=1, keepdims=True)
+            normed = attended * lax.rsqrt(power + EPS) * again_ref[pl.ds(h, 1), :]
+            mixed_ref[:, cols] = (res_ref[:, cols].astype(F32) + normed).astype(BF16)
+
+
+def add_kernel(held, mixed_ref, place_ref, *refs):
+    y_refs, out_ref, y_ref = refs[:held], refs[held], refs[held + 1]
+    me = lax.axis_index("seq")
+    for r, ref in enumerate(y_refs):
+        at = pl.multiple_of(lax.rem(me + held - r, held) * CAP, CAP)
+        y_ref[pl.ds(at, CAP), :] = ref[...].astype(F32)
+    extra = tn(place_ref[...].astype(BF16), y_ref[...].astype(BF16))
+    out_ref[...] = (mixed_ref[...].astype(F32) + extra).astype(BF16)
+
+
+def run(body, out_shape, args, scratch=(), flops=1000, nbytes=1000, vmem=SMALL, anywhere=0):
+    outs = out_shape if isinstance(out_shape, tuple) else (out_shape,)
+    specs = tuple(VMEM for _ in outs)
+    return pl.pallas_call(
+        body,
+        out_shape=out_shape,
+        in_specs=[VMEM] * (len(args) - anywhere) + [pl.BlockSpec(memory_space=pltpu.HBM)] * anywhere,
+        out_specs=specs if isinstance(out_shape, tuple) else specs[0],
+        scratch_shapes=list(scratch),
+        compiler_params=pltpu.CompilerParams(vmem_limit_bytes=vmem),
+        cost_estimate=pl.CostEstimate(flops=flops, bytes_accessed=nbytes, transcendentals=0),
+    )(*args)
+
+
+def keep(weights, after):
+    return run(
+        functools.partial(keep_kernel, len(weights)),
+        tuple(pltpu.VMEM(w.shape, w.dtype) for w in weights),
+        (after, *(pltpu.with_memory_space_constraint(w, pltpu.HBM) for w in weights)),
+        scratch=[pltpu.SemaphoreType.DMA((len(weights),))],
+        nbytes=sum(w.size * 2 for w in weights),
+        anywhere=len(weights),
+    )
+
+
+def rotate(x, axis, count, step):
+    return lax.ppermute(x, axis, [(i, (i + step) % count) for i in range(count)])
+
+
+def spread(pieces, axis, count):
+    return [pieces[0]] + [rotate(pieces[r], axis, count, r) for r in range(1, count)]
+
+
+def ring_body(
+    residual, query_rows, key_rows, value_rows, log_decay, attn_gain, norm_gain, router, expert_ids, priority,
+    gate_weight, up_weight, down_weight,
+):
+    rows, width = residual.shape
+    heads = width // HEAD
+    held = lax.axis_size("exp")
+    seqs = lax.axis_size("seq")
+    experts = router.shape[1]
+    part = width // seqs
+    slot_rows = seqs * CAP
+    hidden_part = gate_weight.shape[2]
+    out_part = down_weight.shape[2]
+    again = attn_gain.reshape(heads, HEAD)
+    *pieces, cum_row, cum_col = run(
+        functools.partial(state_pieces_kernel, heads, seqs),
+        (
+            *(shaped((part + PAD, LANES), BF16) for _ in range(seqs)),
+            shaped((LANES, rows), F32),
+            shaped((rows, LANES), F32),
+        ),
+        (key_rows, value_rows, log_decay.T),
+        scratch=[pltpu.VMEM((LANES, rows), F32), pltpu.VMEM((LANES, rows), F32)],
+    )
+    states = spread(pieces, "seq", seqs)
+    table = run(
+        functools.partial(pack_kernel, heads),
+        shaped((experts + PAD, width), BF16),
+        (router.T, norm_gain.reshape(heads, HEAD)),
+    )
+    tables = spread([table] * held, "exp", held)
+    local, grown, place, *row_pieces = run(
+        functools.partial(rows_kernel, heads, seqs, held),
+        (
+            shaped((rows, width), F32),
+            shaped((rows, width), BF16),
+            shaped((held * CAP, rows), F32),
+            *(shaped((held * CAP, 3 * part + LANES), BF16) for _ in range(seqs)),
+        ),
+        (query_rows, key_rows, value_rows, residual, cum_row, cum_col, expert_ids.T, priority),
+        flops=200_000_000,
+        nbytes=2_000_000,
+    )
+    row_parts = spread(row_pieces, "seq", seqs)
+    weights = keep((gate_weight, up_weight), row_pieces[0])
+    slots, slot_ids, *prefixes = run(
+        functools.partial(owner_kernel, heads, seqs, held),
+        (
+            pltpu.VMEM((seqs, held, slot_rows, part), BF16),
+            shaped((slot_rows, LANES), F32),
+            *(shaped((part, LANES), BF16) for _ in range(seqs)),
+        ),
+        (again, *states, *row_parts),
+        scratch=[
+            pltpu.VMEM((seqs, part + PAD, LANES), BF16),
+            pltpu.VMEM((seqs, held * CAP, 3 * part + LANES), BF16),
+            pltpu.VMEM((seqs, part, LANES), BF16),
+        ],
+    )
+    slots = slots.reshape(seqs * held, slot_rows, part)
+    gathered = lax.all_to_all(slots, ("seq", "exp"), split_axis=0, concat_axis=0, tiled=True)
+    hidden, shares = run(
+        functools.partial(expert_in_kernel, seqs, held, width),
+        (shaped((slot_rows, hidden_part), BF16), shaped((slot_rows, LANES), F32)),
+        (gathered, slot_ids, weights[0], weights[1], *tables),
+        scratch=[pltpu.VMEM((slot_rows, held * width), BF16)],
+        flops=900_000_000,
+        nbytes=28_000_000,
+    )
+    hiddens = spread([hidden] * seqs, "seq", seqs)
+    prefixes, hidden = lax.optimization_barrier((prefixes, hidden))
+    returned = spread(prefixes, "seq", seqs)
+    (down_weight,) = keep((down_weight,), hidden)
+    outs = run(
+        functools.partial(expert_out_kernel, seqs, held),
+        (shaped((CAP, out_part), BF16),) * held,
+        (down_weight, shares, *hiddens),
+        scratch=[pltpu.VMEM((slot_rows, out_part), F32)],
+        flops=450_000_000,
+        nbytes=14_000_000,
+    )
+    y = [
+        lax.ppermute(
+            piece,
+            ("seq", "exp"),
+            [(s * held + e, ((e + r) % seqs) * held + s) for s in range(seqs) for e in range(held)],
+        )
+        for r, piece in enumerate(outs)
+    ]
+    mixed = run(
+        functools.partial(mixed_kernel, heads, seqs),
         shaped((rows, width), BF16),
-        (mixed, hi, lo, *y),
-        "combine",
-    )
+        (grown, local, residual, again, *returned),
+        flops=100_000_000,
+        nbytes=2_000_000,
+    )
+    return run(
+        functools.partial(add_kernel, held),
+        shaped((rows, width), BF16),
+        (mixed, place, *y),
+        scratch=[pltpu.VMEM((held * CAP, width), F32)],
+    )
+
+
+def body(residual, *args):
+    seqs, held = lax.axis_size("seq"), lax.axis_size("exp")
+    if seqs == held and (residual.shape[1] // HEAD) % seqs == 0:
+        return ring_body(residual, *args)
+    return general_body(residual, *args)
 
 
 def solution(mesh):

time: 110 us -> 105 us (0.955)
  local copies, waits for them, and re-layouts: 6.03 us -> 28.4 us
  blocking collectives: 17 us -> 0 us
  Pallas kernels: 41.5 us -> 27.4 us
  starting transfers between devices: 22 us -> 33.5 us
  waiting for transfers between devices: 19.3 us -> 14.6 us
  other arithmetic: 2.96 us -> 0 us
    unnamed x12 -> x32, local copies, waits for them, and re-layouts: 2.1 us -> 28.4 us
    all_to_all x1 -> x0, blocking collectives: 17 us -> none  [body(): lax.all_to_all(payload, 'seq', split_axis=0, concat_axis=0, tiled=True)]
    pallas_call x9 -> x10, Pallas kernels: 41.5 us -> 27.4 us  [run(): pl.pallas_call(body, out_shape=out_shape, in_specs=[VMEM] * (len(args) -...]
    all_to_all x2 -> x1, waiting for transfers between devices: 13.8 us -> 0.01 us  [ring_body(): lax.all_to_all(slots, ('seq', 'exp'), split_axis=0, concat_axis=0, tiled=...]
    ppermute x10 -> x19, starting transfers between devices: 14.3 us -> 27.5 us  [the longest x15 21.1 us: rotate(): lax.ppermute(x, axis, [(i, (i + step) % count) for i in range(count)])]
    ppermute x10 -> x19, waiting for transfers between devices: 5.44 us -> 14.6 us  [the longest x15 10.1 us: rotate(): lax.ppermute(x, axis, [(i, (i + step) % count) for i in range(count)])]
    broadcast_in_dim x2 -> x0, local copies, waits for them, and re-layouts: 2.58 us -> none  [the longest x1 1.29 us: body(): norm_gain[None]]
    another operation x2 -> x0, other arithmetic: 1.66 us -> none  [the longest x1 1.64 us: body(): whole = jnp.stack(parts)]
  transfers between devices with their start and end apart: 12 -> 20, of which waited for: 4 -> 6; matrix products, arithmetic and copies ran while one was open for 5% -> 0% of each run, Pallas kernels for 14% -> 16%
where the time goes in v2:
time: 105 us; the launch traced here: 104 us
  starting transfers between devices  33.5 us (32%)
  local copies, waits for them, and re-layouts  28.4 us (27%)
  Pallas kernels  27.4 us (26%)
  waiting for transfers between devices  14.6 us (14%)
    unnamed x32, local copies, waits for them, and re-layouts  28.4 us
    pallas_call x10, Pallas kernels, run(): pl.pallas_call(body, out_shape=out_shape, in_specs=[VMEM] * (len(args) -...  27.4 us
    ppermute x15, starting transfers between devices, rotate(): lax.ppermute(x, axis, [(i, (i + step) % count) for i in range(count)])  21.1 us
    ppermute x15, waiting for transfers between devices, rotate(): lax.ppermute(x, axis, [(i, (i + step) % count) for i in range(count)])  10.1 us
    ppermute x4, starting transfers between devices, ring_body(): lax.ppermute(piece, ('seq', 'exp'), [(s * held + e, (e + r) % seqs * held...  6.38 us
    all_to_all x1, starting transfers between devices, ring_body(): lax.all_to_all(slots, ('seq', 'exp'), split_axis=0, concat_axis=0, tiled=...  6.08 us
    ppermute x4, waiting for transfers between devices, ring_body(): lax.ppermute(piece, ('seq', 'exp'), [(s * held + e, (e + r) % seqs * held...  4.5 us
  transfers between devices with their start and end apart: 20, of which 6 were waited for; matrix products, arithmetic and copies ran while one was open for 0% of the time, Pallas kernels for 16%

profile of v2, /device:TPU:2, one launch (start us, length us, event | category | flops | bytes accessed | tf_op | source)
XLA Modules:
  0.0 104.2 jit_solution(4174473350348956806)
XLA Ops:
  0.0 1.0 copy-done.6
  1.0 1.0 copy-done.7
  3.4 1.0 copy-done.4
  4.4 1.0 copy-done.8
  6.8 2.3 %shard_map.128 = (f32[128,1536]{1,0:T(8,128)S(1)}, bf16[128,1536]{1,0:T(8,128)(2,1)S(1)}, f32[32,128]{1,0:T(8,128)S(1)}, bf16[32,1280]{1,0:T(8,128)(2,1)S(1)}, b...) custom-call(bf16[128,1536]{1,0:T(8,128)(2,1)S(1)} %copy-done.8, ...), custom_call_target="tpu_custom_call" | custom-call | flops 200000000 | bytes 2000000 | tf_op jit(solution)/shard_map/pallas_call | solution.py:592
  9.1 1.6 %collective-permute-start.3 = (bf16[32,1280]{1,0:T(8,128)(2,1)S(1)}, bf16[32,1280]{1,0:T(8,128)(2,1)S(1)}, u32[]{:S(2)}, u32[]{:S(2)}) collective-permute-start(bf16[32,1280]{1,0:T(8,128)(2,1)S(1)} %get-tuple-element.46), channel_id=1, source_target_pairs={{0,4},{4,8},{8,12},{12,0},{1,5},{5,9},{9,13},{13,1},{2,6},{6,10},{... | collective-permute-start | bytes 245768 | tf_op jit(solution)/shard_map/ppermute | solution.py:615
  10.7 1.6 %collective-permute-start = (bf16[400,128]{1,0:T(8,128)(2,1)S(1)}, bf16[400,128]{1,0:T(8,128)(2,1)S(1)}, u32[]{:S(2)}, u32[]{:S(2)}) collective-permute-start(bf16[400,128]{1,0:T(8,128)(2,1)S(1)} %get-tuple-element.42), channel_id=1, source_target_pairs={{0,4},{4,8},{8,12},{12,0},{1,5},{5,9},{9,13},{13,1},{2,6},{6,10},{... | collective-permute-start | bytes 307208 | tf_op jit(solution)/shard_map/ppermute | solution.py:615
  12.3 1.2 %collective-permute-start.1 = (bf16[400,128]{1,0:T(8,128)(2,1)S(1)}, bf16[400,128]{1,0:T(8,128)(2,1)S(1)}, u32[]{:S(2)}, u32[]{:S(2)}) collective-permute-start(bf16[400,128]{1,0:T(8,128)(2,1)S(1)} %get-tuple-element.43), channel_id=1, source_target_pairs={{0,8},{4,12},{8,0},{12,4},{1,9},{5,13},{9,1},{13,5},{2,10},{6,14},... | collective-permute-start | bytes 307208 | tf_op jit(solution)/shard_map/ppermute | solution.py:615
  13.5 2.7 %collective-permute-start.2 = (bf16[400,128]{1,0:T(8,128)(2,1)S(1)}, bf16[400,128]{1,0:T(8,128)(2,1)S(1)}, u32[]{:S(2)}, u32[]{:S(2)}) collective-permute-start(bf16[400,128]{1,0:T(8,128)(2,1)S(1)} %get-tuple-element.44), channel_id=1, source_target_pairs={{0,12},{4,0},{8,4},{12,8},{1,13},{5,1},{9,5},{13,9},{2,14},{6,2},{... | collective-permute-start | bytes 307208 | tf_op jit(solution)/shard_map/ppermute | solution.py:615
  16.6 1.4 %collective-permute-start.5 = (bf16[32,1280]{1,0:T(8,128)(2,1)S(1)}, bf16[32,1280]{1,0:T(8,128)(2,1)S(1)}, u32[]{:S(2)}, u32[]{:S(2)}) collective-permute-start(bf16[32,1280]{1,0:T(8,128)(2,1)S(1)} %get-tuple-element.48), channel_id=1, source_target_pairs={{0,12},{4,0},{8,4},{12,8},{1,13},{5,1},{9,5},{13,9},{2,14},{6,2},{... | collective-permute-start | bytes 245768 | tf_op jit(solution)/shard_map/ppermute | solution.py:615
  18.0 9.8 %collective-permute-done.4.refs_6_ = bf16[32,1280]{1,0:T(8,128)(2,1)S(1)} collective-permute-done((bf16[32,1280]{1,0:T(8,128)(2,1)S(1)}, bf16[32,1280]{1,0:T(8,128)(2,1)S(1)}, u32[]{:S(2)}, u32[]{:S(2)}) %collective-permute-start.4) | collective-permute-done | bytes 81952 | tf_op jit(solution)/shard_map/ppermute | solution.py:615
  28.5 1.2 %shard_map.129 = (bf16[4,4,32,384]{3,2,1,0:T(8,128)(2,1)}, f32[32,128]{1,0:T(8,128)S(1)}, bf16[384,128]{1,0:T(8,128)(2,1)S(1)}, bf16[384,128]{1,0:T(8,128)(2,1)S...) custom-call(f32[12,128]{1,0:T(8,128)S(1)} %bitcast.7, bf16[400,128]{1,0:T(8,128)(2,1)S(1)} %get-tuple-element.41.refs_0_, ...), custom_call_target="tpu_custom_call" | custom-call | flops 1000 | bytes 1000 | tf_op jit(solution)/shard_map/pallas_call | solution.py:592
  29.7 6.1 %all-to-all-start = ((bf16[16,32,384]{2,1,0:T(8,128)(2,1)}), bf16[16,32,384]{2,1,0:T(8,128)(2,1)S(1)}, u32[]{:S(2)}, u32[]{:S(2)}) async-start(bf16[16,32,384]{2,1,0:T(8,128)(2,1)} %bitcast.3), calls=%async_computation | async-start | bytes 786432 | tf_op jit(solution)/shard_map/all_to_all | solution.py:682
  35.8 0.9 copy-done.9
  37.6 1.6 %collective-permute-start.7 = (bf16[48,1536]{1,0:T(8,128)(2,1)S(1)}, bf16[48,1536]{1,0:T(8,128)(2,1)S(1)}, u32[]{:S(2)}, u32[]{:S(2)}) collective-permute-start(bf16[48,1536]{1,0:T(8,128)(2,1)S(1)} %shard_map.131.refs_0_), channel_id=1, source_target_pairs={{0,2},{1,3},{2,0},{3,1},{4,6},{5,7},{6,4},{7,5},{8,10},{9,11},{10,... | collective-permute-start | bytes 442376 | tf_op jit(solution)/shard_map/ppermute | solution.py:615
  39.2 9.1 %shard_map.130 = (bf16[1,6144,1152]{2,1,0:T(8,128)(2,1)S(1)}, bf16[1,6144,1152]{2,1,0:T(8,128)(2,1)S(1)}) custom-call(bf16[32,1280]{1,0:T(8,128)(2,1)S(1)} %get-tuple-element.45.refs_4_.refs_0_, bf16[1,6144,1152]{2,1,0:T(8,128)(2,1)} %refs_1_.2, bf16[1,6144,1152]{2,1,0:T(8,128)(2,1)} %refs_2_.1), custom_call_target="tpu_custom_call" | custom-call | flops 1000 | bytes 28311552 | tf_op jit(solution)/shard_map/pallas_call | solution.py:592
  48.3 5.0 %copy-done = bf16[1,6144,1152]{2,1,0:T(8,128)(2,1)} copy-done((bf16[1,6144,1152]{2,1,0:T(8,128)(2,1)}, bf16[1,6144,1152]{2,1,0:T(8,128)(2,1)S(1)}, u32[]{:S(2)}) %copy-start) | copy-done | bytes 14155800
  53.3 5.0 %copy-done.2 = bf16[1,6144,1152]{2,1,0:T(8,128)(2,1)} copy-done((bf16[1,6144,1152]{2,1,0:T(8,128)(2,1)}, bf16[1,6144,1152]{2,1,0:T(8,128)(2,1)S(1)}, u32[]{:S(2)}) %copy-start.2) | copy-done | bytes 14155800
  58.4 5.0 %copy-done.1 = bf16[1,6144,1152]{2,1,0:T(8,128)(2,1)S(1)} copy-done((bf16[1,6144,1152]{2,1,0:T(8,128)(2,1)S(1)}, bf16[1,6144,1152]{2,1,0:T(8,128)(2,1)}, u32[]{:S(2)}) %copy-start.1) | copy-done | bytes 14155800
  63.4 5.0 %copy-done.3 = bf16[1,6144,1152]{2,1,0:T(8,128)(2,1)S(1)} copy-done((bf16[1,6144,1152]{2,1,0:T(8,128)(2,1)S(1)}, bf16[1,6144,1152]{2,1,0:T(8,128)(2,1)}, u32[]{:S(2)}) %copy-start.3) | copy-done | bytes 14155800
  68.5 5.0 %shard_map.132 = (bf16[32,1152]{1,0:T(8,128)(2,1)S(1)}, f32[32,128]{1,0:T(8,128)S(1)}) custom-call(bf16[16,32,384]{2,1,0:T(8,128)(2,1)S(1)} %all-to-all-done.in_ref, f32[32,128]{1,0:T(8,128)S(1)} %get-tuple-element.54.ids_ref, bf16[1,6144,1152]{2,1,0:T(8,128)(2,1)S(1)} %copy-done.1, bf16[1,6144,1152]{2,1,0:T(8,128)(2,1)S(1)} %copy-done.3, ...), custom_call_target="tpu_custom_call" | custom-call | flops 900000000 | bytes 28000000 | tf_op jit(solution)/shard_map/pallas_call | solution.py:592
  73.4 3.3 %collective-permute-start.14 = (bf16[32,1152]{1,0:T(8,128)(2,1)S(1)}, bf16[32,1152]{1,0:T(8,128)(2,1)S(1)}, u32[]{:S(2)}, u32[]{:S(2)}) collective-permute-start(bf16[32,1152]{1,0:T(8,128)(2,1)S(1)} %get-tuple-element.63.refs_0_), channel_id=1, source_target_pairs={{0,12},{4,0},{8,4},{12,8},{1,13},{5,1},{9,5},{13,9},{2,14},{6,2},{... | collective-permute-start | bytes 221192 | tf_op jit(solution)/shard_map/ppermute | solution.py:615
  76.8 1.1 %collective-permute-start.12 = (bf16[32,1152]{1,0:T(8,128)(2,1)S(1)}, bf16[32,1152]{1,0:T(8,128)(2,1)S(1)}, u32[]{:S(2)}, u32[]{:S(2)}) collective-permute-start(bf16[32,1152]{1,0:T(8,128)(2,1)S(1)} %get-tuple-element.63.refs_0_), channel_id=1, source_target_pairs={{0,4},{4,8},{8,12},{12,0},{1,5},{5,9},{9,13},{13,1},{2,6},{6,10},{... | collective-permute-start | bytes 221192 | tf_op jit(solution)/shard_map/ppermute | solution.py:615
  77.9 2.4 %collective-permute-start.9 = (bf16[384,128]{1,0:T(8,128)(2,1)S(1)}, bf16[384,128]{1,0:T(8,128)(2,1)S(1)}, u32[]{:S(2)}, u32[]{:S(2)}) collective-permute-start(bf16[384,128]{1,0:T(8,128)(2,1)S(1)} %get-tuple-element.59), channel_id=1, source_target_pairs={{0,4},{4,8},{8,12},{12,0},{1,5},{5,9},{9,13},{13,1},{2,6},{6,10},{... | collective-permute-start | bytes 294920 | tf_op jit(solution)/shard_map/ppermute | solution.py:615
  80.3 0.9 collective-permute-start.10
  81.2 2.6 %collective-permute-start.11 = (bf16[384,128]{1,0:T(8,128)(2,1)S(1)}, bf16[384,128]{1,0:T(8,128)(2,1)S(1)}, u32[]{:S(2)}, u32[]{:S(2)}) collective-permute-start(bf16[384,128]{1,0:T(8,128)(2,1)S(1)} %get-tuple-element.61), channel_id=1, source_target_pairs={{0,12},{4,0},{8,4},{12,8},{1,13},{5,1},{9,5},{13,9},{2,14},{6,2},{... | collective-permute-start | bytes 294920 | tf_op jit(solution)/shard_map/ppermute | solution.py:615
  83.8 5.0 %shard_map.134.w_ref = bf16[1,4608,1536]{2,1,0:T(8,128)(2,1)S(1)} custom-call(bf16[32,1152]{1,0:T(8,128)(2,1)S(1)} %get-tuple-element.63.refs_0_, bf16[1,4608,1536]{2,1,0:T(8,128)(2,1)} %refs_1_.3), custom_call_target="tpu_custom_call" | custom-call | flops 1000 | bytes 14155776 | tf_op jit(solution)/shard_map/pallas_call | solution.py:592
  89.2 2.5 %shard_map.135 = (bf16[8,1536]{1,0:T(8,128)(2,1)S(1)}, bf16[8,1536]{1,0:T(8,128)(2,1)S(1)}, bf16[8,1536]{1,0:T(8,128)(2,1)S(1)}, bf16[8,1536]{1,0:T(8,128)(2,1)S(1)}) custom-call(bf16[1,4608,1536]{2,1,0:T(8,128)(2,1)S(1)} %shard_map.134.w_ref, f32[32,128]{1,0:T(8,128)S(1)} %get-tuple-element.64.share_ref, bf16[32,1152]{1,0:T(8,128)(2,1)S(1)} %get-tuple-element.63.refs_0_, ...), custom_call_target="tpu_custom_call" | custom-call | flops 450000000 | bytes 14000000 | tf_op jit(solution)/shard_map/pallas_call | solution.py:592
  91.7 1.9 %collective-permute-start.15 = (bf16[8,1536]{1,0:T(8,128)(2,1)S(1)}, bf16[8,1536]{1,0:T(8,128)(2,1)S(1)}, u32[]{:S(2)}, u32[]{:S(2)}) collective-permute-start(bf16[8,1536]{1,0:T(8,128)(2,1)S(1)} %get-tuple-element.65), channel_id=1, source_target_pairs={{0,0},{1,4},{2,8},{3,12},{4,1},{5,5},{6,9},{7,13},{8,2},{9,6},{10,... | collective-permute-start | bytes 73736 | tf_op jit(solution)/shard_map/ppermute | solution.py:704
  93.7 4.4 %collective-permute-start.16 = (bf16[8,1536]{1,0:T(8,128)(2,1)S(1)}, bf16[8,1536]{1,0:T(8,128)(2,1)S(1)}, u32[]{:S(2)}, u32[]{:S(2)}) collective-permute-start(bf16[8,1536]{1,0:T(8,128)(2,1)S(1)} %get-tuple-element.66), channel_id=1, source_target_pairs={{0,4},{1,8},{2,12},{3,0},{4,5},{5,9},{6,13},{7,1},{8,6},{9,10},{10... | collective-permute-start | bytes 73736 | tf_op jit(solution)/shard_map/ppermute | solution.py:704
  99.6 3.2 %collective-permute-done.17.refs_2_ = bf16[8,1536]{1,0:T(8,128)(2,1)S(1)} collective-permute-done((bf16[8,1536]{1,0:T(8,128)(2,1)S(1)}, bf16[8,1536]{1,0:T(8,128)(2,1)S(1)}, u32[]{:S(2)}, u32[]{:S(2)}) %collective-permute-start.17) | collective-permute-done | bytes 24608 | tf_op jit(solution)/shard_map/ppermute | solution.py:704
  103.2 1.0 shard_map.136
  (50 shorter events, 6.9 us)
Async XLA Ops:
  0.0 1.0 copy-start.6
  1.0 1.0 copy-start.7
  3.4 1.0 copy-start.4
  4.4 1.0 copy-start.8
  9.1 7.5 %collective-permute-start.3 = (bf16[32,1280]{1,0:T(8,128)(2,1)S(1)}, bf16[32,1280]{1,0:T(8,128)(2,1)S(1)}, u32[]{:S(2)}, u32[]{:S(2)}) collective-permute-start(bf16[32,1280]{1,0:T(8,128)(2,1)S(1)} %get-tuple-element.46), channel_id=1, source_target_pairs={{0,4},{4,8},{8,12},{12,0},{1,5},{5,9},{9,13},{13,1},{2,6},{6,10},{... | collective-permute-start | bytes 245768 | tf_op jit(solution)/shard_map/ppermute | solution.py:615
  10.7 17.1 %collective-permute-start = (bf16[400,128]{1,0:T(8,128)(2,1)S(1)}, bf16[400,128]{1,0:T(8,128)(2,1)S(1)}, u32[]{:S(2)}, u32[]{:S(2)}) collective-permute-start(bf16[400,128]{1,0:T(8,128)(2,1)S(1)} %get-tuple-element.42), channel_id=1, source_target_pairs={{0,4},{4,8},{8,12},{12,0},{1,5},{5,9},{9,13},{13,1},{2,6},{6,10},{... | collective-permute-start | bytes 307208 | tf_op jit(solution)/shard_map/ppermute | solution.py:615
  12.3 15.5 %collective-permute-start.1 = (bf16[400,128]{1,0:T(8,128)(2,1)S(1)}, bf16[400,128]{1,0:T(8,128)(2,1)S(1)}, u32[]{:S(2)}, u32[]{:S(2)}) collective-permute-start(bf16[400,128]{1,0:T(8,128)(2,1)S(1)} %get-tuple-element.43), channel_id=1, source_target_pairs={{0,8},{4,12},{8,0},{12,4},{1,9},{5,13},{9,1},{13,5},{2,10},{6,14},... | collective-permute-start | bytes 307208 | tf_op jit(solution)/shard_map/ppermute | solution.py:615
  13.5 14.3 %collective-permute-start.2 = (bf16[400,128]{1,0:T(8,128)(2,1)S(1)}, bf16[400,128]{1,0:T(8,128)(2,1)S(1)}, u32[]{:S(2)}, u32[]{:S(2)}) collective-permute-start(bf16[400,128]{1,0:T(8,128)(2,1)S(1)} %get-tuple-element.44), channel_id=1, source_target_pairs={{0,12},{4,0},{8,4},{12,8},{1,13},{5,1},{9,5},{13,9},{2,14},{6,2},{... | collective-permute-start | bytes 307208 | tf_op jit(solution)/shard_map/ppermute | solution.py:615
  16.2 11.6 %collective-permute-start.4 = (bf16[32,1280]{1,0:T(8,128)(2,1)S(1)}, bf16[32,1280]{1,0:T(8,128)(2,1)S(1)}, u32[]{:S(2)}, u32[]{:S(2)}) collective-permute-start(bf16[32,1280]{1,0:T(8,128)(2,1)S(1)} %get-tuple-element.47), channel_id=1, source_target_pairs={{0,8},{4,12},{8,0},{12,4},{1,9},{5,13},{9,1},{13,5},{2,10},{6,14},... | collective-permute-start | bytes 245768 | tf_op jit(solution)/shard_map/ppermute | solution.py:615
  16.6 11.2 %collective-permute-start.5 = (bf16[32,1280]{1,0:T(8,128)(2,1)S(1)}, bf16[32,1280]{1,0:T(8,128)(2,1)S(1)}, u32[]{:S(2)}, u32[]{:S(2)}) collective-permute-start(bf16[32,1280]{1,0:T(8,128)(2,1)S(1)} %get-tuple-element.48), channel_id=1, source_target_pairs={{0,12},{4,0},{8,4},{12,8},{1,13},{5,1},{9,5},{13,9},{2,14},{6,2},{... | collective-permute-start | bytes 245768 | tf_op jit(solution)/shard_map/ppermute | solution.py:615
  27.8 0.7 copy-start.10
  29.7 28.7 %all-to-all-start = ((bf16[16,32,384]{2,1,0:T(8,128)(2,1)}), bf16[16,32,384]{2,1,0:T(8,128)(2,1)S(1)}, u32[]{:S(2)}, u32[]{:S(2)}) async-start(bf16[16,32,384]{2,1,0:T(8,128)(2,1)} %bitcast.3), calls=%async_computation | async-start | bytes 786432 | tf_op jit(solution)/shard_map/all_to_all | solution.py:682
  35.8 0.9 copy-start.9
  37.4 21.0 %collective-permute-start.8 = (bf16[48,1536]{1,0:T(8,128)(2,1)S(1)}, bf16[48,1536]{1,0:T(8,128)(2,1)S(1)}, u32[]{:S(2)}, u32[]{:S(2)}) collective-permute-start(bf16[48,1536]{1,0:T(8,128)(2,1)S(1)} %shard_map.131.refs_0_), channel_id=1, source_target_pairs={{0,3},{1,0},{2,1},{3,2},{4,7},{5,4},{6,5},{7,6},{8,11},{9,8},{10,9... | collective-permute-start | bytes 442376 | tf_op jit(solution)/shard_map/ppermute | solution.py:615
  37.6 20.8 %collective-permute-start.7 = (bf16[48,1536]{1,0:T(8,128)(2,1)S(1)}, bf16[48,1536]{1,0:T(8,128)(2,1)S(1)}, u32[]{:S(2)}, u32[]{:S(2)}) collective-permute-start(bf16[48,1536]{1,0:T(8,128)(2,1)S(1)} %shard_map.131.refs_0_), channel_id=1, source_target_pairs={{0,2},{1,3},{2,0},{3,1},{4,6},{5,7},{6,4},{7,5},{8,10},{9,11},{10,... | collective-permute-start | bytes 442376 | tf_op jit(solution)/shard_map/ppermute | solution.py:615
  39.2 19.2 %collective-permute-start.6 = (bf16[48,1536]{1,0:T(8,128)(2,1)S(1)}, bf16[48,1536]{1,0:T(8,128)(2,1)S(1)}, u32[]{:S(2)}, u32[]{:S(2)}) collective-permute-start(bf16[48,1536]{1,0:T(8,128)(2,1)S(1)} %shard_map.131.refs_0_), channel_id=1, source_target_pairs={{0,1},{1,2},{2,3},{3,0},{4,5},{5,6},{6,7},{7,4},{8,9},{9,10},{10,1... | collective-permute-start | bytes 442376 | tf_op jit(solution)/shard_map/ppermute | solution.py:615
  48.3 5.0 %copy-start = (bf16[1,6144,1152]{2,1,0:T(8,128)(2,1)}, bf16[1,6144,1152]{2,1,0:T(8,128)(2,1)S(1)}, u32[]{:S(2)}) copy-start(bf16[1,6144,1152]{2,1,0:T(8,128)(2,1)S(1)} %get-tuple-element.55.gate_ref) | copy-start | bytes 42467332
  53.3 5.0 %copy-start.2 = (bf16[1,6144,1152]{2,1,0:T(8,128)(2,1)}, bf16[1,6144,1152]{2,1,0:T(8,128)(2,1)S(1)}, u32[]{:S(2)}) copy-start(bf16[1,6144,1152]{2,1,0:T(8,128)(2,1)S(1)} %get-tuple-element.56.up_ref) | copy-start | bytes 42467332
  58.4 5.0 %copy-start.1 = (bf16[1,6144,1152]{2,1,0:T(8,128)(2,1)S(1)}, bf16[1,6144,1152]{2,1,0:T(8,128)(2,1)}, u32[]{:S(2)}) copy-start(bf16[1,6144,1152]{2,1,0:T(8,128)(2,1)} %copy-done) | copy-start | bytes 42467332
  63.4 5.0 %copy-start.3 = (bf16[1,6144,1152]{2,1,0:T(8,128)(2,1)S(1)}, bf16[1,6144,1152]{2,1,0:T(8,128)(2,1)}, u32[]{:S(2)}) copy-start(bf16[1,6144,1152]{2,1,0:T(8,128)(2,1)} %copy-done.2) | copy-start | bytes 42467332
  73.4 7.7 %collective-permute-start.14 = (bf16[32,1152]{1,0:T(8,128)(2,1)S(1)}, bf16[32,1152]{1,0:T(8,128)(2,1)S(1)}, u32[]{:S(2)}, u32[]{:S(2)}) collective-permute-start(bf16[32,1152]{1,0:T(8,128)(2,1)S(1)} %get-tuple-element.63.refs_0_), channel_id=1, source_target_pairs={{0,12},{4,0},{8,4},{12,8},{1,13},{5,1},{9,5},{13,9},{2,14},{6,2},{... | collective-permute-start | bytes 221192 | tf_op jit(solution)/shard_map/ppermute | solution.py:615
  76.8 12.4 %collective-permute-start.13 = (bf16[32,1152]{1,0:T(8,128)(2,1)S(1)}, bf16[32,1152]{1,0:T(8,128)(2,1)S(1)}, u32[]{:S(2)}, u32[]{:S(2)}) collective-permute-start(bf16[32,1152]{1,0:T(8,128)(2,1)S(1)} %get-tuple-element.63.refs_0_), channel_id=1, source_target_pairs={{0,8},{4,12},{8,0},{12,4},{1,9},{5,13},{9,1},{13,5},{2,10},{6,14},... | collective-permute-start | bytes 221192 | tf_op jit(solution)/shard_map/ppermute | solution.py:615
  76.8 12.4 %collective-permute-start.12 = (bf16[32,1152]{1,0:T(8,128)(2,1)S(1)}, bf16[32,1152]{1,0:T(8,128)(2,1)S(1)}, u32[]{:S(2)}, u32[]{:S(2)}) collective-permute-start(bf16[32,1152]{1,0:T(8,128)(2,1)S(1)} %get-tuple-element.63.refs_0_), channel_id=1, source_target_pairs={{0,4},{4,8},{8,12},{12,0},{1,5},{5,9},{9,13},{13,1},{2,6},{6,10},{... | collective-permute-start | bytes 221192 | tf_op jit(solution)/shard_map/ppermute | solution.py:615
  77.9 20.2 %collective-permute-start.9 = (bf16[384,128]{1,0:T(8,128)(2,1)S(1)}, bf16[384,128]{1,0:T(8,128)(2,1)S(1)}, u32[]{:S(2)}, u32[]{:S(2)}) collective-permute-start(bf16[384,128]{1,0:T(8,128)(2,1)S(1)} %get-tuple-element.59), channel_id=1, source_target_pairs={{0,4},{4,8},{8,12},{12,0},{1,5},{5,9},{9,13},{13,1},{2,6},{6,10},{... | collective-permute-start | bytes 294920 | tf_op jit(solution)/shard_map/ppermute | solution.py:615
  80.3 17.8 %collective-permute-start.10 = (bf16[384,128]{1,0:T(8,128)(2,1)S(1)}, bf16[384,128]{1,0:T(8,128)(2,1)S(1)}, u32[]{:S(2)}, u32[]{:S(2)}) collective-permute-start(bf16[384,128]{1,0:T(8,128)(2,1)S(1)} %get-tuple-element.60), channel_id=1, source_target_pairs={{0,8},{4,12},{8,0},{12,4},{1,9},{5,13},{9,1},{13,5},{2,10},{6,14},... | collective-permute-start | bytes 294920 | tf_op jit(solution)/shard_map/ppermute | solution.py:615
  81.2 17.0 %collective-permute-start.11 = (bf16[384,128]{1,0:T(8,128)(2,1)S(1)}, bf16[384,128]{1,0:T(8,128)(2,1)S(1)}, u32[]{:S(2)}, u32[]{:S(2)}) collective-permute-start(bf16[384,128]{1,0:T(8,128)(2,1)S(1)} %get-tuple-element.61), channel_id=1, source_target_pairs={{0,12},{4,0},{8,4},{12,8},{1,13},{5,1},{9,5},{13,9},{2,14},{6,2},{... | collective-permute-start | bytes 294920 | tf_op jit(solution)/shard_map/ppermute | solution.py:615
  88.8 9.3 %copy-start.5 = (bf16[128,1536]{1,0:T(8,128)(2,1)S(1)}, bf16[128,1536]{1,0:T(8,128)(2,1)}, u32[]{:S(2)}) copy-start(bf16[128,1536]{1,0:T(8,128)(2,1)} %res_ref.3) | copy-start | bytes 1179652
  88.9 9.3 %copy-start.11 = (f32[1536]{0:T(1024)S(1)}, f32[1536]{0:T(1024)}, u32[]{:S(2)}) copy-start(f32[1536]{0:T(1024)} %param.18) | copy-start | bytes 18436
  91.7 7.5 %collective-permute-start.15 = (bf16[8,1536]{1,0:T(8,128)(2,1)S(1)}, bf16[8,1536]{1,0:T(8,128)(2,1)S(1)}, u32[]{:S(2)}, u32[]{:S(2)}) collective-permute-start(bf16[8,1536]{1,0:T(8,128)(2,1)S(1)} %get-tuple-element.65), channel_id=1, source_target_pairs={{0,0},{1,4},{2,8},{3,12},{4,1},{5,5},{6,9},{7,13},{8,2},{9,6},{10,... | collective-permute-start | bytes 73736 | tf_op jit(solution)/shard_map/ppermute | solution.py:704
  93.7 5.9 %collective-permute-start.16 = (bf16[8,1536]{1,0:T(8,128)(2,1)S(1)}, bf16[8,1536]{1,0:T(8,128)(2,1)S(1)}, u32[]{:S(2)}, u32[]{:S(2)}) collective-permute-start(bf16[8,1536]{1,0:T(8,128)(2,1)S(1)} %get-tuple-element.66), channel_id=1, source_target_pairs={{0,4},{1,8},{2,12},{3,0},{4,5},{5,9},{6,13},{7,1},{8,6},{9,10},{10... | collective-permute-start | bytes 73736 | tf_op jit(solution)/shard_map/ppermute | solution.py:704
  98.0 4.7 %collective-permute-start.17 = (bf16[8,1536]{1,0:T(8,128)(2,1)S(1)}, bf16[8,1536]{1,0:T(8,128)(2,1)S(1)}, u32[]{:S(2)}, u32[]{:S(2)}) collective-permute-start(bf16[8,1536]{1,0:T(8,128)(2,1)S(1)} %get-tuple-element.67), channel_id=1, source_target_pairs={{0,8},{1,12},{2,0},{3,4},{4,9},{5,13},{6,1},{7,5},{8,10},{9,14},{1... | collective-permute-start | bytes 73736 | tf_op jit(solution)/shard_map/ppermute | solution.py:704
  98.1 5.1 %collective-permute-start.18 = (bf16[8,1536]{1,0:T(8,128)(2,1)S(1)}, bf16[8,1536]{1,0:T(8,128)(2,1)S(1)}, u32[]{:S(2)}, u32[]{:S(2)}) collective-permute-start(bf16[8,1536]{1,0:T(8,128)(2,1)S(1)} %get-tuple-element.68), channel_id=1, source_target_pairs={{0,12},{1,0},{2,4},{3,8},{4,13},{5,1},{6,5},{7,9},{8,14},{9,2},{10... | collective-permute-start | bytes 73736 | tf_op jit(solution)/shard_map/ppermute | solution.py:704
  (4 other events, 2.7 us)

commit v3 on v2

--- a/solution.py
+++ b/solution.py
@@ -381,8 +381,14 @@
     return call(functools.partial(combine_kernel, held), shaped((rows, width), BF16), (mixed, hi, lo, *y))
 
 
-def state_pieces_kernel(heads, seqs, k_ref, v_ref, decay_ref, *refs):
-    pieces, row_ref, col_ref, pad_ref, end_ref = refs[:seqs], *refs[seqs:]
+def state_pieces_kernel(heads, seqs, count, *refs):
+    sources, kept, refs = refs[:count], refs[count : 2 * count], refs[2 * count :]
+    pieces, row_ref, col_ref, pad_ref, end_ref, sems = refs[:seqs], *refs[seqs:]
+    copies = [pltpu.make_async_copy(a, b, sems.at[i]) for i, (a, b) in enumerate(zip(sources, kept))]
+    for copy in copies:
+        copy.start()
+    k_ref, v_ref, decay_ref = kept[:3]
+    copies[2].wait()
     rows = k_ref.shape[0]
     per = heads // seqs
     me = lax.axis_index("seq")
@@ -401,6 +407,8 @@
     end_ref[...] = jnp.exp(cum_row[:, rows - 1 : rows] - cum_row)
     hi, lo = split_hi_lo(jnp.exp(cum_col[rows - 1 : rows, :]))
     tail = jnp.concatenate([jnp.broadcast_to(hi, (8, LANES)), jnp.broadcast_to(lo, (8, LANES))], axis=0)
+    copies[0].wait()
+    copies[1].wait()
     for r in range(seqs):
         share = lax.rem(me + r, seqs)
         for j in range(per):
@@ -409,6 +417,8 @@
             keyed = (k_ref[:, cols].astype(F32).T * end_ref[pl.ds(h, 1), :]).astype(BF16)
             pieces[r][j * HEAD : (j + 1) * HEAD, :] = nn(keyed, v_ref[:, cols]).astype(BF16)
         pieces[r][per * HEAD : per * HEAD + PAD, :] = tail
+    for copy in copies[3:]:
+        copy.wait()
 
 
 def pack_kernel(heads, router_ref, gain_ref, out_ref):
@@ -423,9 +433,12 @@
 
 
 def rows_kernel(
-    heads, seqs, held, q_ref, k_ref, v_ref, res_ref, row_ref, col_ref, ids_ref, prio_ref, local_ref, grown_ref,
-    place_ref, *pieces,
+    heads, seqs, held, q_ref, k_ref, v_ref, res_ref, row_ref, col_ref, ids_ref, prio_ref, gate_ref, local_ref,
+    grown_ref, place_ref, kept_ref, *pieces_and_sem,
 ):
+    pieces, sem = pieces_and_sem[:-1], pieces_and_sem[-1]
+    copy = pltpu.make_async_copy(gate_ref.at[:, pl.ds(0, kept_ref.shape[1]), :], kept_ref, sem)
+    copy.start()
     place_kernel(held, ids_ref, prio_ref, place_ref)
     rows = q_ref.shape[0]
     causal = iota((rows, rows), 0) >= iota((rows, rows), 1)
@@ -453,11 +466,14 @@
         pieces[r][:, part : 2 * part] = nn(place, local_ref[:, cols].astype(BF16)).astype(BF16)
         pieces[r][:, 2 * part : 3 * part] = nn(place, res_ref[:, cols]).astype(BF16)
         pieces[r][:, 3 * part : 3 * part + LANES] = extra.astype(BF16)
-
-
-def keep_kernel(count, *refs):
-    sources, kept, sems = refs[1 : count + 1], refs[count + 1 : 2 * count + 1], refs[2 * count + 1]
-    copies = [pltpu.make_async_copy(w, b, sems.at[i]) for i, (w, b) in enumerate(zip(sources, kept))]
+    copy.wait()
+
+
+def keep_kernel(early, after_ref, gate_ref, up_ref, late_ref, kept_ref, sems):
+    copies = (
+        pltpu.make_async_copy(gate_ref.at[:, pl.ds(early, late_ref.shape[1]), :], late_ref, sems.at[0]),
+        pltpu.make_async_copy(up_ref, kept_ref, sems.at[1]),
+    )
     for copy in copies:
         copy.start()
     for copy in copies:
@@ -509,8 +525,10 @@
         prefixes[r][...] = prefix_ref[lax.rem(me + r, seqs)]
 
 
-def expert_in_kernel(seqs, held, width, in_ref, ids_ref, gate_ref, up_ref, *refs):
-    tables, (out_ref, share_ref, x_ref) = refs[:held], refs[held:]
+def expert_in_kernel(seqs, held, width, in_ref, ids_ref, gate_early_ref, gate_late_ref, up_ref, *refs):
+    tables, (down_ref, out_ref, share_ref, kept_ref, x_ref, sem) = refs[:held], refs[held:]
+    copy = pltpu.make_async_copy(down_ref, kept_ref, sem)
+    copy.start()
     part = in_ref.shape[2]
     slot_rows = in_ref.shape[1]
     experts = tables[0].shape[0] - PAD
@@ -540,9 +558,11 @@
     own = jnp.sum(jnp.where(lane == expert, probs, 0.0), axis=1, keepdims=True)
     share_ref[...] = jnp.broadcast_to(own / total, share_ref.shape)
     x = x_ref[...]
-    gate = nn(x, gate_ref[0])
+    early = gate_early_ref.shape[1]
+    gate = nn(x[:, 0:early], gate_early_ref[0]) + nn(x[:, early:], gate_late_ref[0])
     up = nn(x, up_ref[0])
     out_ref[...] = (gate * (1.0 / (1.0 + jnp.exp(-gate))) * up).astype(BF16)
+    copy.wait()
 
 
 def expert_out_kernel(seqs, held, w_ref, share_ref, *refs):
@@ -589,7 +609,7 @@
 def run(body, out_shape, args, scratch=(), flops=1000, nbytes=1000, vmem=SMALL, anywhere=0):
     outs = out_shape if isinstance(out_shape, tuple) else (out_shape,)
     specs = tuple(VMEM for _ in outs)
-    return pl.pallas_call(
+    kernel = pl.pallas_call(
         body,
         out_shape=out_shape,
         in_specs=[VMEM] * (len(args) - anywhere) + [pl.BlockSpec(memory_space=pltpu.HBM)] * anywhere,
@@ -597,18 +617,9 @@
         scratch_shapes=list(scratch),
         compiler_params=pltpu.CompilerParams(vmem_limit_bytes=vmem),
         cost_estimate=pl.CostEstimate(flops=flops, bytes_accessed=nbytes, transcendentals=0),
-    )(*args)
-
-
-def keep(weights, after):
-    return run(
-        functools.partial(keep_kernel, len(weights)),
-        tuple(pltpu.VMEM(w.shape, w.dtype) for w in weights),
-        (after, *(pltpu.with_memory_space_constraint(w, pltpu.HBM) for w in weights)),
-        scratch=[pltpu.SemaphoreType.DMA((len(weights),))],
-        nbytes=sum(w.size * 2 for w in weights),
-        anywhere=len(weights),
-    )
+    )
+    near = len(args) - anywhere
+    return kernel(*args[:near], *(pltpu.with_memory_space_constraint(x, pltpu.HBM) for x in args[near:]))
 
 
 def rotate(x, axis, count, step):
@@ -632,38 +643,59 @@
     slot_rows = seqs * CAP
     hidden_part = gate_weight.shape[2]
     out_part = down_weight.shape[2]
-    again = attn_gain.reshape(heads, HEAD)
-    *pieces, cum_row, cum_col = run(
-        functools.partial(state_pieces_kernel, heads, seqs),
+    small = (
+        key_rows, value_rows, log_decay.T, query_rows, residual, expert_ids.T, priority, router.T,
+        norm_gain.reshape(heads, HEAD), attn_gain.reshape(heads, HEAD),
+    )
+    *outs, cum_row, cum_col = run(
+        functools.partial(state_pieces_kernel, heads, seqs, len(small)),
         (
+            *(pltpu.VMEM(x.shape, x.dtype) for x in small),
             *(shaped((part + PAD, LANES), BF16) for _ in range(seqs)),
             shaped((LANES, rows), F32),
             shaped((rows, LANES), F32),
         ),
-        (key_rows, value_rows, log_decay.T),
-        scratch=[pltpu.VMEM((LANES, rows), F32), pltpu.VMEM((LANES, rows), F32)],
-    )
+        small,
+        scratch=[
+            pltpu.VMEM((LANES, rows), F32),
+            pltpu.VMEM((LANES, rows), F32),
+            pltpu.SemaphoreType.DMA((len(small),)),
+        ],
+        anywhere=len(small),
+    )
+    keys, values, _, queries, stream, ids, order, router_rows, gain, again = outs[: len(small)]
+    pieces = outs[len(small) :]
     states = spread(pieces, "seq", seqs)
-    table = run(
-        functools.partial(pack_kernel, heads),
-        shaped((experts + PAD, width), BF16),
-        (router.T, norm_gain.reshape(heads, HEAD)),
-    )
+    table = run(functools.partial(pack_kernel, heads), shaped((experts + PAD, width), BF16), (router_rows, gain))
     tables = spread([table] * held, "exp", held)
-    local, grown, place, *row_pieces = run(
+    early = held * width // 2
+    local, grown, place, gate_early, *row_pieces = run(
         functools.partial(rows_kernel, heads, seqs, held),
         (
             shaped((rows, width), F32),
             shaped((rows, width), BF16),
             shaped((held * CAP, rows), F32),
+            pltpu.VMEM((1, early, hidden_part), BF16),
             *(shaped((held * CAP, 3 * part + LANES), BF16) for _ in range(seqs)),
         ),
-        (query_rows, key_rows, value_rows, residual, cum_row, cum_col, expert_ids.T, priority),
+        (queries, keys, values, stream, cum_row, cum_col, ids, order, gate_weight),
+        scratch=[pltpu.SemaphoreType.DMA],
         flops=200_000_000,
-        nbytes=2_000_000,
+        nbytes=9_000_000,
+        anywhere=1,
     )
     row_parts = spread(row_pieces, "seq", seqs)
-    weights = keep((gate_weight, up_weight), row_pieces[0])
+    gate_late, up_kept = run(
+        functools.partial(keep_kernel, early),
+        (
+            pltpu.VMEM((1, held * width - early, hidden_part), BF16),
+            pltpu.VMEM(up_weight.shape, BF16),
+        ),
+        (row_pieces[0], gate_weight, up_weight),
+        scratch=[pltpu.SemaphoreType.DMA((2,))],
+        nbytes=21_000_000,
+        anywhere=2,
+    )
     slots, slot_ids, *prefixes = run(
         functools.partial(owner_kernel, heads, seqs, held),
         (
@@ -680,22 +712,26 @@
     )
     slots = slots.reshape(seqs * held, slot_rows, part)
     gathered = lax.all_to_all(slots, ("seq", "exp"), split_axis=0, concat_axis=0, tiled=True)
-    hidden, shares = run(
+    hidden, shares, down_kept = run(
         functools.partial(expert_in_kernel, seqs, held, width),
-        (shaped((slot_rows, hidden_part), BF16), shaped((slot_rows, LANES), F32)),
-        (gathered, slot_ids, weights[0], weights[1], *tables),
-        scratch=[pltpu.VMEM((slot_rows, held * width), BF16)],
+        (
+            shaped((slot_rows, hidden_part), BF16),
+            shaped((slot_rows, LANES), F32),
+            pltpu.VMEM(down_weight.shape, BF16),
+        ),
+        (gathered, slot_ids, gate_early, gate_late, up_kept, *tables, down_weight),
+        scratch=[pltpu.VMEM((slot_rows, held * width), BF16), pltpu.SemaphoreType.DMA],
         flops=900_000_000,
         nbytes=28_000_000,
+        anywhere=1,
     )
     hiddens = spread([hidden] * seqs, "seq", seqs)
     prefixes, hidden = lax.optimization_barrier((prefixes, hidden))
     returned = spread(prefixes, "seq", seqs)
-    (down_weight,) = keep((down_weight,), hidden)
     outs = run(
         functools.partial(expert_out_kernel, seqs, held),
         (shaped((CAP, out_part), BF16),) * held,
-        (down_weight, shares, *hiddens),
+        (down_kept, shares, *hiddens),
         scratch=[pltpu.VMEM((slot_rows, out_part), F32)],
         flops=450_000_000,
         nbytes=14_000_000,
@@ -711,7 +747,7 @@
     mixed = run(
         functools.partial(mixed_kernel, heads, seqs),
         shaped((rows, width), BF16),
-        (grown, local, residual, again, *returned),
+        (grown, local, stream, again, *returned),
         flops=100_000_000,
         nbytes=2_000_000,
     )

time: 105 us -> 101 us (0.962)
  local copies, waits for them, and re-layouts: 28.4 us -> 21.8 us
  waiting for transfers between devices: 14.6 us -> 19.7 us
  Pallas kernels: 27.4 us -> 25.2 us
    unnamed x32 -> x12, local copies, waits for them, and re-layouts: 28.4 us -> 21.8 us
    ppermute x15, waiting for transfers between devices: 10.1 us -> 15.2 us  [rotate(): lax.ppermute(x, axis, [(i, (i + step) % count) for i in range(count)])]
    pallas_call x10 -> x9, Pallas kernels: 27.4 us -> 25.2 us  [run(): kernel(*args[:near], *(pltpu.with_memory_space_constraint(x, pltpu.HBM) f...]
  transfers between devices with their start and end apart: 20 -> 20, of which waited for: 6 -> 6; matrix products, arithmetic and copies ran while one was open for 0% -> 0% of each run, Pallas kernels for 16% -> 10%
where the time goes in v3:
time: 101 us; the launch traced here: 100 us
  starting transfers between devices  33.5 us (33%)
  Pallas kernels  25.2 us (25%)
  local copies, waits for them, and re-layouts  21.8 us (22%)
  waiting for transfers between devices  19.7 us (20%)
    pallas_call x9, Pallas kernels, run(): kernel(*args[:near], *(pltpu.with_memory_space_constraint(x, pltpu.HBM) f...  25.2 us
    unnamed x12, local copies, waits for them, and re-layouts  21.8 us
    ppermute x15, starting transfers between devices, rotate(): lax.ppermute(x, axis, [(i, (i + step) % count) for i in range(count)])  21 us
    ppermute x15, waiting for transfers between devices, rotate(): lax.ppermute(x, axis, [(i, (i + step) % count) for i in range(count)])  15.2 us
    ppermute x4, starting transfers between devices, ring_body(): lax.ppermute(piece, ('seq', 'exp'), [(s * held + e, (e + r) % seqs * held...  6.38 us
    all_to_all x1, starting transfers between devices, ring_body(): lax.all_to_all(slots, ('seq', 'exp'), split_axis=0, concat_axis=0, tiled=...  6.08 us
    ppermute x4, waiting for transfers between devices, ring_body(): lax.ppermute(piece, ('seq', 'exp'), [(s * held + e, (e + r) % seqs * held...  4.52 us
  transfers between devices with their start and end apart: 20, of which 6 were waited for; matrix products, arithmetic and copies ran while one was open for 0% of the time, Pallas kernels for 10%

profile of v3, /device:TPU:2, one launch (start us, length us, event | category | flops | bytes accessed | tf_op | source)
XLA Modules:
  0.0 100.4 jit_solution(12218498201083955258)
XLA Ops:
  0.0 2.4 %shard_map.127 = (bf16[128,1536]{1,0:T(8,128)(2,1)S(1)}, bf16[128,1536]{1,0:T(8,128)(2,1)S(1)}, f32[12,128]{1,0:T(8,128)}, bf16[128,1536]{1,0:T(8,128)(2,1)S(1)}...) custom-call(bf16[128,1536]{1,0:T(8,128)(2,1)} %refs_0_.1, ...), custom_call_target="tpu_custom_call" | custom-call | flops 1000 | bytes 1000 | tf_op jit(solution)/shard_map/pallas_call | solution.py:622
  2.4 5.1 %shard_map.128 = (f32[128,1536]{1,0:T(8,128)S(1)}, bf16[128,1536]{1,0:T(8,128)(2,1)S(1)}, f32[32,128]{1,0:T(8,128)S(1)}, bf16[1,3072,1152]{2,1,0:T(8,128)(2,1)S(...) custom-call(bf16[128,1536]{1,0:T(8,128)(2,1)S(1)} %get-tuple-element, ...), custom_call_target="tpu_custom_call" | custom-call | flops 200000000 | bytes 9000000 | tf_op jit(solution)/shard_map/pallas_call | solution.py:622
  7.6 2.8 %copy-done.2 = bf16[1,3072,1152]{2,1,0:T(8,128)(2,1)} copy-done((bf16[1,3072,1152]{2,1,0:T(8,128)(2,1)}, bf16[1,3072,1152]{2,1,0:T(8,128)(2,1)S(1)}, u32[]{:S(2)}) %copy-start.2) | copy-done | bytes 7077912
  10.4 1.6 %collective-permute-start.3 = (bf16[32,1280]{1,0:T(8,128)(2,1)S(1)}, bf16[32,1280]{1,0:T(8,128)(2,1)S(1)}, u32[]{:S(2)}, u32[]{:S(2)}) collective-permute-start(bf16[32,1280]{1,0:T(8,128)(2,1)S(1)} %get-tuple-element.63), channel_id=1, source_target_pairs={{0,4},{4,8},{8,12},{12,0},{1,5},{5,9},{9,13},{13,1},{2,6},{6,10},{... | collective-permute-start | bytes 245768 | tf_op jit(solution)/shard_map/ppermute | solution.py:626
  12.0 1.6 %collective-permute-start = (bf16[400,128]{1,0:T(8,128)(2,1)S(1)}, bf16[400,128]{1,0:T(8,128)(2,1)S(1)}, u32[]{:S(2)}, u32[]{:S(2)}) collective-permute-start(bf16[400,128]{1,0:T(8,128)(2,1)S(1)} %get-tuple-element.59), channel_id=1, source_target_pairs={{0,4},{4,8},{8,12},{12,0},{1,5},{5,9},{9,13},{13,1},{2,6},{6,10},{... | collective-permute-start | bytes 307208 | tf_op jit(solution)/shard_map/ppermute | solution.py:626
  13.6 1.2 %collective-permute-start.1 = (bf16[400,128]{1,0:T(8,128)(2,1)S(1)}, bf16[400,128]{1,0:T(8,128)(2,1)S(1)}, u32[]{:S(2)}, u32[]{:S(2)}) collective-permute-start(bf16[400,128]{1,0:T(8,128)(2,1)S(1)} %get-tuple-element.60), channel_id=1, source_target_pairs={{0,8},{4,12},{8,0},{12,4},{1,9},{5,13},{9,1},{13,5},{2,10},{6,14},... | collective-permute-start | bytes 307208 | tf_op jit(solution)/shard_map/ppermute | solution.py:626
  14.8 2.7 %collective-permute-start.2 = (bf16[400,128]{1,0:T(8,128)(2,1)S(1)}, bf16[400,128]{1,0:T(8,128)(2,1)S(1)}, u32[]{:S(2)}, u32[]{:S(2)}) collective-permute-start(bf16[400,128]{1,0:T(8,128)(2,1)S(1)} %get-tuple-element.61), channel_id=1, source_target_pairs={{0,12},{4,0},{8,4},{12,8},{1,13},{5,1},{9,5},{13,9},{2,14},{6,2},{... | collective-permute-start | bytes 307208 | tf_op jit(solution)/shard_map/ppermute | solution.py:626
  17.9 1.5 %collective-permute-start.5 = (bf16[32,1280]{1,0:T(8,128)(2,1)S(1)}, bf16[32,1280]{1,0:T(8,128)(2,1)S(1)}, u32[]{:S(2)}, u32[]{:S(2)}) collective-permute-start(bf16[32,1280]{1,0:T(8,128)(2,1)S(1)} %get-tuple-element.65), channel_id=1, source_target_pairs={{0,12},{4,0},{8,4},{12,8},{1,13},{5,1},{9,5},{13,9},{2,14},{6,2},{... | collective-permute-start | bytes 245768 | tf_op jit(solution)/shard_map/ppermute | solution.py:626
  19.3 9.8 %collective-permute-done.4.refs_6_ = bf16[32,1280]{1,0:T(8,128)(2,1)S(1)} collective-permute-done((bf16[32,1280]{1,0:T(8,128)(2,1)S(1)}, bf16[32,1280]{1,0:T(8,128)(2,1)S(1)}, u32[]{:S(2)}, u32[]{:S(2)}) %collective-permute-start.4) | collective-permute-done | bytes 81952 | tf_op jit(solution)/shard_map/ppermute | solution.py:626
  29.1 1.2 %shard_map.129 = (bf16[4,4,32,384]{3,2,1,0:T(8,128)(2,1)}, f32[32,128]{1,0:T(8,128)S(1)}, bf16[384,128]{1,0:T(8,128)(2,1)S(1)}, bf16[384,128]{1,0:T(8,128)(2,1)S...) custom-call(f32[12,128]{1,0:T(8,128)S(1)} %get-tuple-element.57.again_ref, ...), custom_call_target="tpu_custom_call" | custom-call | flops 1000 | bytes 1000 | tf_op jit(solution)/shard_map/pallas_call | solution.py:622
  30.4 6.1 %all-to-all-start = ((bf16[16,32,384]{2,1,0:T(8,128)(2,1)}), bf16[16,32,384]{2,1,0:T(8,128)(2,1)S(1)}, u32[]{:S(2)}, u32[]{:S(2)}) async-start(bf16[16,32,384]{2,1,0:T(8,128)(2,1)} %bitcast.5), calls=%async_computation | async-start | bytes 786432 | tf_op jit(solution)/shard_map/all_to_all | solution.py:714
  36.6 1.6 %collective-permute-start.7 = (bf16[48,1536]{1,0:T(8,128)(2,1)S(1)}, bf16[48,1536]{1,0:T(8,128)(2,1)S(1)}, u32[]{:S(2)}, u32[]{:S(2)}) collective-permute-start(bf16[48,1536]{1,0:T(8,128)(2,1)S(1)} %shard_map.131.refs_0_), channel_id=1, source_target_pairs={{0,2},{1,3},{2,0},{3,1},{4,6},{5,7},{6,4},{7,5},{8,10},{9,11},{10,... | collective-permute-start | bytes 442376 | tf_op jit(solution)/shard_map/ppermute | solution.py:626
  38.3 7.1 %shard_map.130 = (bf16[1,3072,1152]{2,1,0:T(8,128)(2,1)S(1)}, bf16[1,6144,1152]{2,1,0:T(8,128)(2,1)S(1)}) custom-call(bf16[32,1280]{1,0:T(8,128)(2,1)S(1)} %get-tuple-element.62.refs_4_.after_ref, bf16[1,6144,1152]{2,1,0:T(8,128)(2,1)} %gate_ref.3, bf16[1,6144,1152]{2,1,0:T(8,128)(2,1)} %up_ref.1), custom_call_target="tpu_custom_call" | custom-call | flops 1000 | bytes 21000000 | tf_op jit(solution)/shard_map/pallas_call | solution.py:622
  45.3 5.0 %copy-done = bf16[1,6144,1152]{2,1,0:T(8,128)(2,1)} copy-done((bf16[1,6144,1152]{2,1,0:T(8,128)(2,1)}, bf16[1,6144,1152]{2,1,0:T(8,128)(2,1)S(1)}, u32[]{:S(2)}) %copy-start) | copy-done | bytes 14155800
  50.4 2.9 %copy-done.4 = bf16[1,3072,1152]{2,1,0:T(8,128)(2,1)} copy-done((bf16[1,3072,1152]{2,1,0:T(8,128)(2,1)}, bf16[1,3072,1152]{2,1,0:T(8,128)(2,1)S(1)}, u32[]{:S(2)}) %copy-start.4) | copy-done | bytes 7077912
  53.3 5.0 %copy-done.1 = bf16[1,6144,1152]{2,1,0:T(8,128)(2,1)S(1)} copy-done((bf16[1,6144,1152]{2,1,0:T(8,128)(2,1)S(1)}, bf16[1,6144,1152]{2,1,0:T(8,128)(2,1)}, u32[]{:S(2)}) %copy-start.1) | copy-done | bytes 14155800
  58.3 3.0 %copy-done.3 = bf16[1,3072,1152]{2,1,0:T(8,128)(2,1)S(1)} copy-done((bf16[1,3072,1152]{2,1,0:T(8,128)(2,1)S(1)}, bf16[1,3072,1152]{2,1,0:T(8,128)(2,1)}, u32[]{:S(2)}) %copy-start.3) | copy-done | bytes 7077912
  61.3 3.0 %copy-done.5 = bf16[1,3072,1152]{2,1,0:T(8,128)(2,1)S(1)} copy-done((bf16[1,3072,1152]{2,1,0:T(8,128)(2,1)S(1)}, bf16[1,3072,1152]{2,1,0:T(8,128)(2,1)}, u32[]{:S(2)}) %copy-start.5) | copy-done | bytes 7077912
  64.3 5.3 %shard_map.132 = (bf16[32,1152]{1,0:T(8,128)(2,1)S(1)}, f32[32,128]{1,0:T(8,128)S(1)}, bf16[1,4608,1536]{2,1,0:T(8,128)(2,1)S(1)}) custom-call(bf16[16,32,384]{2,1,0:T(8,128)(2,1)S(1)} %all-to-all-done.in_ref, f32[32,128]{1,0:T(8,128)S(1)} %get-tuple-element.71.ids_ref, bf16[1,3072,1152]{2,1,0:T(8,128)(2,1)S(1)} %copy-done.3, ...), custom_call_target="tpu_custom_call" | custom-call | flops 900000000 | bytes 28000000 | tf_op jit(solution)/shard_map/pallas_call | solution.py:622
  69.6 3.3 %collective-permute-start.14 = (bf16[32,1152]{1,0:T(8,128)(2,1)S(1)}, bf16[32,1152]{1,0:T(8,128)(2,1)S(1)}, u32[]{:S(2)}, u32[]{:S(2)}) collective-permute-start(bf16[32,1152]{1,0:T(8,128)(2,1)S(1)} %get-tuple-element.77.refs_0_), channel_id=1, source_target_pairs={{0,12},{4,0},{8,4},{12,8},{1,13},{5,1},{9,5},{13,9},{2,14},{6,2},{... | collective-permute-start | bytes 221192 | tf_op jit(solution)/shard_map/ppermute | solution.py:626
  72.9 1.1 %collective-permute-start.12 = (bf16[32,1152]{1,0:T(8,128)(2,1)S(1)}, bf16[32,1152]{1,0:T(8,128)(2,1)S(1)}, u32[]{:S(2)}, u32[]{:S(2)}) collective-permute-start(bf16[32,1152]{1,0:T(8,128)(2,1)S(1)} %get-tuple-element.77.refs_0_), channel_id=1, source_target_pairs={{0,4},{4,8},{8,12},{12,0},{1,5},{5,9},{9,13},{13,1},{2,6},{6,10},{... | collective-permute-start | bytes 221192 | tf_op jit(solution)/shard_map/ppermute | solution.py:626
  74.1 2.4 %collective-permute-start.9 = (bf16[384,128]{1,0:T(8,128)(2,1)S(1)}, bf16[384,128]{1,0:T(8,128)(2,1)S(1)}, u32[]{:S(2)}, u32[]{:S(2)}) collective-permute-start(bf16[384,128]{1,0:T(8,128)(2,1)S(1)} %get-tuple-element.79), channel_id=1, source_target_pairs={{0,4},{4,8},{8,12},{12,0},{1,5},{5,9},{9,13},{13,1},{2,6},{6,10},{... | collective-permute-start | bytes 294920 | tf_op jit(solution)/shard_map/ppermute | solution.py:626
  76.4 0.9 collective-permute-start.10
  77.3 2.6 %collective-permute-start.11 = (bf16[384,128]{1,0:T(8,128)(2,1)S(1)}, bf16[384,128]{1,0:T(8,128)(2,1)S(1)}, u32[]{:S(2)}, u32[]{:S(2)}) collective-permute-start(bf16[384,128]{1,0:T(8,128)(2,1)S(1)} %get-tuple-element.81), channel_id=1, source_target_pairs={{0,12},{4,0},{8,4},{12,8},{1,13},{5,1},{9,5},{13,9},{2,14},{6,2},{... | collective-permute-start | bytes 294920 | tf_op jit(solution)/shard_map/ppermute | solution.py:626
  80.0 5.4 %collective-permute-done.13.refs_2_ = bf16[32,1152]{1,0:T(8,128)(2,1)S(1)} collective-permute-done((bf16[32,1152]{1,0:T(8,128)(2,1)S(1)}, bf16[32,1152]{1,0:T(8,128)(2,1)S(1)}, u32[]{:S(2)}, u32[]{:S(2)}) %collective-permute-start.13) | collective-permute-done | bytes 73760 | tf_op jit(solution)/shard_map/ppermute | solution.py:626
  85.4 2.5 %shard_map.134 = (bf16[8,1536]{1,0:T(8,128)(2,1)S(1)}, bf16[8,1536]{1,0:T(8,128)(2,1)S(1)}, bf16[8,1536]{1,0:T(8,128)(2,1)S(1)}, bf16[8,1536]{1,0:T(8,128)(2,1)S(1)}) custom-call(bf16[1,4608,1536]{2,1,0:T(8,128)(2,1)S(1)} %get-tuple-element.83.w_ref, f32[32,128]{1,0:T(8,128)S(1)} %get-tuple-element.84.share_ref, ...), custom_call_target="tpu_custom_call" | custom-call | flops 450000000 | bytes 14000000 | tf_op jit(solution)/shard_map/pallas_call | solution.py:622
  87.9 1.9 %collective-permute-start.15 = (bf16[8,1536]{1,0:T(8,128)(2,1)S(1)}, bf16[8,1536]{1,0:T(8,128)(2,1)S(1)}, u32[]{:S(2)}, u32[]{:S(2)}) collective-permute-start(bf16[8,1536]{1,0:T(8,128)(2,1)S(1)} %get-tuple-element.85), channel_id=1, source_target_pairs={{0,0},{1,4},{2,8},{3,12},{4,1},{5,5},{6,9},{7,13},{8,2},{9,6},{10,... | collective-permute-start | bytes 73736 | tf_op jit(solution)/shard_map/ppermute | solution.py:740
  89.8 4.4 %collective-permute-start.16 = (bf16[8,1536]{1,0:T(8,128)(2,1)S(1)}, bf16[8,1536]{1,0:T(8,128)(2,1)S(1)}, u32[]{:S(2)}, u32[]{:S(2)}) collective-permute-start(bf16[8,1536]{1,0:T(8,128)(2,1)S(1)} %get-tuple-element.86), channel_id=1, source_target_pairs={{0,4},{1,8},{2,12},{3,0},{4,5},{5,9},{6,13},{7,1},{8,6},{9,10},{10... | collective-permute-start | bytes 73736 | tf_op jit(solution)/shard_map/ppermute | solution.py:740
  94.3 0.5 shard_map.133.mixed_ref
  94.8 0.6 collective-permute-done.15.refs_0_
  95.7 3.2 %collective-permute-done.17.refs_2_ = bf16[8,1536]{1,0:T(8,128)(2,1)S(1)} collective-permute-done((bf16[8,1536]{1,0:T(8,128)(2,1)S(1)}, bf16[8,1536]{1,0:T(8,128)(2,1)S(1)}, u32[]{:S(2)}, u32[]{:S(2)}) %collective-permute-start.17) | collective-permute-done | bytes 24608 | tf_op jit(solution)/shard_map/ppermute | solution.py:740
  99.3 1.0 %shard_map.135 = bf16[128,1536]{1,0:T(8,128)(2,1)} custom-call(bf16[128,1536]{1,0:T(8,128)(2,1)S(1)} %shard_map.133.mixed_ref, f32[32,128]{1,0:T(8,128)S(1)} %get-tuple-element.82.place_ref, bf16[8,1536]{1,0:T(8,128)(2,1)S(1)} %collective-permute-done.15.refs_0_, bf16[8,1536]{1,0:T(8,128)(2,1)S(1)} %collective-permute-done.16.refs_1_, ...), custom_call_target="tpu_custom_call" | custom-call | flops 1000 | bytes 1000 | tf_op jit(solution)/shard_map/pallas_call | solution.py:622
  (29 shorter events, 1.4 us)
Async XLA Ops:
  7.6 2.8 %copy-start.2 = (bf16[1,3072,1152]{2,1,0:T(8,128)(2,1)}, bf16[1,3072,1152]{2,1,0:T(8,128)(2,1)S(1)}, u32[]{:S(2)}) copy-start(bf16[1,3072,1152]{2,1,0:T(8,128)(2,1)S(1)} %get-tuple-element.72.gate_early_ref) | copy-start | bytes 21233668
  10.4 7.4 %collective-permute-start.3 = (bf16[32,1280]{1,0:T(8,128)(2,1)S(1)}, bf16[32,1280]{1,0:T(8,128)(2,1)S(1)}, u32[]{:S(2)}, u32[]{:S(2)}) collective-permute-start(bf16[32,1280]{1,0:T(8,128)(2,1)S(1)} %get-tuple-element.63), channel_id=1, source_target_pairs={{0,4},{4,8},{8,12},{12,0},{1,5},{5,9},{9,13},{13,1},{2,6},{6,10},{... | collective-permute-start | bytes 245768 | tf_op jit(solution)/shard_map/ppermute | solution.py:626
  12.0 17.1 %collective-permute-start = (bf16[400,128]{1,0:T(8,128)(2,1)S(1)}, bf16[400,128]{1,0:T(8,128)(2,1)S(1)}, u32[]{:S(2)}, u32[]{:S(2)}) collective-permute-start(bf16[400,128]{1,0:T(8,128)(2,1)S(1)} %get-tuple-element.59), channel_id=1, source_target_pairs={{0,4},{4,8},{8,12},{12,0},{1,5},{5,9},{9,13},{13,1},{2,6},{6,10},{... | collective-permute-start | bytes 307208 | tf_op jit(solution)/shard_map/ppermute | solution.py:626
  13.6 15.5 %collective-permute-start.1 = (bf16[400,128]{1,0:T(8,128)(2,1)S(1)}, bf16[400,128]{1,0:T(8,128)(2,1)S(1)}, u32[]{:S(2)}, u32[]{:S(2)}) collective-permute-start(bf16[400,128]{1,0:T(8,128)(2,1)S(1)} %get-tuple-element.60), channel_id=1, source_target_pairs={{0,8},{4,12},{8,0},{12,4},{1,9},{5,13},{9,1},{13,5},{2,10},{6,14},... | collective-permute-start | bytes 307208 | tf_op jit(solution)/shard_map/ppermute | solution.py:626
  14.8 14.3 %collective-permute-start.2 = (bf16[400,128]{1,0:T(8,128)(2,1)S(1)}, bf16[400,128]{1,0:T(8,128)(2,1)S(1)}, u32[]{:S(2)}, u32[]{:S(2)}) collective-permute-start(bf16[400,128]{1,0:T(8,128)(2,1)S(1)} %get-tuple-element.61), channel_id=1, source_target_pairs={{0,12},{4,0},{8,4},{12,8},{1,13},{5,1},{9,5},{13,9},{2,14},{6,2},{... | collective-permute-start | bytes 307208 | tf_op jit(solution)/shard_map/ppermute | solution.py:626
  17.5 11.6 %collective-permute-start.4 = (bf16[32,1280]{1,0:T(8,128)(2,1)S(1)}, bf16[32,1280]{1,0:T(8,128)(2,1)S(1)}, u32[]{:S(2)}, u32[]{:S(2)}) collective-permute-start(bf16[32,1280]{1,0:T(8,128)(2,1)S(1)} %get-tuple-element.64), channel_id=1, source_target_pairs={{0,8},{4,12},{8,0},{12,4},{1,9},{5,13},{9,1},{13,5},{2,10},{6,14},... | collective-permute-start | bytes 245768 | tf_op jit(solution)/shard_map/ppermute | solution.py:626
  17.9 11.2 %collective-permute-start.5 = (bf16[32,1280]{1,0:T(8,128)(2,1)S(1)}, bf16[32,1280]{1,0:T(8,128)(2,1)S(1)}, u32[]{:S(2)}, u32[]{:S(2)}) collective-permute-start(bf16[32,1280]{1,0:T(8,128)(2,1)S(1)} %get-tuple-element.65), channel_id=1, source_target_pairs={{0,12},{4,0},{8,4},{12,8},{1,13},{5,1},{9,5},{13,9},{2,14},{6,2},{... | collective-permute-start | bytes 245768 | tf_op jit(solution)/shard_map/ppermute | solution.py:626
  30.4 22.9 %all-to-all-start = ((bf16[16,32,384]{2,1,0:T(8,128)(2,1)}), bf16[16,32,384]{2,1,0:T(8,128)(2,1)S(1)}, u32[]{:S(2)}, u32[]{:S(2)}) async-start(bf16[16,32,384]{2,1,0:T(8,128)(2,1)} %bitcast.5), calls=%async_computation | async-start | bytes 786432 | tf_op jit(solution)/shard_map/all_to_all | solution.py:714
  36.5 16.8 %collective-permute-start.8 = (bf16[48,1536]{1,0:T(8,128)(2,1)S(1)}, bf16[48,1536]{1,0:T(8,128)(2,1)S(1)}, u32[]{:S(2)}, u32[]{:S(2)}) collective-permute-start(bf16[48,1536]{1,0:T(8,128)(2,1)S(1)} %shard_map.131.refs_0_), channel_id=1, source_target_pairs={{0,3},{1,0},{2,1},{3,2},{4,7},{5,4},{6,5},{7,6},{8,11},{9,8},{10,9... | collective-permute-start | bytes 442376 | tf_op jit(solution)/shard_map/ppermute | solution.py:626
  36.6 16.7 %collective-permute-start.7 = (bf16[48,1536]{1,0:T(8,128)(2,1)S(1)}, bf16[48,1536]{1,0:T(8,128)(2,1)S(1)}, u32[]{:S(2)}, u32[]{:S(2)}) collective-permute-start(bf16[48,1536]{1,0:T(8,128)(2,1)S(1)} %shard_map.131.refs_0_), channel_id=1, source_target_pairs={{0,2},{1,3},{2,0},{3,1},{4,6},{5,7},{6,4},{7,5},{8,10},{9,11},{10,... | collective-permute-start | bytes 442376 | tf_op jit(solution)/shard_map/ppermute | solution.py:626
  38.2 15.0 %collective-permute-start.6 = (bf16[48,1536]{1,0:T(8,128)(2,1)S(1)}, bf16[48,1536]{1,0:T(8,128)(2,1)S(1)}, u32[]{:S(2)}, u32[]{:S(2)}) collective-permute-start(bf16[48,1536]{1,0:T(8,128)(2,1)S(1)} %shard_map.131.refs_0_), channel_id=1, source_target_pairs={{0,1},{1,2},{2,3},{3,0},{4,5},{5,6},{6,7},{7,4},{8,9},{9,10},{10,1... | collective-permute-start | bytes 442376 | tf_op jit(solution)/shard_map/ppermute | solution.py:626
  45.3 5.1 %copy-start = (bf16[1,6144,1152]{2,1,0:T(8,128)(2,1)}, bf16[1,6144,1152]{2,1,0:T(8,128)(2,1)S(1)}, u32[]{:S(2)}) copy-start(bf16[1,6144,1152]{2,1,0:T(8,128)(2,1)S(1)} %get-tuple-element.74.up_ref) | copy-start | bytes 42467332
  50.4 2.9 %copy-start.4 = (bf16[1,3072,1152]{2,1,0:T(8,128)(2,1)}, bf16[1,3072,1152]{2,1,0:T(8,128)(2,1)S(1)}, u32[]{:S(2)}) copy-start(bf16[1,3072,1152]{2,1,0:T(8,128)(2,1)S(1)} %get-tuple-element.73.gate_late_ref) | copy-start | bytes 21233668
  53.3 5.0 %copy-start.1 = (bf16[1,6144,1152]{2,1,0:T(8,128)(2,1)S(1)}, bf16[1,6144,1152]{2,1,0:T(8,128)(2,1)}, u32[]{:S(2)}) copy-start(bf16[1,6144,1152]{2,1,0:T(8,128)(2,1)} %copy-done) | copy-start | bytes 42467332
  58.3 3.0 %copy-start.3 = (bf16[1,3072,1152]{2,1,0:T(8,128)(2,1)S(1)}, bf16[1,3072,1152]{2,1,0:T(8,128)(2,1)}, u32[]{:S(2)}) copy-start(bf16[1,3072,1152]{2,1,0:T(8,128)(2,1)} %copy-done.2) | copy-start | bytes 21233668
  61.3 3.0 %copy-start.5 = (bf16[1,3072,1152]{2,1,0:T(8,128)(2,1)S(1)}, bf16[1,3072,1152]{2,1,0:T(8,128)(2,1)}, u32[]{:S(2)}) copy-start(bf16[1,3072,1152]{2,1,0:T(8,128)(2,1)} %copy-done.4) | copy-start | bytes 21233668
  69.6 7.7 %collective-permute-start.14 = (bf16[32,1152]{1,0:T(8,128)(2,1)S(1)}, bf16[32,1152]{1,0:T(8,128)(2,1)S(1)}, u32[]{:S(2)}, u32[]{:S(2)}) collective-permute-start(bf16[32,1152]{1,0:T(8,128)(2,1)S(1)} %get-tuple-element.77.refs_0_), channel_id=1, source_target_pairs={{0,12},{4,0},{8,4},{12,8},{1,13},{5,1},{9,5},{13,9},{2,14},{6,2},{... | collective-permute-start | bytes 221192 | tf_op jit(solution)/shard_map/ppermute | solution.py:626
  72.9 12.4 %collective-permute-start.13 = (bf16[32,1152]{1,0:T(8,128)(2,1)S(1)}, bf16[32,1152]{1,0:T(8,128)(2,1)S(1)}, u32[]{:S(2)}, u32[]{:S(2)}) collective-permute-start(bf16[32,1152]{1,0:T(8,128)(2,1)S(1)} %get-tuple-element.77.refs_0_), channel_id=1, source_target_pairs={{0,8},{4,12},{8,0},{12,4},{1,9},{5,13},{9,1},{13,5},{2,10},{6,14},... | collective-permute-start | bytes 221192 | tf_op jit(solution)/shard_map/ppermute | solution.py:626
  72.9 12.4 %collective-permute-start.12 = (bf16[32,1152]{1,0:T(8,128)(2,1)S(1)}, bf16[32,1152]{1,0:T(8,128)(2,1)S(1)}, u32[]{:S(2)}, u32[]{:S(2)}) collective-permute-start(bf16[32,1152]{1,0:T(8,128)(2,1)S(1)} %get-tuple-element.77.refs_0_), channel_id=1, source_target_pairs={{0,4},{4,8},{8,12},{12,0},{1,5},{5,9},{9,13},{13,1},{2,6},{6,10},{... | collective-permute-start | bytes 221192 | tf_op jit(solution)/shard_map/ppermute | solution.py:626
  74.1 20.2 %collective-permute-start.9 = (bf16[384,128]{1,0:T(8,128)(2,1)S(1)}, bf16[384,128]{1,0:T(8,128)(2,1)S(1)}, u32[]{:S(2)}, u32[]{:S(2)}) collective-permute-start(bf16[384,128]{1,0:T(8,128)(2,1)S(1)} %get-tuple-element.79), channel_id=1, source_target_pairs={{0,4},{4,8},{8,12},{12,0},{1,5},{5,9},{9,13},{13,1},{2,6},{6,10},{... | collective-permute-start | bytes 294920 | tf_op jit(solution)/shard_map/ppermute | solution.py:626
  76.4 17.8 %collective-permute-start.10 = (bf16[384,128]{1,0:T(8,128)(2,1)S(1)}, bf16[384,128]{1,0:T(8,128)(2,1)S(1)}, u32[]{:S(2)}, u32[]{:S(2)}) collective-permute-start(bf16[384,128]{1,0:T(8,128)(2,1)S(1)} %get-tuple-element.80), channel_id=1, source_target_pairs={{0,8},{4,12},{8,0},{12,4},{1,9},{5,13},{9,1},{13,5},{2,10},{6,14},... | collective-permute-start | bytes 294920 | tf_op jit(solution)/shard_map/ppermute | solution.py:626
  77.3 17.0 %collective-permute-start.11 = (bf16[384,128]{1,0:T(8,128)(2,1)S(1)}, bf16[384,128]{1,0:T(8,128)(2,1)S(1)}, u32[]{:S(2)}, u32[]{:S(2)}) collective-permute-start(bf16[384,128]{1,0:T(8,128)(2,1)S(1)} %get-tuple-element.81), channel_id=1, source_target_pairs={{0,12},{4,0},{8,4},{12,8},{1,13},{5,1},{9,5},{13,9},{2,14},{6,2},{... | collective-permute-start | bytes 294920 | tf_op jit(solution)/shard_map/ppermute | solution.py:626
  87.9 7.5 %collective-permute-start.15 = (bf16[8,1536]{1,0:T(8,128)(2,1)S(1)}, bf16[8,1536]{1,0:T(8,128)(2,1)S(1)}, u32[]{:S(2)}, u32[]{:S(2)}) collective-permute-start(bf16[8,1536]{1,0:T(8,128)(2,1)S(1)} %get-tuple-element.85), channel_id=1, source_target_pairs={{0,0},{1,4},{2,8},{3,12},{4,1},{5,5},{6,9},{7,13},{8,2},{9,6},{10,... | collective-permute-start | bytes 73736 | tf_op jit(solution)/shard_map/ppermute | solution.py:740
  89.8 5.9 %collective-permute-start.16 = (bf16[8,1536]{1,0:T(8,128)(2,1)S(1)}, bf16[8,1536]{1,0:T(8,128)(2,1)S(1)}, u32[]{:S(2)}, u32[]{:S(2)}) collective-permute-start(bf16[8,1536]{1,0:T(8,128)(2,1)S(1)} %get-tuple-element.86), channel_id=1, source_target_pairs={{0,4},{1,8},{2,12},{3,0},{4,5},{5,9},{6,13},{7,1},{8,6},{9,10},{10... | collective-permute-start | bytes 73736 | tf_op jit(solution)/shard_map/ppermute | solution.py:740
  94.2 4.7 %collective-permute-start.17 = (bf16[8,1536]{1,0:T(8,128)(2,1)S(1)}, bf16[8,1536]{1,0:T(8,128)(2,1)S(1)}, u32[]{:S(2)}, u32[]{:S(2)}) collective-permute-start(bf16[8,1536]{1,0:T(8,128)(2,1)S(1)} %get-tuple-element.87), channel_id=1, source_target_pairs={{0,8},{1,12},{2,0},{3,4},{4,9},{5,13},{6,1},{7,5},{8,10},{9,14},{1... | collective-permute-start | bytes 73736 | tf_op jit(solution)/shard_map/ppermute | solution.py:740
  94.2 5.1 %collective-permute-start.18 = (bf16[8,1536]{1,0:T(8,128)(2,1)S(1)}, bf16[8,1536]{1,0:T(8,128)(2,1)S(1)}, u32[]{:S(2)}, u32[]{:S(2)}) collective-permute-start(bf16[8,1536]{1,0:T(8,128)(2,1)S(1)} %get-tuple-element.88), channel_id=1, source_target_pairs={{0,12},{1,0},{2,4},{3,8},{4,13},{5,1},{6,5},{7,9},{8,14},{9,2},{10... | collective-permute-start | bytes 73736 | tf_op jit(solution)/shard_map/ppermute | solution.py:740

commit v4 on v3

--- a/solution.py
+++ b/solution.py
@@ -433,12 +433,9 @@
 
 
 def rows_kernel(
-    heads, seqs, held, q_ref, k_ref, v_ref, res_ref, row_ref, col_ref, ids_ref, prio_ref, gate_ref, local_ref,
-    grown_ref, place_ref, kept_ref, *pieces_and_sem,
+    heads, seqs, held, q_ref, k_ref, v_ref, res_ref, row_ref, col_ref, ids_ref, prio_ref, local_ref,
+    grown_ref, place_ref, *pieces,
 ):
-    pieces, sem = pieces_and_sem[:-1], pieces_and_sem[-1]
-    copy = pltpu.make_async_copy(gate_ref.at[:, pl.ds(0, kept_ref.shape[1]), :], kept_ref, sem)
-    copy.start()
     place_kernel(held, ids_ref, prio_ref, place_ref)
     rows = q_ref.shape[0]
     causal = iota((rows, rows), 0) >= iota((rows, rows), 1)
@@ -466,14 +463,17 @@
         pieces[r][:, part : 2 * part] = nn(place, local_ref[:, cols].astype(BF16)).astype(BF16)
         pieces[r][:, 2 * part : 3 * part] = nn(place, res_ref[:, cols]).astype(BF16)
         pieces[r][:, 3 * part : 3 * part + LANES] = extra.astype(BF16)
-    copy.wait()
-
-
-def keep_kernel(early, after_ref, gate_ref, up_ref, late_ref, kept_ref, sems):
-    copies = (
-        pltpu.make_async_copy(gate_ref.at[:, pl.ds(early, late_ref.shape[1]), :], late_ref, sems.at[0]),
-        pltpu.make_async_copy(up_ref, kept_ref, sems.at[1]),
-    )
+
+
+def copy_rows(source, start, target, sem):
+    return pltpu.make_async_copy(source.at[:, pl.ds(start, target.shape[1]), :], target, sem)
+
+
+def keep_kernel(starts, after_ref, *refs):
+    count = len(starts)
+    copies = [
+        copy_rows(refs[i], starts[i], refs[count + i], refs[2 * count].at[i]) for i in range(count)
+    ]
     for copy in copies:
         copy.start()
     for copy in copies:
@@ -482,8 +482,8 @@
 
 def owner_kernel(heads, seqs, held, again_ref, *refs):
     states, rows_in = refs[:seqs], refs[seqs : 2 * seqs]
-    slots_ref, ids_ref, *rest = refs[2 * seqs :]
-    prefixes, (state_ref, rows_ref, prefix_ref) = rest[:seqs], rest[seqs:]
+    slots_refs, ids_ref, *rest = refs[2 * seqs : 2 * seqs + held], *refs[2 * seqs + held :]
+    prefixes, (state_ref, rows_ref, prefix_ref, mixed_ref) = rest[:seqs], rest[seqs:]
     per = heads // seqs
     part = per * HEAD
     me = lax.axis_index("seq")
@@ -512,42 +512,47 @@
             power = jnp.mean(attended * attended, axis=1, keepdims=True)
             normed = attended * lax.rsqrt(power + EPS) * again
             residual = rows_ref[b, :, 2 * part + j * HEAD : 2 * part + (j + 1) * HEAD].astype(F32)
-            mixed = (residual + normed).astype(BF16)
-            for e in range(held):
-                piece = mixed[e * CAP : (e + 1) * CAP, :]
-                for s in range(seqs):
-                    slots_ref[s, e, b * CAP : (b + 1) * CAP, cols] = piece
+            mixed_ref[b, :, cols] = residual + normed
             if b + 1 < seqs:
                 tail = state_ref[b, part : part + PAD, :].astype(F32)
                 decay = jnp.where(lane == h, tail[0:1, :] + tail[8:9, :], 0.0)
                 carry = jnp.sum(decay, axis=1, keepdims=True) * carry + state_ref[b, cols, :].astype(F32)
+    for r in range(held):
+        at = pl.ds(pl.multiple_of(lax.rem(expert + r, held) * CAP, CAP), CAP)
+        slots_refs[r][...] = jnp.concatenate([mixed_ref[b, at, :] for b in range(seqs)], axis=0).astype(BF16)
     for r in range(seqs):
         prefixes[r][...] = prefix_ref[lax.rem(me + r, seqs)]
 
 
-def expert_in_kernel(seqs, held, width, in_ref, ids_ref, gate_early_ref, gate_late_ref, up_ref, *refs):
-    tables, (down_ref, out_ref, share_ref, kept_ref, x_ref, sem) = refs[:held], refs[held:]
+def join_kernel(*refs):
+    for r, ref in enumerate(refs[:-1]):
+        refs[-1][r] = ref[...]
+
+
+def expert_in_kernel(seqs, held, width, ids_ref, gate_ref, up_ref, *refs):
+    gathered, tables, refs = refs[:seqs], refs[seqs : seqs + held], refs[seqs + held :]
+    down_ref, out_ref, share_ref, kept_ref, x_ref, sem = refs
     copy = pltpu.make_async_copy(down_ref, kept_ref, sem)
     copy.start()
-    part = in_ref.shape[2]
-    slot_rows = in_ref.shape[1]
+    slot_rows, part = gathered[0].shape[1:]
     experts = tables[0].shape[0] - PAD
-    expert = lax.axis_index("exp")
+    me, expert = lax.axis_index("seq"), lax.axis_index("exp")
     squares = jnp.zeros((slot_rows, 1), F32)
-    for i in range(seqs * held):
-        piece = in_ref[i].astype(F32)
-        squares += jnp.sum(piece * piece, axis=1, keepdims=True)
+    for source in gathered:
+        for r in range(held):
+            piece = source[r].astype(F32)
+            squares += jnp.sum(piece * piece, axis=1, keepdims=True)
     inverse = lax.rsqrt(squares / (held * width) + EPS)
     logits = jnp.zeros((slot_rows, experts), F32)
     for r in range(held):
         k = lax.rem(expert + held - r, held)
-        for s in range(seqs):
-            cols = slice(s * part, (s + 1) * part)
+        for i in range(seqs):
+            start = pl.multiple_of(lax.rem(me + seqs - i, seqs) * part, part)
+            cols = pl.ds(start, part)
             gain = tables[r][experts : experts + PAD, cols].astype(F32)
             gain = gain[0:1, :] + gain[1:2, :]
-            scaled = in_ref[s * held + k].astype(F32) * gain * inverse
-            hi, lo = split_hi_lo(scaled)
-            x_ref[:, pl.ds(pl.multiple_of(k * width + s * part, part), part)] = hi
+            hi, lo = split_hi_lo(gathered[i][r].astype(F32) * gain * inverse)
+            x_ref[:, pl.ds(pl.multiple_of(k * width + start, part), part)] = hi
             logits += nt(hi, tables[r][0:experts, cols]) + nt(lo, tables[r][0:experts, cols])
     probs = 1.0 / (1.0 + jnp.exp(-logits))
     lane = iota(probs.shape, 1)
@@ -558,8 +563,7 @@
     own = jnp.sum(jnp.where(lane == expert, probs, 0.0), axis=1, keepdims=True)
     share_ref[...] = jnp.broadcast_to(own / total, share_ref.shape)
     x = x_ref[...]
-    early = gate_early_ref.shape[1]
-    gate = nn(x[:, 0:early], gate_early_ref[0]) + nn(x[:, early:], gate_late_ref[0])
+    gate = nn(x, gate_ref[0])
     up = nn(x, up_ref[0])
     out_ref[...] = (gate * (1.0 / (1.0 + jnp.exp(-gate))) * up).astype(BF16)
     copy.wait()
@@ -569,11 +573,11 @@
     h_refs, out_refs, acc_ref = refs[:seqs], refs[seqs : seqs + held], refs[seqs + held]
     part = h_refs[0].shape[-1]
     me, expert = lax.axis_index("seq"), lax.axis_index("exp")
-    total = None
+    all_ref = refs[seqs + held + 1]
     for r in range(seqs):
         at = pl.multiple_of(lax.rem(me + seqs - r, seqs) * part, part)
-        term = nn(h_refs[r][...], w_ref[0, pl.ds(at, part), :])
-        total = term if total is None else total + term
+        all_ref[:, pl.ds(at, part)] = h_refs[r][...]
+    total = nn(all_ref[...], w_ref[0])
     acc_ref[...] = total * share_ref[:, 0:1]
     for r in range(held):
         at = pl.multiple_of(lax.rem(expert + r, seqs) * CAP, CAP)
@@ -622,12 +626,11 @@
     return kernel(*args[:near], *(pltpu.with_memory_space_constraint(x, pltpu.HBM) for x in args[near:]))
 
 
-def rotate(x, axis, count, step):
-    return lax.ppermute(x, axis, [(i, (i + step) % count) for i in range(count)])
-
-
 def spread(pieces, axis, count):
-    return [pieces[0]] + [rotate(pieces[r], axis, count, r) for r in range(1, count)]
+    parts = [pieces[0]]
+    for r in range(1, count):
+        parts.append(lax.ppermute(pieces[r], axis, [(i, (i + r) % count) for i in range(count)]))
+    return parts
 
 
 def ring_body(
@@ -668,38 +671,31 @@
     states = spread(pieces, "seq", seqs)
     table = run(functools.partial(pack_kernel, heads), shaped((experts + PAD, width), BF16), (router_rows, gain))
     tables = spread([table] * held, "exp", held)
-    early = held * width // 2
-    local, grown, place, gate_early, *row_pieces = run(
+    local, grown, place, *row_pieces = run(
         functools.partial(rows_kernel, heads, seqs, held),
         (
             shaped((rows, width), F32),
             shaped((rows, width), BF16),
             shaped((held * CAP, rows), F32),
-            pltpu.VMEM((1, early, hidden_part), BF16),
             *(shaped((held * CAP, 3 * part + LANES), BF16) for _ in range(seqs)),
         ),
-        (queries, keys, values, stream, cum_row, cum_col, ids, order, gate_weight),
-        scratch=[pltpu.SemaphoreType.DMA],
+        (queries, keys, values, stream, cum_row, cum_col, ids, order),
         flops=200_000_000,
-        nbytes=9_000_000,
+        nbytes=2_000_000,
+    )
+    row_parts = spread(row_pieces, "seq", seqs)
+    (gate_kept,) = run(
+        functools.partial(keep_kernel, (0,)),
+        (pltpu.VMEM(gate_weight.shape, BF16),),
+        (row_pieces[0], gate_weight),
+        scratch=[pltpu.SemaphoreType.DMA((1,))],
+        nbytes=14_000_000,
         anywhere=1,
     )
-    row_parts = spread(row_pieces, "seq", seqs)
-    gate_late, up_kept = run(
-        functools.partial(keep_kernel, early),
-        (
-            pltpu.VMEM((1, held * width - early, hidden_part), BF16),
-            pltpu.VMEM(up_weight.shape, BF16),
-        ),
-        (row_pieces[0], gate_weight, up_weight),
-        scratch=[pltpu.SemaphoreType.DMA((2,))],
-        nbytes=21_000_000,
-        anywhere=2,
-    )
-    slots, slot_ids, *prefixes = run(
+    *outs, slot_ids = run(
         functools.partial(owner_kernel, heads, seqs, held),
         (
-            pltpu.VMEM((seqs, held, slot_rows, part), BF16),
+            *(shaped((slot_rows, part), BF16) for _ in range(held)),
             shaped((slot_rows, LANES), F32),
             *(shaped((part, LANES), BF16) for _ in range(seqs)),
         ),
@@ -708,10 +704,20 @@
             pltpu.VMEM((seqs, part + PAD, LANES), BF16),
             pltpu.VMEM((seqs, held * CAP, 3 * part + LANES), BF16),
             pltpu.VMEM((seqs, part, LANES), BF16),
+            pltpu.VMEM((seqs, held * CAP, part), F32),
         ],
     )
-    slots = slots.reshape(seqs * held, slot_rows, part)
-    gathered = lax.all_to_all(slots, ("seq", "exp"), split_axis=0, concat_axis=0, tiled=True)
+    slots, slot_ids, prefixes = outs[:held], outs[held], outs[held + 1 :] + [slot_ids]
+    swapped = run(join_kernel, shaped((held, slot_rows, part), BF16), spread(slots, "exp", held))
+    gathered = spread([swapped] * seqs, "seq", seqs)
+    (up_kept,) = run(
+        functools.partial(keep_kernel, (0,)),
+        (pltpu.VMEM(up_weight.shape, BF16),),
+        (swapped, up_weight),
+        scratch=[pltpu.SemaphoreType.DMA((1,))],
+        nbytes=14_000_000,
+        anywhere=1,
+    )
     hidden, shares, down_kept = run(
         functools.partial(expert_in_kernel, seqs, held, width),
         (
@@ -719,20 +725,19 @@
             shaped((slot_rows, LANES), F32),
             pltpu.VMEM(down_weight.shape, BF16),
         ),
-        (gathered, slot_ids, gate_early, gate_late, up_kept, *tables, down_weight),
+        (slot_ids, gate_kept, up_kept, *gathered, *tables, down_weight),
         scratch=[pltpu.VMEM((slot_rows, held * width), BF16), pltpu.SemaphoreType.DMA],
         flops=900_000_000,
         nbytes=28_000_000,
         anywhere=1,
     )
     hiddens = spread([hidden] * seqs, "seq", seqs)
-    prefixes, hidden = lax.optimization_barrier((prefixes, hidden))
     returned = spread(prefixes, "seq", seqs)
     outs = run(
         functools.partial(expert_out_kernel, seqs, held),
         (shaped((CAP, out_part), BF16),) * held,
         (down_kept, shares, *hiddens),
-        scratch=[pltpu.VMEM((slot_rows, out_part), F32)],
+        scratch=[pltpu.VMEM((slot_rows, out_part), F32), pltpu.VMEM((slot_rows, seqs * hidden_part), BF16)],
         flops=450_000_000,
         nbytes=14_000_000,
     )

time: 101 us -> 83.2 us (0.82)
  local copies, waits for them, and re-layouts: 21.8 us -> 0 us
  waiting for transfers between devices: 19.7 us -> 23.1 us
  starting transfers between devices: 33.5 us -> 34.7 us
    unnamed x12 -> x0, local copies, waits for them, and re-layouts: 21.8 us -> none
    ppermute x15 -> x21, starting transfers between devices: 21 us -> 28.6 us  [spread(): lax.ppermute(pieces[r], axis, [(i, (i + r) % count) for i in range(count)])]
    all_to_all x1 -> x0, starting transfers between devices: 6.08 us -> none  [ring_body(): lax.all_to_all(slots, ('seq', 'exp'), split_axis=0, concat_axis=0, tiled=...]
    ppermute x15 -> x21, waiting for transfers between devices: 15.2 us -> 18.6 us  [spread(): lax.ppermute(pieces[r], axis, [(i, (i + r) % count) for i in range(count)])]
    pallas_call x9 -> x11, Pallas kernels: 25.2 us -> 25 us  [run(): kernel(*args[:near], *(pltpu.with_memory_space_constraint(x, pltpu.HBM) f...]
  transfers between devices with their start and end apart: 20 -> 25, of which waited for: 6 -> 9; matrix products, arithmetic and copies ran while one was open for 0% -> 0% of each run, Pallas kernels for 10% -> 16%
where the time goes in v4:
time: 83.2 us; the launch traced here: 82.9 us
  starting transfers between devices  34.7 us (42%)
  Pallas kernels  25 us (30%)
  waiting for transfers between devices  23.1 us (28%)
    ppermute x21, starting transfers between devices, spread(): lax.ppermute(pieces[r], axis, [(i, (i + r) % count) for i in range(count)])  28.6 us
    pallas_call x11, Pallas kernels, run(): kernel(*args[:near], *(pltpu.with_memory_space_constraint(x, pltpu.HBM) f...  25 us
    ppermute x21, waiting for transfers between devices, spread(): lax.ppermute(pieces[r], axis, [(i, (i + r) % count) for i in range(count)])  18.6 us
    ppermute x4, starting transfers between devices, ring_body(): lax.ppermute(piece, ('seq', 'exp'), [(s * held + e, (e + r) % seqs * held...  6.13 us
    ppermute x4, waiting for transfers between devices, ring_body(): lax.ppermute(piece, ('seq', 'exp'), [(s * held + e, (e + r) % seqs * held...  4.52 us
  transfers between devices with their start and end apart: 25, of which 9 were waited for; matrix products, arithmetic and copies ran while one was open for 0% of the time, Pallas kernels for 16%

profile of v4, /device:TPU:2, one launch (start us, length us, event | category | flops | bytes accessed | tf_op | source)
XLA Modules:
  0.0 82.9 jit_solution(16496473806225551133)
XLA Ops:
  0.0 2.5 %shard_map.127 = (bf16[128,1536]{1,0:T(8,128)(2,1)S(1)}, bf16[128,1536]{1,0:T(8,128)(2,1)S(1)}, f32[12,128]{1,0:T(8,128)}, bf16[128,1536]{1,0:T(8,128)(2,1)S(1)}...) custom-call(bf16[128,1536]{1,0:T(8,128)(2,1)} %refs_0_.3, ...), custom_call_target="tpu_custom_call" | custom-call | flops 1000 | bytes 1000 | tf_op jit(solution)/shard_map/pallas_call | solution.py:626
  2.5 2.3 %shard_map.128 = (f32[128,1536]{1,0:T(8,128)S(1)}, bf16[128,1536]{1,0:T(8,128)(2,1)S(1)}, f32[32,128]{1,0:T(8,128)S(1)}, bf16[32,1280]{1,0:T(8,128)(2,1)S(1)}, b...) custom-call(bf16[128,1536]{1,0:T(8,128)(2,1)S(1)} %get-tuple-element.43.q_ref, ...), custom_call_target="tpu_custom_call" | custom-call | flops 200000000 | bytes 2000000 | tf_op jit(solution)/shard_map/pallas_call | solution.py:626
  4.8 1.6 %collective-permute-start.3 = (bf16[32,1280]{1,0:T(8,128)(2,1)S(1)}, bf16[32,1280]{1,0:T(8,128)(2,1)S(1)}, u32[]{:S(2)}, u32[]{:S(2)}) collective-permute-start(bf16[32,1280]{1,0:T(8,128)(2,1)S(1)} %get-tuple-element.59), channel_id=1, source_target_pairs={{0,4},{4,8},{8,12},{12,0},{1,5},{5,9},{9,13},{13,1},{2,6},{6,10},{... | collective-permute-start | bytes 245768 | tf_op jit(solution)/shard_map/ppermute | solution.py:632
  6.4 2.6 %collective-permute-start.4 = (bf16[32,1280]{1,0:T(8,128)(2,1)S(1)}, bf16[32,1280]{1,0:T(8,128)(2,1)S(1)}, u32[]{:S(2)}, u32[]{:S(2)}) collective-permute-start(bf16[32,1280]{1,0:T(8,128)(2,1)S(1)} %get-tuple-element.60), channel_id=1, source_target_pairs={{0,8},{4,12},{8,0},{12,4},{1,9},{5,13},{9,1},{13,5},{2,10},{6,14},... | collective-permute-start | bytes 245768 | tf_op jit(solution)/shard_map/ppermute | solution.py:632
  9.2 1.7 %collective-permute-start.1 = (bf16[400,128]{1,0:T(8,128)(2,1)S(1)}, bf16[400,128]{1,0:T(8,128)(2,1)S(1)}, u32[]{:S(2)}, u32[]{:S(2)}) collective-permute-start(bf16[400,128]{1,0:T(8,128)(2,1)S(1)} %get-tuple-element.56), channel_id=1, source_target_pairs={{0,8},{4,12},{8,0},{12,4},{1,9},{5,13},{9,1},{13,5},{2,10},{6,14},... | collective-permute-start | bytes 307208 | tf_op jit(solution)/shard_map/ppermute | solution.py:632
  10.9 1.9 %collective-permute-start.2 = (bf16[400,128]{1,0:T(8,128)(2,1)S(1)}, bf16[400,128]{1,0:T(8,128)(2,1)S(1)}, u32[]{:S(2)}, u32[]{:S(2)}) collective-permute-start(bf16[400,128]{1,0:T(8,128)(2,1)S(1)} %get-tuple-element.57), channel_id=1, source_target_pairs={{0,12},{4,0},{8,4},{12,8},{1,13},{5,1},{9,5},{13,9},{2,14},{6,2},{... | collective-permute-start | bytes 307208 | tf_op jit(solution)/shard_map/ppermute | solution.py:632
  13.0 6.0 %collective-permute-done.4.refs_6_ = bf16[32,1280]{1,0:T(8,128)(2,1)S(1)} collective-permute-done((bf16[32,1280]{1,0:T(8,128)(2,1)S(1)}, bf16[32,1280]{1,0:T(8,128)(2,1)S(1)}, u32[]{:S(2)}, u32[]{:S(2)}) %collective-permute-start.4) | collective-permute-done | bytes 81952 | tf_op jit(solution)/shard_map/ppermute | solution.py:632
  19.0 2.6 %collective-permute-start.5 = (bf16[32,1280]{1,0:T(8,128)(2,1)S(1)}, bf16[32,1280]{1,0:T(8,128)(2,1)S(1)}, u32[]{:S(2)}, u32[]{:S(2)}) collective-permute-start(bf16[32,1280]{1,0:T(8,128)(2,1)S(1)} %get-tuple-element.61), channel_id=1, source_target_pairs={{0,12},{4,0},{8,4},{12,8},{1,13},{5,1},{9,5},{13,9},{2,14},{6,2},{... | collective-permute-start | bytes 245768 | tf_op jit(solution)/shard_map/ppermute | solution.py:632
  21.6 2.1 %collective-permute-done.5.refs_7_ = bf16[32,1280]{1,0:T(8,128)(2,1)S(1)} collective-permute-done((bf16[32,1280]{1,0:T(8,128)(2,1)S(1)}, bf16[32,1280]{1,0:T(8,128)(2,1)S(1)}, u32[]{:S(2)}, u32[]{:S(2)}) %collective-permute-start.5) | collective-permute-done | bytes 81952 | tf_op jit(solution)/shard_map/ppermute | solution.py:632
  23.6 0.5 shard_map.129
  24.2 0.6 collective-permute-start.16
  24.8 1.2 %collective-permute-start.15 = (bf16[48,1536]{1,0:T(8,128)(2,1)S(1)}, bf16[48,1536]{1,0:T(8,128)(2,1)S(1)}, u32[]{:S(2)}, u32[]{:S(2)}) collective-permute-start(bf16[48,1536]{1,0:T(8,128)(2,1)S(1)} %shard_map.134.refs_4_), channel_id=1, source_target_pairs={{0,1},{1,2},{2,3},{3,0},{4,5},{5,6},{6,7},{7,4},{8,9},{9,10},{10,1... | collective-permute-start | bytes 442376 | tf_op jit(solution)/shard_map/ppermute | solution.py:632
  26.1 0.5 collective-permute-start.10
  26.6 0.8 %collective-permute-done.9.refs_1_ = bf16[32,384]{1,0:T(8,128)(2,1)S(1)} collective-permute-done((bf16[32,384]{1,0:T(8,128)(2,1)S(1)}, bf16[32,384]{1,0:T(8,128)(2,1)S(1)}, u32[]{:S(2)}, u32[]{:S(2)}) %collective-permute-start.9) | collective-permute-done | bytes 24608 | tf_op jit(solution)/shard_map/ppermute | solution.py:632
  27.8 3.8 %collective-permute-done.10.refs_2_ = bf16[32,384]{1,0:T(8,128)(2,1)S(1)} collective-permute-done((bf16[32,384]{1,0:T(8,128)(2,1)S(1)}, bf16[32,384]{1,0:T(8,128)(2,1)S(1)}, u32[]{:S(2)}, u32[]{:S(2)}) %collective-permute-start.10) | collective-permute-done | bytes 24608 | tf_op jit(solution)/shard_map/ppermute | solution.py:632
  31.5 4.2 %collective-permute-start.14 = (bf16[4,32,384]{2,1,0:T(8,128)(2,1)S(1)}, bf16[4,32,384]{2,1,0:T(8,128)(2,1)S(1)}, u32[]{:S(2)}, u32[]{:S(2)}) collective-permute-start(bf16[4,32,384]{2,1,0:T(8,128)(2,1)S(1)} %shard_map.132.after_ref.refs_0_), channel_id=1, source_target_pairs={{0,12},{4,0},{8,4},{12,8},{1,13},{5,1},{9,5},{13,9},{2,14},{6,2},{... | collective-permute-start | bytes 294920 | tf_op jit(solution)/shard_map/ppermute | solution.py:632
  35.8 0.6 collective-permute-start.12
  36.4 5.0 %shard_map.131.gate_ref = bf16[1,6144,1152]{2,1,0:T(8,128)(2,1)S(1)} custom-call(bf16[32,1280]{1,0:T(8,128)(2,1)S(1)} %get-tuple-element.58.refs_4_.after_ref, bf16[1,6144,1152]{2,1,0:T(8,128)(2,1)} %refs_0_.4), custom_call_target="tpu_custom_call" | custom-call | flops 1000 | bytes 14000000 | tf_op jit(solution)/shard_map/pallas_call | solution.py:626
  41.5 5.0 %shard_map.133.up_ref = bf16[1,6144,1152]{2,1,0:T(8,128)(2,1)S(1)} custom-call(bf16[4,32,384]{2,1,0:T(8,128)(2,1)S(1)} %shard_map.132.after_ref.refs_0_, bf16[1,6144,1152]{2,1,0:T(8,128)(2,1)} %refs_0_.5), custom_call_target="tpu_custom_call" | custom-call | flops 1000 | bytes 14000000 | tf_op jit(solution)/shard_map/pallas_call | solution.py:626
  46.6 5.5 %shard_map.135 = (bf16[32,1152]{1,0:T(8,128)(2,1)S(1)}, f32[32,128]{1,0:T(8,128)S(1)}, bf16[1,4608,1536]{2,1,0:T(8,128)(2,1)S(1)}) custom-call(f32[32,128]{1,0:T(8,128)S(1)} %get-tuple-element.67.ids_ref, bf16[1,6144,1152]{2,1,0:T(8,128)(2,1)S(1)} %shard_map.131.gate_ref, bf16[1,6144,1152]{2,1,0:T(8,128)(2,1)S(1)} %shard_map.133.up_ref, ...), custom_call_target="tpu_custom_call" | custom-call | flops 900000000 | bytes 28000000 | tf_op jit(solution)/shard_map/pallas_call | solution.py:626
  52.1 3.2 %collective-permute-start.20 = (bf16[32,1152]{1,0:T(8,128)(2,1)S(1)}, bf16[32,1152]{1,0:T(8,128)(2,1)S(1)}, u32[]{:S(2)}, u32[]{:S(2)}) collective-permute-start(bf16[32,1152]{1,0:T(8,128)(2,1)S(1)} %get-tuple-element.76.refs_0_), channel_id=1, source_target_pairs={{0,12},{4,0},{8,4},{12,8},{1,13},{5,1},{9,5},{13,9},{2,14},{6,2},{... | collective-permute-start | bytes 221192 | tf_op jit(solution)/shard_map/ppermute | solution.py:632
  55.3 1.1 %collective-permute-start.19 = (bf16[32,1152]{1,0:T(8,128)(2,1)S(1)}, bf16[32,1152]{1,0:T(8,128)(2,1)S(1)}, u32[]{:S(2)}, u32[]{:S(2)}) collective-permute-start(bf16[32,1152]{1,0:T(8,128)(2,1)S(1)} %get-tuple-element.76.refs_0_), channel_id=1, source_target_pairs={{0,8},{4,12},{8,0},{12,4},{1,9},{5,13},{9,1},{13,5},{2,10},{6,14},... | collective-permute-start | bytes 221192 | tf_op jit(solution)/shard_map/ppermute | solution.py:632
  56.4 2.4 %collective-permute-start.6 = (bf16[384,128]{1,0:T(8,128)(2,1)S(1)}, bf16[384,128]{1,0:T(8,128)(2,1)S(1)}, u32[]{:S(2)}, u32[]{:S(2)}) collective-permute-start(bf16[384,128]{1,0:T(8,128)(2,1)S(1)} %get-tuple-element.63), channel_id=1, source_target_pairs={{0,4},{4,8},{8,12},{12,0},{1,5},{5,9},{9,13},{13,1},{2,6},{6,10},{... | collective-permute-start | bytes 294920 | tf_op jit(solution)/shard_map/ppermute | solution.py:632
  58.8 2.0 %collective-permute-start.7 = (bf16[384,128]{1,0:T(8,128)(2,1)S(1)}, bf16[384,128]{1,0:T(8,128)(2,1)S(1)}, u32[]{:S(2)}, u32[]{:S(2)}) collective-permute-start(bf16[384,128]{1,0:T(8,128)(2,1)S(1)} %get-tuple-element.64), channel_id=1, source_target_pairs={{0,8},{4,12},{8,0},{12,4},{1,9},{5,13},{9,1},{13,5},{2,10},{6,14},... | collective-permute-start | bytes 294920 | tf_op jit(solution)/shard_map/ppermute | solution.py:632
  60.8 1.5 %collective-permute-start.8 = (bf16[384,128]{1,0:T(8,128)(2,1)S(1)}, bf16[384,128]{1,0:T(8,128)(2,1)S(1)}, u32[]{:S(2)}, u32[]{:S(2)}) collective-permute-start(bf16[384,128]{1,0:T(8,128)(2,1)S(1)} %get-tuple-element.65), channel_id=1, source_target_pairs={{0,12},{4,0},{8,4},{12,8},{1,13},{5,1},{9,5},{13,9},{2,14},{6,2},{... | collective-permute-start | bytes 294920 | tf_op jit(solution)/shard_map/ppermute | solution.py:632
  62.3 5.8 %collective-permute-done.19.refs_2_ = bf16[32,1152]{1,0:T(8,128)(2,1)S(1)} collective-permute-done((bf16[32,1152]{1,0:T(8,128)(2,1)S(1)}, bf16[32,1152]{1,0:T(8,128)(2,1)S(1)}, u32[]{:S(2)}, u32[]{:S(2)}) %collective-permute-start.19) | collective-permute-done | bytes 73760 | tf_op jit(solution)/shard_map/ppermute | solution.py:632
  68.2 2.5 %shard_map.136 = (bf16[8,1536]{1,0:T(8,128)(2,1)S(1)}, bf16[8,1536]{1,0:T(8,128)(2,1)S(1)}, bf16[8,1536]{1,0:T(8,128)(2,1)S(1)}, bf16[8,1536]{1,0:T(8,128)(2,1)S(1)}) custom-call(bf16[1,4608,1536]{2,1,0:T(8,128)(2,1)S(1)} %get-tuple-element.74.w_ref, f32[32,128]{1,0:T(8,128)S(1)} %get-tuple-element.75.share_ref, ...), custom_call_target="tpu_custom_call" | custom-call | flops 450000000 | bytes 14000000 | tf_op jit(solution)/shard_map/pallas_call | solution.py:626
  70.7 1.9 %collective-permute-start.21 = (bf16[8,1536]{1,0:T(8,128)(2,1)S(1)}, bf16[8,1536]{1,0:T(8,128)(2,1)S(1)}, u32[]{:S(2)}, u32[]{:S(2)}) collective-permute-start(bf16[8,1536]{1,0:T(8,128)(2,1)S(1)} %get-tuple-element.77), channel_id=1, source_target_pairs={{0,0},{1,4},{2,8},{3,12},{4,1},{5,5},{6,9},{7,13},{8,2},{9,6},{10,... | collective-permute-start | bytes 73736 | tf_op jit(solution)/shard_map/ppermute | solution.py:745
  72.6 4.1 %collective-permute-start.22 = (bf16[8,1536]{1,0:T(8,128)(2,1)S(1)}, bf16[8,1536]{1,0:T(8,128)(2,1)S(1)}, u32[]{:S(2)}, u32[]{:S(2)}) collective-permute-start(bf16[8,1536]{1,0:T(8,128)(2,1)S(1)} %get-tuple-element.78), channel_id=1, source_target_pairs={{0,4},{1,8},{2,12},{3,0},{4,5},{5,9},{6,13},{7,1},{8,6},{9,10},{10... | collective-permute-start | bytes 73736 | tf_op jit(solution)/shard_map/ppermute | solution.py:745
  77.4 0.9 %collective-permute-done.21.refs_0_ = bf16[8,1536]{1,0:T(8,128)(2,1)S(1)} collective-permute-done((bf16[8,1536]{1,0:T(8,128)(2,1)S(1)}, bf16[8,1536]{1,0:T(8,128)(2,1)S(1)}, u32[]{:S(2)}, u32[]{:S(2)}) %collective-permute-start.21) | collective-permute-done | bytes 24608 | tf_op jit(solution)/shard_map/ppermute | solution.py:745
  78.3 3.2 %collective-permute-done.23.refs_2_ = bf16[8,1536]{1,0:T(8,128)(2,1)S(1)} collective-permute-done((bf16[8,1536]{1,0:T(8,128)(2,1)S(1)}, bf16[8,1536]{1,0:T(8,128)(2,1)S(1)}, u32[]{:S(2)}, u32[]{:S(2)}) %collective-permute-start.23) | collective-permute-done | bytes 24608 | tf_op jit(solution)/shard_map/ppermute | solution.py:745
  81.9 1.0 %shard_map.137 = bf16[128,1536]{1,0:T(8,128)(2,1)} custom-call(bf16[128,1536]{1,0:T(8,128)(2,1)S(1)} %shard_map.130.mixed_ref, f32[32,128]{1,0:T(8,128)S(1)} %get-tuple-element.66.place_ref, bf16[8,1536]{1,0:T(8,128)(2,1)S(1)} %collective-permute-done.21.refs_0_, bf16[8,1536]{1,0:T(8,128)(2,1)S(1)} %collective-permute-done.22.refs_1_, ...), custom_call_target="tpu_custom_call" | custom-call | flops 1000 | bytes 1000 | tf_op jit(solution)/shard_map/pallas_call | solution.py:626
  (29 shorter events, 1.8 us)
Async XLA Ops:
  4.8 8.1 %collective-permute-start.3 = (bf16[32,1280]{1,0:T(8,128)(2,1)S(1)}, bf16[32,1280]{1,0:T(8,128)(2,1)S(1)}, u32[]{:S(2)}, u32[]{:S(2)}) collective-permute-start(bf16[32,1280]{1,0:T(8,128)(2,1)S(1)} %get-tuple-element.59), channel_id=1, source_target_pairs={{0,4},{4,8},{8,12},{12,0},{1,5},{5,9},{9,13},{13,1},{2,6},{6,10},{... | collective-permute-start | bytes 245768 | tf_op jit(solution)/shard_map/ppermute | solution.py:632
  6.4 12.6 %collective-permute-start.4 = (bf16[32,1280]{1,0:T(8,128)(2,1)S(1)}, bf16[32,1280]{1,0:T(8,128)(2,1)S(1)}, u32[]{:S(2)}, u32[]{:S(2)}) collective-permute-start(bf16[32,1280]{1,0:T(8,128)(2,1)S(1)} %get-tuple-element.60), channel_id=1, source_target_pairs={{0,8},{4,12},{8,0},{12,4},{1,9},{5,13},{9,1},{13,5},{2,10},{6,14},... | collective-permute-start | bytes 245768 | tf_op jit(solution)/shard_map/ppermute | solution.py:632
  9.0 14.6 %collective-permute-start = (bf16[400,128]{1,0:T(8,128)(2,1)S(1)}, bf16[400,128]{1,0:T(8,128)(2,1)S(1)}, u32[]{:S(2)}, u32[]{:S(2)}) collective-permute-start(bf16[400,128]{1,0:T(8,128)(2,1)S(1)} %get-tuple-element.55), channel_id=1, source_target_pairs={{0,4},{4,8},{8,12},{12,0},{1,5},{5,9},{9,13},{13,1},{2,6},{6,10},{... | collective-permute-start | bytes 307208 | tf_op jit(solution)/shard_map/ppermute | solution.py:632
  9.2 14.4 %collective-permute-start.1 = (bf16[400,128]{1,0:T(8,128)(2,1)S(1)}, bf16[400,128]{1,0:T(8,128)(2,1)S(1)}, u32[]{:S(2)}, u32[]{:S(2)}) collective-permute-start(bf16[400,128]{1,0:T(8,128)(2,1)S(1)} %get-tuple-element.56), channel_id=1, source_target_pairs={{0,8},{4,12},{8,0},{12,4},{1,9},{5,13},{9,1},{13,5},{2,10},{6,14},... | collective-permute-start | bytes 307208 | tf_op jit(solution)/shard_map/ppermute | solution.py:632
  10.9 12.7 %collective-permute-start.2 = (bf16[400,128]{1,0:T(8,128)(2,1)S(1)}, bf16[400,128]{1,0:T(8,128)(2,1)S(1)}, u32[]{:S(2)}, u32[]{:S(2)}) collective-permute-start(bf16[400,128]{1,0:T(8,128)(2,1)S(1)} %get-tuple-element.57), channel_id=1, source_target_pairs={{0,12},{4,0},{8,4},{12,8},{1,13},{5,1},{9,5},{13,9},{2,14},{6,2},{... | collective-permute-start | bytes 307208 | tf_op jit(solution)/shard_map/ppermute | solution.py:632
  12.9 22.9 %collective-permute-start.17 = (bf16[48,1536]{1,0:T(8,128)(2,1)S(1)}, bf16[48,1536]{1,0:T(8,128)(2,1)S(1)}, u32[]{:S(2)}, u32[]{:S(2)}) collective-permute-start(bf16[48,1536]{1,0:T(8,128)(2,1)S(1)} %shard_map.134.refs_4_), channel_id=1, source_target_pairs={{0,3},{1,0},{2,1},{3,2},{4,7},{5,4},{6,5},{7,6},{8,11},{9,8},{10,9... | collective-permute-start | bytes 442376 | tf_op jit(solution)/shard_map/ppermute | solution.py:632
  19.0 4.6 %collective-permute-start.5 = (bf16[32,1280]{1,0:T(8,128)(2,1)S(1)}, bf16[32,1280]{1,0:T(8,128)(2,1)S(1)}, u32[]{:S(2)}, u32[]{:S(2)}) collective-permute-start(bf16[32,1280]{1,0:T(8,128)(2,1)S(1)} %get-tuple-element.61), channel_id=1, source_target_pairs={{0,12},{4,0},{8,4},{12,8},{1,13},{5,1},{9,5},{13,9},{2,14},{6,2},{... | collective-permute-start | bytes 245768 | tf_op jit(solution)/shard_map/ppermute | solution.py:632
  24.1 3.3 %collective-permute-start.9 = (bf16[32,384]{1,0:T(8,128)(2,1)S(1)}, bf16[32,384]{1,0:T(8,128)(2,1)S(1)}, u32[]{:S(2)}, u32[]{:S(2)}) collective-permute-start(bf16[32,384]{1,0:T(8,128)(2,1)S(1)} %get-tuple-element.69), channel_id=1, source_target_pairs={{0,1},{1,2},{2,3},{3,0},{4,5},{5,6},{6,7},{7,4},{8,9},{9,10},{10,1... | collective-permute-start | bytes 73736 | tf_op jit(solution)/shard_map/ppermute | solution.py:632
  24.2 22.3 %collective-permute-start.16 = (bf16[48,1536]{1,0:T(8,128)(2,1)S(1)}, bf16[48,1536]{1,0:T(8,128)(2,1)S(1)}, u32[]{:S(2)}, u32[]{:S(2)}) collective-permute-start(bf16[48,1536]{1,0:T(8,128)(2,1)S(1)} %shard_map.134.refs_4_), channel_id=1, source_target_pairs={{0,2},{1,3},{2,0},{3,1},{4,6},{5,7},{6,4},{7,5},{8,10},{9,11},{10,... | collective-permute-start | bytes 442376 | tf_op jit(solution)/shard_map/ppermute | solution.py:632
  24.8 21.7 %collective-permute-start.15 = (bf16[48,1536]{1,0:T(8,128)(2,1)S(1)}, bf16[48,1536]{1,0:T(8,128)(2,1)S(1)}, u32[]{:S(2)}, u32[]{:S(2)}) collective-permute-start(bf16[48,1536]{1,0:T(8,128)(2,1)S(1)} %shard_map.134.refs_4_), channel_id=1, source_target_pairs={{0,1},{1,2},{2,3},{3,0},{4,5},{5,6},{6,7},{7,4},{8,9},{9,10},{10,1... | collective-permute-start | bytes 442376 | tf_op jit(solution)/shard_map/ppermute | solution.py:632
  26.1 5.5 %collective-permute-start.10 = (bf16[32,384]{1,0:T(8,128)(2,1)S(1)}, bf16[32,384]{1,0:T(8,128)(2,1)S(1)}, u32[]{:S(2)}, u32[]{:S(2)}) collective-permute-start(bf16[32,384]{1,0:T(8,128)(2,1)S(1)} %get-tuple-element.70), channel_id=1, source_target_pairs={{0,2},{1,3},{2,0},{3,1},{4,6},{5,7},{6,4},{7,5},{8,10},{9,11},{10,... | collective-permute-start | bytes 73736 | tf_op jit(solution)/shard_map/ppermute | solution.py:632
  27.5 4.1 %collective-permute-start.11 = (bf16[32,384]{1,0:T(8,128)(2,1)S(1)}, bf16[32,384]{1,0:T(8,128)(2,1)S(1)}, u32[]{:S(2)}, u32[]{:S(2)}) collective-permute-start(bf16[32,384]{1,0:T(8,128)(2,1)S(1)} %get-tuple-element.71), channel_id=1, source_target_pairs={{0,3},{1,0},{2,1},{3,2},{4,7},{5,4},{6,5},{7,6},{8,11},{9,8},{10,9... | collective-permute-start | bytes 73736 | tf_op jit(solution)/shard_map/ppermute | solution.py:632
  31.5 15.0 %collective-permute-start.14 = (bf16[4,32,384]{2,1,0:T(8,128)(2,1)S(1)}, bf16[4,32,384]{2,1,0:T(8,128)(2,1)S(1)}, u32[]{:S(2)}, u32[]{:S(2)}) collective-permute-start(bf16[4,32,384]{2,1,0:T(8,128)(2,1)S(1)} %shard_map.132.after_ref.refs_0_), channel_id=1, source_target_pairs={{0,12},{4,0},{8,4},{12,8},{1,13},{5,1},{9,5},{13,9},{2,14},{6,2},{... | collective-permute-start | bytes 294920 | tf_op jit(solution)/shard_map/ppermute | solution.py:632
  35.8 10.8 %collective-permute-start.13 = (bf16[4,32,384]{2,1,0:T(8,128)(2,1)S(1)}, bf16[4,32,384]{2,1,0:T(8,128)(2,1)S(1)}, u32[]{:S(2)}, u32[]{:S(2)}) collective-permute-start(bf16[4,32,384]{2,1,0:T(8,128)(2,1)S(1)} %shard_map.132.after_ref.refs_0_), channel_id=1, source_target_pairs={{0,8},{4,12},{8,0},{12,4},{1,9},{5,13},{9,1},{13,5},{2,10},{6,14},... | collective-permute-start | bytes 294920 | tf_op jit(solution)/shard_map/ppermute | solution.py:632
  35.8 10.8 %collective-permute-start.12 = (bf16[4,32,384]{2,1,0:T(8,128)(2,1)S(1)}, bf16[4,32,384]{2,1,0:T(8,128)(2,1)S(1)}, u32[]{:S(2)}, u32[]{:S(2)}) collective-permute-start(bf16[4,32,384]{2,1,0:T(8,128)(2,1)S(1)} %shard_map.132.after_ref.refs_0_), channel_id=1, source_target_pairs={{0,4},{4,8},{8,12},{12,0},{1,5},{5,9},{9,13},{13,1},{2,6},{6,10},{... | collective-permute-start | bytes 294920 | tf_op jit(solution)/shard_map/ppermute | solution.py:632
  52.1 8.7 %collective-permute-start.20 = (bf16[32,1152]{1,0:T(8,128)(2,1)S(1)}, bf16[32,1152]{1,0:T(8,128)(2,1)S(1)}, u32[]{:S(2)}, u32[]{:S(2)}) collective-permute-start(bf16[32,1152]{1,0:T(8,128)(2,1)S(1)} %get-tuple-element.76.refs_0_), channel_id=1, source_target_pairs={{0,12},{4,0},{8,4},{12,8},{1,13},{5,1},{9,5},{13,9},{2,14},{6,2},{... | collective-permute-start | bytes 221192 | tf_op jit(solution)/shard_map/ppermute | solution.py:632
  55.3 12.9 %collective-permute-start.19 = (bf16[32,1152]{1,0:T(8,128)(2,1)S(1)}, bf16[32,1152]{1,0:T(8,128)(2,1)S(1)}, u32[]{:S(2)}, u32[]{:S(2)}) collective-permute-start(bf16[32,1152]{1,0:T(8,128)(2,1)S(1)} %get-tuple-element.76.refs_0_), channel_id=1, source_target_pairs={{0,8},{4,12},{8,0},{12,4},{1,9},{5,13},{9,1},{13,5},{2,10},{6,14},... | collective-permute-start | bytes 221192 | tf_op jit(solution)/shard_map/ppermute | solution.py:632
  56.4 11.7 %collective-permute-start.18 = (bf16[32,1152]{1,0:T(8,128)(2,1)S(1)}, bf16[32,1152]{1,0:T(8,128)(2,1)S(1)}, u32[]{:S(2)}, u32[]{:S(2)}) collective-permute-start(bf16[32,1152]{1,0:T(8,128)(2,1)S(1)} %get-tuple-element.76.refs_0_), channel_id=1, source_target_pairs={{0,4},{4,8},{8,12},{12,0},{1,5},{5,9},{9,13},{13,1},{2,6},{6,10},{... | collective-permute-start | bytes 221192 | tf_op jit(solution)/shard_map/ppermute | solution.py:632
  56.4 20.3 %collective-permute-start.6 = (bf16[384,128]{1,0:T(8,128)(2,1)S(1)}, bf16[384,128]{1,0:T(8,128)(2,1)S(1)}, u32[]{:S(2)}, u32[]{:S(2)}) collective-permute-start(bf16[384,128]{1,0:T(8,128)(2,1)S(1)} %get-tuple-element.63), channel_id=1, source_target_pairs={{0,4},{4,8},{8,12},{12,0},{1,5},{5,9},{9,13},{13,1},{2,6},{6,10},{... | collective-permute-start | bytes 294920 | tf_op jit(solution)/shard_map/ppermute | solution.py:632
  58.8 18.0 %collective-permute-start.7 = (bf16[384,128]{1,0:T(8,128)(2,1)S(1)}, bf16[384,128]{1,0:T(8,128)(2,1)S(1)}, u32[]{:S(2)}, u32[]{:S(2)}) collective-permute-start(bf16[384,128]{1,0:T(8,128)(2,1)S(1)} %get-tuple-element.64), channel_id=1, source_target_pairs={{0,8},{4,12},{8,0},{12,4},{1,9},{5,13},{9,1},{13,5},{2,10},{6,14},... | collective-permute-start | bytes 294920 | tf_op jit(solution)/shard_map/ppermute | solution.py:632
  60.8 16.0 %collective-permute-start.8 = (bf16[384,128]{1,0:T(8,128)(2,1)S(1)}, bf16[384,128]{1,0:T(8,128)(2,1)S(1)}, u32[]{:S(2)}, u32[]{:S(2)}) collective-permute-start(bf16[384,128]{1,0:T(8,128)(2,1)S(1)} %get-tuple-element.65), channel_id=1, source_target_pairs={{0,12},{4,0},{8,4},{12,8},{1,13},{5,1},{9,5},{13,9},{2,14},{6,2},{... | collective-permute-start | bytes 294920 | tf_op jit(solution)/shard_map/ppermute | solution.py:632
  70.7 7.5 %collective-permute-start.21 = (bf16[8,1536]{1,0:T(8,128)(2,1)S(1)}, bf16[8,1536]{1,0:T(8,128)(2,1)S(1)}, u32[]{:S(2)}, u32[]{:S(2)}) collective-permute-start(bf16[8,1536]{1,0:T(8,128)(2,1)S(1)} %get-tuple-element.77), channel_id=1, source_target_pairs={{0,0},{1,4},{2,8},{3,12},{4,1},{5,5},{6,9},{7,13},{8,2},{9,6},{10,... | collective-permute-start | bytes 73736 | tf_op jit(solution)/shard_map/ppermute | solution.py:745
  72.6 5.7 %collective-permute-start.22 = (bf16[8,1536]{1,0:T(8,128)(2,1)S(1)}, bf16[8,1536]{1,0:T(8,128)(2,1)S(1)}, u32[]{:S(2)}, u32[]{:S(2)}) collective-permute-start(bf16[8,1536]{1,0:T(8,128)(2,1)S(1)} %get-tuple-element.78), channel_id=1, source_target_pairs={{0,4},{1,8},{2,12},{3,0},{4,5},{5,9},{6,13},{7,1},{8,6},{9,10},{10... | collective-permute-start | bytes 73736 | tf_op jit(solution)/shard_map/ppermute | solution.py:745
  76.8 4.7 %collective-permute-start.23 = (bf16[8,1536]{1,0:T(8,128)(2,1)S(1)}, bf16[8,1536]{1,0:T(8,128)(2,1)S(1)}, u32[]{:S(2)}, u32[]{:S(2)}) collective-permute-start(bf16[8,1536]{1,0:T(8,128)(2,1)S(1)} %get-tuple-element.79), channel_id=1, source_target_pairs={{0,8},{1,12},{2,0},{3,4},{4,9},{5,13},{6,1},{7,5},{8,10},{9,14},{1... | collective-permute-start | bytes 73736 | tf_op jit(solution)/shard_map/ppermute | solution.py:745
  76.8 5.1 %collective-permute-start.24 = (bf16[8,1536]{1,0:T(8,128)(2,1)S(1)}, bf16[8,1536]{1,0:T(8,128)(2,1)S(1)}, u32[]{:S(2)}, u32[]{:S(2)}) collective-permute-start(bf16[8,1536]{1,0:T(8,128)(2,1)S(1)} %get-tuple-element.80), channel_id=1, source_target_pairs={{0,12},{1,0},{2,4},{3,8},{4,13},{5,1},{6,5},{7,9},{8,14},{9,2},{10... | collective-permute-start | bytes 73736 | tf_op jit(solution)/shard_map/ppermute | solution.py:745

commit v5 on v4

--- a/solution.py
+++ b/solution.py
@@ -569,15 +569,25 @@
     copy.wait()
 
 
-def expert_out_kernel(seqs, held, w_ref, share_ref, *refs):
-    h_refs, out_refs, acc_ref = refs[:seqs], refs[seqs : seqs + held], refs[seqs + held]
+def down_part(me, seqs, steps, w_ref, h_refs):
     part = h_refs[0].shape[-1]
-    me, expert = lax.axis_index("seq"), lax.axis_index("exp")
-    all_ref = refs[seqs + held + 1]
-    for r in range(seqs):
+    total = None
+    for r, h_ref in zip(steps, h_refs):
         at = pl.multiple_of(lax.rem(me + seqs - r, seqs) * part, part)
-        all_ref[:, pl.ds(at, part)] = h_refs[r][...]
-    total = nn(all_ref[...], w_ref[0])
+        term = nn(h_ref[...], w_ref[0, pl.ds(at, part), :])
+        total = term if total is None else total + term
+    return total
+
+
+def expert_first_kernel(seqs, steps, w_ref, *refs):
+    refs[-1][...] = down_part(lax.axis_index("seq"), seqs, steps, w_ref, refs[:-1])
+
+
+def expert_out_kernel(seqs, held, steps, w_ref, share_ref, first_ref, *refs):
+    count = len(steps)
+    h_refs, out_refs, acc_ref = refs[:count], refs[count : count + held], refs[count + held]
+    expert = lax.axis_index("exp")
+    total = first_ref[...] + down_part(lax.axis_index("seq"), seqs, steps, w_ref, h_refs)
     acc_ref[...] = total * share_ref[:, 0:1]
     for r in range(held):
         at = pl.multiple_of(lax.rem(expert + r, seqs) * CAP, CAP)
@@ -733,13 +743,22 @@
     )
     hiddens = spread([hidden] * seqs, "seq", seqs)
     returned = spread(prefixes, "seq", seqs)
+    early_steps = [0]
+    late_steps = [r for r in range(seqs) if r not in early_steps]
+    first = run(
+        functools.partial(expert_first_kernel, seqs, early_steps),
+        shaped((slot_rows, out_part), F32),
+        (down_kept, *(hiddens[r] for r in early_steps)),
+        flops=200_000_000,
+        nbytes=7_000_000,
+    )
     outs = run(
-        functools.partial(expert_out_kernel, seqs, held),
+        functools.partial(expert_out_kernel, seqs, held, late_steps),
         (shaped((CAP, out_part), BF16),) * held,
-        (down_kept, shares, *hiddens),
-        scratch=[pltpu.VMEM((slot_rows, out_part), F32), pltpu.VMEM((slot_rows, seqs * hidden_part), BF16)],
-        flops=450_000_000,
-        nbytes=14_000_000,
+        (down_kept, shares, first, *(hiddens[r] for r in late_steps)),
+        scratch=[pltpu.VMEM((slot_rows, out_part), F32)],
+        flops=200_000_000,
+        nbytes=7_000_000,
     )
     y = [
         lax.ppermute(

time: 83.2 us -> 87.2 us (1.048)
  the two profiles are of different devices: /device:TPU:2 before, /device:TPU:0 now
where the time goes in v5:
time: 87.2 us; the launch traced here: 87 us
  starting transfers between devices  41.7 us (48%)
  Pallas kernels  25 us (29%)
  waiting for transfers between devices  20 us (23%)
    ppermute x21, starting transfers between devices, spread(): lax.ppermute(pieces[r], axis, [(i, (i + r) % count) for i in range(count)])  30.7 us
    pallas_call x12, Pallas kernels, run(): kernel(*args[:near], *(pltpu.with_memory_space_constraint(x, pltpu.HBM) f...  25 us
    ppermute x21, waiting for transfers between devices, spread(): lax.ppermute(pieces[r], axis, [(i, (i + r) % count) for i in range(count)])  19 us
    ppermute x4, starting transfers between devices, ring_body(): lax.ppermute(piece, ('seq', 'exp'), [(s * held + e, (e + r) % seqs * held...  11 us
  transfers between devices with their start and end apart: 25, of which 6 were waited for; matrix products, arithmetic and copies ran while one was open for 0% of the time, Pallas kernels for 16%

profile of v5, /device:TPU:0, one launch (start us, length us, event | category | flops | bytes accessed | tf_op | source)
XLA Modules:
  0.0 87.0 jit_solution(15989800234822319134)
XLA Ops:
  0.0 2.5 %shard_map.127 = (bf16[128,1536]{1,0:T(8,128)(2,1)S(1)}, bf16[128,1536]{1,0:T(8,128)(2,1)S(1)}, f32[12,128]{1,0:T(8,128)}, bf16[128,1536]{1,0:T(8,128)(2,1)S(1)}...) custom-call(bf16[128,1536]{1,0:T(8,128)(2,1)} %refs_0_.3, ...), custom_call_target="tpu_custom_call" | custom-call | flops 1000 | bytes 1000 | tf_op jit(solution)/shard_map/pallas_call | solution.py:636
  2.5 2.3 %shard_map.128 = (f32[128,1536]{1,0:T(8,128)S(1)}, bf16[128,1536]{1,0:T(8,128)(2,1)S(1)}, f32[32,128]{1,0:T(8,128)S(1)}, bf16[32,1280]{1,0:T(8,128)(2,1)S(1)}, b...) custom-call(bf16[128,1536]{1,0:T(8,128)(2,1)S(1)} %get-tuple-element.43.q_ref, ...), custom_call_target="tpu_custom_call" | custom-call | flops 200000000 | bytes 2000000 | tf_op jit(solution)/shard_map/pallas_call | solution.py:636
  4.8 3.1 %collective-permute-start.3 = (bf16[32,1280]{1,0:T(8,128)(2,1)S(1)}, bf16[32,1280]{1,0:T(8,128)(2,1)S(1)}, u32[]{:S(2)}, u32[]{:S(2)}) collective-permute-start(bf16[32,1280]{1,0:T(8,128)(2,1)S(1)} %get-tuple-element.59), channel_id=1, source_target_pairs={{0,4},{4,8},{8,12},{12,0},{1,5},{5,9},{9,13},{13,1},{2,6},{6,10},{... | collective-permute-start | bytes 245768 | tf_op jit(solution)/shard_map/ppermute | solution.py:642
  7.9 2.6 %collective-permute-start.4 = (bf16[32,1280]{1,0:T(8,128)(2,1)S(1)}, bf16[32,1280]{1,0:T(8,128)(2,1)S(1)}, u32[]{:S(2)}, u32[]{:S(2)}) collective-permute-start(bf16[32,1280]{1,0:T(8,128)(2,1)S(1)} %get-tuple-element.60), channel_id=1, source_target_pairs={{0,8},{4,12},{8,0},{12,4},{1,9},{5,13},{9,1},{13,5},{2,10},{6,14},... | collective-permute-start | bytes 245768 | tf_op jit(solution)/shard_map/ppermute | solution.py:642
  10.6 1.8 %collective-permute-start.1 = (bf16[400,128]{1,0:T(8,128)(2,1)S(1)}, bf16[400,128]{1,0:T(8,128)(2,1)S(1)}, u32[]{:S(2)}, u32[]{:S(2)}) collective-permute-start(bf16[400,128]{1,0:T(8,128)(2,1)S(1)} %get-tuple-element.56), channel_id=1, source_target_pairs={{0,8},{4,12},{8,0},{12,4},{1,9},{5,13},{9,1},{13,5},{2,10},{6,14},... | collective-permute-start | bytes 307208 | tf_op jit(solution)/shard_map/ppermute | solution.py:642
  12.4 1.9 %collective-permute-start.2 = (bf16[400,128]{1,0:T(8,128)(2,1)S(1)}, bf16[400,128]{1,0:T(8,128)(2,1)S(1)}, u32[]{:S(2)}, u32[]{:S(2)}) collective-permute-start(bf16[400,128]{1,0:T(8,128)(2,1)S(1)} %get-tuple-element.57), channel_id=1, source_target_pairs={{0,12},{4,0},{8,4},{12,8},{1,13},{5,1},{9,5},{13,9},{2,14},{6,2},{... | collective-permute-start | bytes 307208 | tf_op jit(solution)/shard_map/ppermute | solution.py:642
  14.4 5.9 %collective-permute-done.4.refs_6_ = bf16[32,1280]{1,0:T(8,128)(2,1)S(1)} collective-permute-done((bf16[32,1280]{1,0:T(8,128)(2,1)S(1)}, bf16[32,1280]{1,0:T(8,128)(2,1)S(1)}, u32[]{:S(2)}, u32[]{:S(2)}) %collective-permute-start.4) | collective-permute-done | bytes 81952 | tf_op jit(solution)/shard_map/ppermute | solution.py:642
  20.4 2.7 %collective-permute-start.5 = (bf16[32,1280]{1,0:T(8,128)(2,1)S(1)}, bf16[32,1280]{1,0:T(8,128)(2,1)S(1)}, u32[]{:S(2)}, u32[]{:S(2)}) collective-permute-start(bf16[32,1280]{1,0:T(8,128)(2,1)S(1)} %get-tuple-element.61), channel_id=1, source_target_pairs={{0,12},{4,0},{8,4},{12,8},{1,13},{5,1},{9,5},{13,9},{2,14},{6,2},{... | collective-permute-start | bytes 245768 | tf_op jit(solution)/shard_map/ppermute | solution.py:642
  23.0 2.1 %collective-permute-done.5.refs_7_ = bf16[32,1280]{1,0:T(8,128)(2,1)S(1)} collective-permute-done((bf16[32,1280]{1,0:T(8,128)(2,1)S(1)}, bf16[32,1280]{1,0:T(8,128)(2,1)S(1)}, u32[]{:S(2)}, u32[]{:S(2)}) %collective-permute-start.5) | collective-permute-done | bytes 81952 | tf_op jit(solution)/shard_map/ppermute | solution.py:642
  25.1 0.5 shard_map.129
  25.7 1.6 %collective-permute-start.16 = (bf16[48,1536]{1,0:T(8,128)(2,1)S(1)}, bf16[48,1536]{1,0:T(8,128)(2,1)S(1)}, u32[]{:S(2)}, u32[]{:S(2)}) collective-permute-start(bf16[48,1536]{1,0:T(8,128)(2,1)S(1)} %shard_map.134.refs_4_), channel_id=1, source_target_pairs={{0,2},{1,3},{2,0},{3,1},{4,6},{5,7},{6,4},{7,5},{8,10},{9,11},{10,... | collective-permute-start | bytes 442376 | tf_op jit(solution)/shard_map/ppermute | solution.py:642
  27.5 1.5 %collective-permute-start.10 = (bf16[32,384]{1,0:T(8,128)(2,1)S(1)}, bf16[32,384]{1,0:T(8,128)(2,1)S(1)}, u32[]{:S(2)}, u32[]{:S(2)}) collective-permute-start(bf16[32,384]{1,0:T(8,128)(2,1)S(1)} %get-tuple-element.70), channel_id=1, source_target_pairs={{0,2},{1,3},{2,0},{3,1},{4,6},{5,7},{6,4},{7,5},{8,10},{9,11},{10,... | collective-permute-start | bytes 73736 | tf_op jit(solution)/shard_map/ppermute | solution.py:642
  29.3 3.2 %collective-permute-done.10.refs_2_ = bf16[32,384]{1,0:T(8,128)(2,1)S(1)} collective-permute-done((bf16[32,384]{1,0:T(8,128)(2,1)S(1)}, bf16[32,384]{1,0:T(8,128)(2,1)S(1)}, u32[]{:S(2)}, u32[]{:S(2)}) %collective-permute-start.10) | collective-permute-done | bytes 24608 | tf_op jit(solution)/shard_map/ppermute | solution.py:642
  32.6 4.2 %collective-permute-start.14 = (bf16[4,32,384]{2,1,0:T(8,128)(2,1)S(1)}, bf16[4,32,384]{2,1,0:T(8,128)(2,1)S(1)}, u32[]{:S(2)}, u32[]{:S(2)}) collective-permute-start(bf16[4,32,384]{2,1,0:T(8,128)(2,1)S(1)} %shard_map.132.after_ref.refs_0_), channel_id=1, source_target_pairs={{0,12},{4,0},{8,4},{12,8},{1,13},{5,1},{9,5},{13,9},{2,14},{6,2},{... | collective-permute-start | bytes 294920 | tf_op jit(solution)/shard_map/ppermute | solution.py:642
  36.8 0.6 collective-permute-start.12
  37.4 5.0 %shard_map.131.gate_ref = bf16[1,6144,1152]{2,1,0:T(8,128)(2,1)S(1)} custom-call(bf16[32,1280]{1,0:T(8,128)(2,1)S(1)} %get-tuple-element.58.refs_4_.after_ref, bf16[1,6144,1152]{2,1,0:T(8,128)(2,1)} %refs_0_.4), custom_call_target="tpu_custom_call" | custom-call | flops 1000 | bytes 14000000 | tf_op jit(solution)/shard_map/pallas_call | solution.py:636
  42.5 5.0 %shard_map.133.up_ref = bf16[1,6144,1152]{2,1,0:T(8,128)(2,1)S(1)} custom-call(bf16[4,32,384]{2,1,0:T(8,128)(2,1)S(1)} %shard_map.132.after_ref.refs_0_, bf16[1,6144,1152]{2,1,0:T(8,128)(2,1)} %refs_0_.5), custom_call_target="tpu_custom_call" | custom-call | flops 1000 | bytes 14000000 | tf_op jit(solution)/shard_map/pallas_call | solution.py:636
  47.6 5.5 %shard_map.135 = (bf16[32,1152]{1,0:T(8,128)(2,1)S(1)}, f32[32,128]{1,0:T(8,128)S(1)}, bf16[1,4608,1536]{2,1,0:T(8,128)(2,1)S(1)}) custom-call(f32[32,128]{1,0:T(8,128)S(1)} %get-tuple-element.67.ids_ref, bf16[1,6144,1152]{2,1,0:T(8,128)(2,1)S(1)} %shard_map.131.gate_ref, bf16[1,6144,1152]{2,1,0:T(8,128)(2,1)S(1)} %shard_map.133.up_ref, ...), custom_call_target="tpu_custom_call" | custom-call | flops 900000000 | bytes 28000000 | tf_op jit(solution)/shard_map/pallas_call | solution.py:636
  53.1 3.2 %collective-permute-start.20 = (bf16[32,1152]{1,0:T(8,128)(2,1)S(1)}, bf16[32,1152]{1,0:T(8,128)(2,1)S(1)}, u32[]{:S(2)}, u32[]{:S(2)}) collective-permute-start(bf16[32,1152]{1,0:T(8,128)(2,1)S(1)} %get-tuple-element.76.refs_0_), channel_id=1, source_target_pairs={{0,12},{4,0},{8,4},{12,8},{1,13},{5,1},{9,5},{13,9},{2,14},{6,2},{... | collective-permute-start | bytes 221192 | tf_op jit(solution)/shard_map/ppermute | solution.py:642
  56.3 1.1 %collective-permute-start.7 = (bf16[384,128]{1,0:T(8,128)(2,1)S(1)}, bf16[384,128]{1,0:T(8,128)(2,1)S(1)}, u32[]{:S(2)}, u32[]{:S(2)}) collective-permute-start(bf16[384,128]{1,0:T(8,128)(2,1)S(1)} %get-tuple-element.64), channel_id=1, source_target_pairs={{0,8},{4,12},{8,0},{12,4},{1,9},{5,13},{9,1},{13,5},{2,10},{6,14},... | collective-permute-start | bytes 294920 | tf_op jit(solution)/shard_map/ppermute | solution.py:642
  57.4 1.8 %collective-permute-start.19 = (bf16[32,1152]{1,0:T(8,128)(2,1)S(1)}, bf16[32,1152]{1,0:T(8,128)(2,1)S(1)}, u32[]{:S(2)}, u32[]{:S(2)}) collective-permute-start(bf16[32,1152]{1,0:T(8,128)(2,1)S(1)} %get-tuple-element.76.refs_0_), channel_id=1, source_target_pairs={{0,8},{4,12},{8,0},{12,4},{1,9},{5,13},{9,1},{13,5},{2,10},{6,14},... | collective-permute-start | bytes 221192 | tf_op jit(solution)/shard_map/ppermute | solution.py:642
  59.2 1.7 %collective-permute-start.18 = (bf16[32,1152]{1,0:T(8,128)(2,1)S(1)}, bf16[32,1152]{1,0:T(8,128)(2,1)S(1)}, u32[]{:S(2)}, u32[]{:S(2)}) collective-permute-start(bf16[32,1152]{1,0:T(8,128)(2,1)S(1)} %get-tuple-element.76.refs_0_), channel_id=1, source_target_pairs={{0,4},{4,8},{8,12},{12,0},{1,5},{5,9},{9,13},{13,1},{2,6},{6,10},{... | collective-permute-start | bytes 221192 | tf_op jit(solution)/shard_map/ppermute | solution.py:642
  60.9 2.1 %collective-permute-start.8 = (bf16[384,128]{1,0:T(8,128)(2,1)S(1)}, bf16[384,128]{1,0:T(8,128)(2,1)S(1)}, u32[]{:S(2)}, u32[]{:S(2)}) collective-permute-start(bf16[384,128]{1,0:T(8,128)(2,1)S(1)} %get-tuple-element.65), channel_id=1, source_target_pairs={{0,12},{4,0},{8,4},{12,8},{1,13},{5,1},{9,5},{13,9},{2,14},{6,2},{... | collective-permute-start | bytes 294920 | tf_op jit(solution)/shard_map/ppermute | solution.py:642
  63.1 0.7 shard_map.136.first_ref
  63.8 7.7 %collective-permute-done.19.refs_1_ = bf16[32,1152]{1,0:T(8,128)(2,1)S(1)} collective-permute-done((bf16[32,1152]{1,0:T(8,128)(2,1)S(1)}, bf16[32,1152]{1,0:T(8,128)(2,1)S(1)}, u32[]{:S(2)}, u32[]{:S(2)}) %collective-permute-start.19) | collective-permute-done | bytes 73760 | tf_op jit(solution)/shard_map/ppermute | solution.py:642
  71.5 1.9 %shard_map.137 = (bf16[8,1536]{1,0:T(8,128)(2,1)S(1)}, bf16[8,1536]{1,0:T(8,128)(2,1)S(1)}, bf16[8,1536]{1,0:T(8,128)(2,1)S(1)}, bf16[8,1536]{1,0:T(8,128)(2,1)S(1)}) custom-call(bf16[1,4608,1536]{2,1,0:T(8,128)(2,1)S(1)} %get-tuple-element.74.w_ref, f32[32,128]{1,0:T(8,128)S(1)} %get-tuple-element.75.share_ref, f32[32,1536]{1,0:T(8,128)S(1)} %shard_map.136.first_ref, ...), custom_call_target="tpu_custom_call" | custom-call | flops 200000000 | bytes 7000000 | tf_op jit(solution)/shard_map/pallas_call | solution.py:636
  73.4 0.7 collective-permute-start.21
  74.1 3.5 %collective-permute-start.22 = (bf16[8,1536]{1,0:T(8,128)(2,1)S(1)}, bf16[8,1536]{1,0:T(8,128)(2,1)S(1)}, u32[]{:S(2)}, u32[]{:S(2)}) collective-permute-start(bf16[8,1536]{1,0:T(8,128)(2,1)S(1)} %get-tuple-element.78), channel_id=1, source_target_pairs={{0,4},{1,8},{2,12},{3,0},{4,5},{5,9},{6,13},{7,1},{8,6},{9,10},{10... | collective-permute-start | bytes 73736 | tf_op jit(solution)/shard_map/ppermute | solution.py:764
  77.6 4.5 %collective-permute-start.23 = (bf16[8,1536]{1,0:T(8,128)(2,1)S(1)}, bf16[8,1536]{1,0:T(8,128)(2,1)S(1)}, u32[]{:S(2)}, u32[]{:S(2)}) collective-permute-start(bf16[8,1536]{1,0:T(8,128)(2,1)S(1)} %get-tuple-element.79), channel_id=1, source_target_pairs={{0,8},{1,12},{2,0},{3,4},{4,9},{5,13},{6,1},{7,5},{8,10},{9,14},{1... | collective-permute-start | bytes 73736 | tf_op jit(solution)/shard_map/ppermute | solution.py:764
  82.1 2.4 %collective-permute-start.24 = (bf16[8,1536]{1,0:T(8,128)(2,1)S(1)}, bf16[8,1536]{1,0:T(8,128)(2,1)S(1)}, u32[]{:S(2)}, u32[]{:S(2)}) collective-permute-start(bf16[8,1536]{1,0:T(8,128)(2,1)S(1)} %get-tuple-element.80), channel_id=1, source_target_pairs={{0,12},{1,0},{2,4},{3,8},{4,13},{5,1},{6,5},{7,9},{8,14},{9,2},{10... | collective-permute-start | bytes 73736 | tf_op jit(solution)/shard_map/ppermute | solution.py:764
  85.0 1.0 %collective-permute-done.24.refs_3_ = bf16[8,1536]{1,0:T(8,128)(2,1)S(1)} collective-permute-done((bf16[8,1536]{1,0:T(8,128)(2,1)S(1)}, bf16[8,1536]{1,0:T(8,128)(2,1)S(1)}, u32[]{:S(2)}, u32[]{:S(2)}) %collective-permute-start.24) | collective-permute-done | bytes 24608 | tf_op jit(solution)/shard_map/ppermute | solution.py:764
  85.9 1.0 %shard_map.138 = bf16[128,1536]{1,0:T(8,128)(2,1)} custom-call(bf16[128,1536]{1,0:T(8,128)(2,1)S(1)} %shard_map.130.mixed_ref, f32[32,128]{1,0:T(8,128)S(1)} %get-tuple-element.66.place_ref, bf16[8,1536]{1,0:T(8,128)(2,1)S(1)} %collective-permute-done.21.refs_0_, bf16[8,1536]{1,0:T(8,128)(2,1)S(1)} %collective-permute-done.22.refs_1_, ...), custom_call_target="tpu_custom_call" | custom-call | flops 1000 | bytes 1000 | tf_op jit(solution)/shard_map/pallas_call | solution.py:636
  (30 shorter events, 1.4 us)
Async XLA Ops:
  4.8 9.5 %collective-permute-start.3 = (bf16[32,1280]{1,0:T(8,128)(2,1)S(1)}, bf16[32,1280]{1,0:T(8,128)(2,1)S(1)}, u32[]{:S(2)}, u32[]{:S(2)}) collective-permute-start(bf16[32,1280]{1,0:T(8,128)(2,1)S(1)} %get-tuple-element.59), channel_id=1, source_target_pairs={{0,4},{4,8},{8,12},{12,0},{1,5},{5,9},{9,13},{13,1},{2,6},{6,10},{... | collective-permute-start | bytes 245768 | tf_op jit(solution)/shard_map/ppermute | solution.py:642
  7.9 12.5 %collective-permute-start.4 = (bf16[32,1280]{1,0:T(8,128)(2,1)S(1)}, bf16[32,1280]{1,0:T(8,128)(2,1)S(1)}, u32[]{:S(2)}, u32[]{:S(2)}) collective-permute-start(bf16[32,1280]{1,0:T(8,128)(2,1)S(1)} %get-tuple-element.60), channel_id=1, source_target_pairs={{0,8},{4,12},{8,0},{12,4},{1,9},{5,13},{9,1},{13,5},{2,10},{6,14},... | collective-permute-start | bytes 245768 | tf_op jit(solution)/shard_map/ppermute | solution.py:642
  10.5 14.6 %collective-permute-start = (bf16[400,128]{1,0:T(8,128)(2,1)S(1)}, bf16[400,128]{1,0:T(8,128)(2,1)S(1)}, u32[]{:S(2)}, u32[]{:S(2)}) collective-permute-start(bf16[400,128]{1,0:T(8,128)(2,1)S(1)} %get-tuple-element.55), channel_id=1, source_target_pairs={{0,4},{4,8},{8,12},{12,0},{1,5},{5,9},{9,13},{13,1},{2,6},{6,10},{... | collective-permute-start | bytes 307208 | tf_op jit(solution)/shard_map/ppermute | solution.py:642
  10.6 14.5 %collective-permute-start.1 = (bf16[400,128]{1,0:T(8,128)(2,1)S(1)}, bf16[400,128]{1,0:T(8,128)(2,1)S(1)}, u32[]{:S(2)}, u32[]{:S(2)}) collective-permute-start(bf16[400,128]{1,0:T(8,128)(2,1)S(1)} %get-tuple-element.56), channel_id=1, source_target_pairs={{0,8},{4,12},{8,0},{12,4},{1,9},{5,13},{9,1},{13,5},{2,10},{6,14},... | collective-permute-start | bytes 307208 | tf_op jit(solution)/shard_map/ppermute | solution.py:642
  12.4 12.7 %collective-permute-start.2 = (bf16[400,128]{1,0:T(8,128)(2,1)S(1)}, bf16[400,128]{1,0:T(8,128)(2,1)S(1)}, u32[]{:S(2)}, u32[]{:S(2)}) collective-permute-start(bf16[400,128]{1,0:T(8,128)(2,1)S(1)} %get-tuple-element.57), channel_id=1, source_target_pairs={{0,12},{4,0},{8,4},{12,8},{1,13},{5,1},{9,5},{13,9},{2,14},{6,2},{... | collective-permute-start | bytes 307208 | tf_op jit(solution)/shard_map/ppermute | solution.py:642
  14.4 22.4 %collective-permute-start.17 = (bf16[48,1536]{1,0:T(8,128)(2,1)S(1)}, bf16[48,1536]{1,0:T(8,128)(2,1)S(1)}, u32[]{:S(2)}, u32[]{:S(2)}) collective-permute-start(bf16[48,1536]{1,0:T(8,128)(2,1)S(1)} %shard_map.134.refs_4_), channel_id=1, source_target_pairs={{0,3},{1,0},{2,1},{3,2},{4,7},{5,4},{6,5},{7,6},{8,11},{9,8},{10,9... | collective-permute-start | bytes 442376 | tf_op jit(solution)/shard_map/ppermute | solution.py:642
  20.4 4.7 %collective-permute-start.5 = (bf16[32,1280]{1,0:T(8,128)(2,1)S(1)}, bf16[32,1280]{1,0:T(8,128)(2,1)S(1)}, u32[]{:S(2)}, u32[]{:S(2)}) collective-permute-start(bf16[32,1280]{1,0:T(8,128)(2,1)S(1)} %get-tuple-element.61), channel_id=1, source_target_pairs={{0,12},{4,0},{8,4},{12,8},{1,13},{5,1},{9,5},{13,9},{2,14},{6,2},{... | collective-permute-start | bytes 245768 | tf_op jit(solution)/shard_map/ppermute | solution.py:642
  25.6 3.4 %collective-permute-start.9 = (bf16[32,384]{1,0:T(8,128)(2,1)S(1)}, bf16[32,384]{1,0:T(8,128)(2,1)S(1)}, u32[]{:S(2)}, u32[]{:S(2)}) collective-permute-start(bf16[32,384]{1,0:T(8,128)(2,1)S(1)} %get-tuple-element.69), channel_id=1, source_target_pairs={{0,1},{1,2},{2,3},{3,0},{4,5},{5,6},{6,7},{7,4},{8,9},{9,10},{10,1... | collective-permute-start | bytes 73736 | tf_op jit(solution)/shard_map/ppermute | solution.py:642
  25.7 21.8 %collective-permute-start.16 = (bf16[48,1536]{1,0:T(8,128)(2,1)S(1)}, bf16[48,1536]{1,0:T(8,128)(2,1)S(1)}, u32[]{:S(2)}, u32[]{:S(2)}) collective-permute-start(bf16[48,1536]{1,0:T(8,128)(2,1)S(1)} %shard_map.134.refs_4_), channel_id=1, source_target_pairs={{0,2},{1,3},{2,0},{3,1},{4,6},{5,7},{6,4},{7,5},{8,10},{9,11},{10,... | collective-permute-start | bytes 442376 | tf_op jit(solution)/shard_map/ppermute | solution.py:642
  27.2 20.3 %collective-permute-start.15 = (bf16[48,1536]{1,0:T(8,128)(2,1)S(1)}, bf16[48,1536]{1,0:T(8,128)(2,1)S(1)}, u32[]{:S(2)}, u32[]{:S(2)}) collective-permute-start(bf16[48,1536]{1,0:T(8,128)(2,1)S(1)} %shard_map.134.refs_4_), channel_id=1, source_target_pairs={{0,1},{1,2},{2,3},{3,0},{4,5},{5,6},{6,7},{7,4},{8,9},{9,10},{10,1... | collective-permute-start | bytes 442376 | tf_op jit(solution)/shard_map/ppermute | solution.py:642
  27.5 4.9 %collective-permute-start.10 = (bf16[32,384]{1,0:T(8,128)(2,1)S(1)}, bf16[32,384]{1,0:T(8,128)(2,1)S(1)}, u32[]{:S(2)}, u32[]{:S(2)}) collective-permute-start(bf16[32,384]{1,0:T(8,128)(2,1)S(1)} %get-tuple-element.70), channel_id=1, source_target_pairs={{0,2},{1,3},{2,0},{3,1},{4,6},{5,7},{6,4},{7,5},{8,10},{9,11},{10,... | collective-permute-start | bytes 73736 | tf_op jit(solution)/shard_map/ppermute | solution.py:642
  29.0 3.5 %collective-permute-start.11 = (bf16[32,384]{1,0:T(8,128)(2,1)S(1)}, bf16[32,384]{1,0:T(8,128)(2,1)S(1)}, u32[]{:S(2)}, u32[]{:S(2)}) collective-permute-start(bf16[32,384]{1,0:T(8,128)(2,1)S(1)} %get-tuple-element.71), channel_id=1, source_target_pairs={{0,3},{1,0},{2,1},{3,2},{4,7},{5,4},{6,5},{7,6},{8,11},{9,8},{10,9... | collective-permute-start | bytes 73736 | tf_op jit(solution)/shard_map/ppermute | solution.py:642
  32.6 15.0 %collective-permute-start.14 = (bf16[4,32,384]{2,1,0:T(8,128)(2,1)S(1)}, bf16[4,32,384]{2,1,0:T(8,128)(2,1)S(1)}, u32[]{:S(2)}, u32[]{:S(2)}) collective-permute-start(bf16[4,32,384]{2,1,0:T(8,128)(2,1)S(1)} %shard_map.132.after_ref.refs_0_), channel_id=1, source_target_pairs={{0,12},{4,0},{8,4},{12,8},{1,13},{5,1},{9,5},{13,9},{2,14},{6,2},{... | collective-permute-start | bytes 294920 | tf_op jit(solution)/shard_map/ppermute | solution.py:642
  36.8 10.8 %collective-permute-start.13 = (bf16[4,32,384]{2,1,0:T(8,128)(2,1)S(1)}, bf16[4,32,384]{2,1,0:T(8,128)(2,1)S(1)}, u32[]{:S(2)}, u32[]{:S(2)}) collective-permute-start(bf16[4,32,384]{2,1,0:T(8,128)(2,1)S(1)} %shard_map.132.after_ref.refs_0_), channel_id=1, source_target_pairs={{0,8},{4,12},{8,0},{12,4},{1,9},{5,13},{9,1},{13,5},{2,10},{6,14},... | collective-permute-start | bytes 294920 | tf_op jit(solution)/shard_map/ppermute | solution.py:642
  36.8 10.8 %collective-permute-start.12 = (bf16[4,32,384]{2,1,0:T(8,128)(2,1)S(1)}, bf16[4,32,384]{2,1,0:T(8,128)(2,1)S(1)}, u32[]{:S(2)}, u32[]{:S(2)}) collective-permute-start(bf16[4,32,384]{2,1,0:T(8,128)(2,1)S(1)} %shard_map.132.after_ref.refs_0_), channel_id=1, source_target_pairs={{0,4},{4,8},{8,12},{12,0},{1,5},{5,9},{9,13},{13,1},{2,6},{6,10},{... | collective-permute-start | bytes 294920 | tf_op jit(solution)/shard_map/ppermute | solution.py:642
  53.1 7.9 %collective-permute-start.20 = (bf16[32,1152]{1,0:T(8,128)(2,1)S(1)}, bf16[32,1152]{1,0:T(8,128)(2,1)S(1)}, u32[]{:S(2)}, u32[]{:S(2)}) collective-permute-start(bf16[32,1152]{1,0:T(8,128)(2,1)S(1)} %get-tuple-element.76.refs_0_), channel_id=1, source_target_pairs={{0,12},{4,0},{8,4},{12,8},{1,13},{5,1},{9,5},{13,9},{2,14},{6,2},{... | collective-permute-start | bytes 221192 | tf_op jit(solution)/shard_map/ppermute | solution.py:642
  56.3 21.3 %collective-permute-start.6 = (bf16[384,128]{1,0:T(8,128)(2,1)S(1)}, bf16[384,128]{1,0:T(8,128)(2,1)S(1)}, u32[]{:S(2)}, u32[]{:S(2)}) collective-permute-start(bf16[384,128]{1,0:T(8,128)(2,1)S(1)} %get-tuple-element.63), channel_id=1, source_target_pairs={{0,4},{4,8},{8,12},{12,0},{1,5},{5,9},{9,13},{13,1},{2,6},{6,10},{... | collective-permute-start | bytes 294920 | tf_op jit(solution)/shard_map/ppermute | solution.py:642
  56.3 25.8 %collective-permute-start.7 = (bf16[384,128]{1,0:T(8,128)(2,1)S(1)}, bf16[384,128]{1,0:T(8,128)(2,1)S(1)}, u32[]{:S(2)}, u32[]{:S(2)}) collective-permute-start(bf16[384,128]{1,0:T(8,128)(2,1)S(1)} %get-tuple-element.64), channel_id=1, source_target_pairs={{0,8},{4,12},{8,0},{12,4},{1,9},{5,13},{9,1},{13,5},{2,10},{6,14},... | collective-permute-start | bytes 294920 | tf_op jit(solution)/shard_map/ppermute | solution.py:642
  57.4 14.0 %collective-permute-start.19 = (bf16[32,1152]{1,0:T(8,128)(2,1)S(1)}, bf16[32,1152]{1,0:T(8,128)(2,1)S(1)}, u32[]{:S(2)}, u32[]{:S(2)}) collective-permute-start(bf16[32,1152]{1,0:T(8,128)(2,1)S(1)} %get-tuple-element.76.refs_0_), channel_id=1, source_target_pairs={{0,8},{4,12},{8,0},{12,4},{1,9},{5,13},{9,1},{13,5},{2,10},{6,14},... | collective-permute-start | bytes 221192 | tf_op jit(solution)/shard_map/ppermute | solution.py:642
  59.2 12.2 %collective-permute-start.18 = (bf16[32,1152]{1,0:T(8,128)(2,1)S(1)}, bf16[32,1152]{1,0:T(8,128)(2,1)S(1)}, u32[]{:S(2)}, u32[]{:S(2)}) collective-permute-start(bf16[32,1152]{1,0:T(8,128)(2,1)S(1)} %get-tuple-element.76.refs_0_), channel_id=1, source_target_pairs={{0,4},{4,8},{8,12},{12,0},{1,5},{5,9},{9,13},{13,1},{2,6},{6,10},{... | collective-permute-start | bytes 221192 | tf_op jit(solution)/shard_map/ppermute | solution.py:642
  60.9 23.5 %collective-permute-start.8 = (bf16[384,128]{1,0:T(8,128)(2,1)S(1)}, bf16[384,128]{1,0:T(8,128)(2,1)S(1)}, u32[]{:S(2)}, u32[]{:S(2)}) collective-permute-start(bf16[384,128]{1,0:T(8,128)(2,1)S(1)} %get-tuple-element.65), channel_id=1, source_target_pairs={{0,12},{4,0},{8,4},{12,8},{1,13},{5,1},{9,5},{13,9},{2,14},{6,2},{... | collective-permute-start | bytes 294920 | tf_op jit(solution)/shard_map/ppermute | solution.py:642
  73.4 11.5 %collective-permute-start.21 = (bf16[8,1536]{1,0:T(8,128)(2,1)S(1)}, bf16[8,1536]{1,0:T(8,128)(2,1)S(1)}, u32[]{:S(2)}, u32[]{:S(2)}) collective-permute-start(bf16[8,1536]{1,0:T(8,128)(2,1)S(1)} %get-tuple-element.77), channel_id=1, source_target_pairs={{0,0},{1,4},{2,8},{3,12},{4,1},{5,5},{6,9},{7,13},{8,2},{9,6},{10,... | collective-permute-start | bytes 73736 | tf_op jit(solution)/shard_map/ppermute | solution.py:764
  74.1 10.9 %collective-permute-start.22 = (bf16[8,1536]{1,0:T(8,128)(2,1)S(1)}, bf16[8,1536]{1,0:T(8,128)(2,1)S(1)}, u32[]{:S(2)}, u32[]{:S(2)}) collective-permute-start(bf16[8,1536]{1,0:T(8,128)(2,1)S(1)} %get-tuple-element.78), channel_id=1, source_target_pairs={{0,4},{1,8},{2,12},{3,0},{4,5},{5,9},{6,13},{7,1},{8,6},{9,10},{10... | collective-permute-start | bytes 73736 | tf_op jit(solution)/shard_map/ppermute | solution.py:764
  77.6 7.4 %collective-permute-start.23 = (bf16[8,1536]{1,0:T(8,128)(2,1)S(1)}, bf16[8,1536]{1,0:T(8,128)(2,1)S(1)}, u32[]{:S(2)}, u32[]{:S(2)}) collective-permute-start(bf16[8,1536]{1,0:T(8,128)(2,1)S(1)} %get-tuple-element.79), channel_id=1, source_target_pairs={{0,8},{1,12},{2,0},{3,4},{4,9},{5,13},{6,1},{7,5},{8,10},{9,14},{1... | collective-permute-start | bytes 73736 | tf_op jit(solution)/shard_map/ppermute | solution.py:764
  82.1 3.9 %collective-permute-start.24 = (bf16[8,1536]{1,0:T(8,128)(2,1)S(1)}, bf16[8,1536]{1,0:T(8,128)(2,1)S(1)}, u32[]{:S(2)}, u32[]{:S(2)}) collective-permute-start(bf16[8,1536]{1,0:T(8,128)(2,1)S(1)} %get-tuple-element.80), channel_id=1, source_target_pairs={{0,12},{1,0},{2,4},{3,8},{4,13},{5,1},{6,5},{7,9},{8,14},{9,2},{10... | collective-permute-start | bytes 73736 | tf_op jit(solution)/shard_map/ppermute | solution.py:764
